TPU v7x, 768 devices: a whole 4x8x12 slice. The times are simulated.
768 devices in a mesh: dp: 96 (over x, z, core), chan: 8 (over y).
Axes of the slice: x: 4, y: 8, z: 12, core: 2. Of those that a mesh axis runs over, the one named last changes fastest.
Arguments:
- features: bfloat16 [96, 16, 16, 1024], P('dp'), may hold values from -6 to 6
- styles: float32 [96, 1024], P('dp'), may hold values from 0.3 to 3
- conv_weight: bfloat16 [9, 1024, 1024], P(None, None, 'chan'), may hold values from -0.0625 to 0.0625
- grad_out: bfloat16 [96, 16, 16, 1024], P('dp', None, None, 'chan'), may hold values from -6 to 6
- crossover: int32 [96], P('dp'), may hold values from 0 to 13
- partner: int32 [96], P('dp'), may hold values from 0 to 95
- latents: float32 [96, 1024], P('dp'), may hold values from -6 to 6
- map_pre: float32 [96, 1024], P('dp'), may hold values from -6 to 6
- map_weight: float32 [1024, 1024], P(None, 'chan'), may hold values from -0.1875 to 0.1875
Outputs:
- grad_weight: float32 [9216, 1024], P('dp', 'chan')
- grad_input: bfloat16 [96, 16, 16, 1024], P('dp', None, None, 'chan')
- grad_map_out: float32 [1024, 1024], P(None, 'chan')
- grad_map_in: float32 [1024, 1024], P(None, 'chan')
All inputs are finite; a program needn't handle non-finite values.
Results may differ from a plain program's by a relative error of at most 0.005.
Values sent between devices are 32-bit elements; how exact they have to be, the bound alone decides.
No kernel may reach another device: no remote copies, remote signals or barrier semaphores. Data moves between devices by JAX's collectives and lax.ppermute only.
A program may use at most 64 MiB of HBM per device.

v0:
```python
import jax
import jax.numpy as jnp
from jax import lax
from jax.sharding import PartitionSpec as P

KTAPS = 9
LAYER = 6


highest = lax.Precision.HIGHEST


def tap_window(padded, tap_index, side_len):
    row_off = tap_index // 3
    col_off = tap_index % 3
    return padded[:, row_off : row_off + side_len, col_off : col_off + side_len, :]


def local(
    features, styles, conv_weight, grad_out, crossover, partner, latents, map_pre, map_weight
):
    samples = features.shape[0]
    side_len = features.shape[1]
    channels = features.shape[3]
    cols_dev = conv_weight.shape[2]
    pixels = samples * side_len * side_len
    dp_count = lax.axis_size("dp")
    batch_size = samples * dp_count
    chan_start = lax.axis_index("chan") * cols_dev
    scaled = (features.astype(jnp.float32) * styles[:, None, None, :]).astype(jnp.bfloat16)
    weight_sq = jnp.sum(jnp.square(conv_weight.astype(jnp.float32)), axis=0)
    style_sq = styles * styles
    demodulate = lax.rsqrt(jnp.dot(style_sq, weight_sq, precision=highest) + 1e-08)
    padded = jnp.pad(scaled, ((0, 0), (1, 1), (1, 1), (0, 0)))
    patches = jnp.concatenate(
        [
            tap_window(padded, tap_index, side_len).reshape(pixels, channels)
            for tap_index in range(KTAPS)
        ],
        axis=1,
    )
    weight_flat = conv_weight.reshape(KTAPS * channels, cols_dev)
    conv_out = jnp.dot(patches, weight_flat, preferred_element_type=jnp.float32)
    grad_wide = grad_out.astype(jnp.float32).reshape(samples, side_len * side_len, cols_dev)
    demod_grad = jnp.sum(
        grad_wide * conv_out.reshape(samples, side_len * side_len, cols_dev), axis=1
    )
    square_grad = -0.5 * demodulate**3 * demod_grad
    grad_scaled = (
        (grad_wide * demodulate[:, None, :]).astype(jnp.bfloat16).reshape(pixels, cols_dev)
    )
    accumulated = jnp.zeros((samples, side_len + 2, side_len + 2, channels), jnp.float32)
    for tap_index in range(KTAPS):
        row_off = tap_index // 3
        col_off = tap_index % 3
        product_piece = lax.dot_general(
            grad_scaled,
            conv_weight[tap_index],
            (((1,), (1,)), ((), ())),
            preferred_element_type=jnp.float32,
        )
        accumulated = accumulated.at[
            :, row_off : row_off + side_len, col_off : col_off + side_len, :
        ].add(product_piece.reshape(samples, side_len, side_len, channels))
    inner_part = accumulated[:, 1:-1, 1:-1, :]
    demod_part = 2.0 * styles * jnp.dot(square_grad, weight_sq.T, precision=highest)
    grad_inner, demod_cols = (
        lax.psum_scatter(inner_part, "chan", scatter_dimension=3, tiled=True),
        lax.psum_scatter(demod_part[:, None, None, :], "chan", scatter_dimension=3, tiled=True),
    )
    feature_cols = lax.dynamic_slice_in_dim(features, chan_start, cols_dev, 3)
    style_cols = lax.dynamic_slice_in_dim(styles, chan_start, cols_dev, 1)
    grad_input = (grad_inner * style_cols[:, None, None, :]).astype(jnp.bfloat16)
    style_grad = (
        jnp.sum(grad_inner * feature_cols.astype(jnp.float32), axis=(1, 2)) + demod_cols[:, 0, 0, :]
    )
    style_factor = jnp.dot(style_sq.T, square_grad, precision=highest)
    tiled_factor = jnp.tile(style_factor, (KTAPS, 1))
    weight_part = weight_flat.astype(jnp.float32)
    product_rows = lax.dot_general(
        patches, grad_scaled, (((0,), (0,)), ((), ())), preferred_element_type=jnp.float32
    )
    summed = lax.psum_scatter(
        product_rows + 2.0 * weight_part * tiled_factor, "dp", scatter_dimension=0, tiled=True
    )
    grad_weight = summed / batch_size
    global_ids = lax.axis_index("dp") * samples + jnp.arange(samples, dtype=jnp.int32)
    source = jnp.where(crossover <= LAYER, partner, global_ids)
    matches = (jnp.arange(batch_size, dtype=jnp.int32)[:, None] == source[None, :]).astype(
        jnp.float32
    )
    send_rows = jnp.dot(matches, style_grad, precision=highest)
    received = lax.all_to_all(
        send_rows.reshape(dp_count, samples, cols_dev),
        "dp",
        split_axis=0,
        concat_axis=0,
        tiled=True,
    )
    incoming = jnp.sum(received, axis=0)
    hidden = jnp.where(map_pre > 0, map_pre, 0.2 * map_pre)
    map_out_part = jnp.dot(hidden.T, incoming, precision=highest)
    hidden_part = jnp.dot(incoming, map_weight.T, precision=highest)
    hidden_grad = lax.psum_scatter(hidden_part, "chan", scatter_dimension=1, tiled=True)
    hid_dev = hidden_grad.shape[1]
    pre_cols = lax.dynamic_slice_in_dim(map_pre, lax.axis_index("chan") * hid_dev, hid_dev, 1)
    pre_grad = hidden_grad * jnp.where(pre_cols > 0, 1.0, 0.2).astype(jnp.float32)
    map_in_part = jnp.dot(latents.T, pre_grad, precision=highest)
    map_out_sum, map_in_sum = lax.psum((map_out_part, map_in_part), "dp")
    grad_map_out = map_out_sum / batch_size
    grad_map_in = map_in_sum / batch_size
    return (grad_weight, grad_input, grad_map_out, grad_map_in)


def solution(mesh):
    in_specs = (
        P("dp", None, None, None),
        P("dp", None),
        P(None, None, "chan"),
        P("dp", None, None, "chan"),
        P("dp"),
        P("dp"),
        P("dp", None),
        P("dp", None),
        P(None, "chan"),
    )
    out_specs = (P("dp", "chan"), P("dp", None, None, "chan"), P(None, "chan"), P(None, "chan"))
    return jax.shard_map(local, mesh=mesh, in_specs=in_specs, out_specs=out_specs, check_vma=False)
```

profile of v0, /device:TPU:1, one launch (start us, length us, event | category | flops | bytes accessed | tf_op | source)
XLA Modules:
  0.0 672.3 jit_solution(1244274296714422991)
XLA Ops:
  7.2 1.3 multiply_convert_fusion
  10.1 2.1 copy-done.2
  12.2 1.4 fusion.9
  14.6 1.0 copy.13
  17.4 2.5 fusion
  20.7 2.6 scatter-add.31
  23.3 3.2 add_select_fusion
  26.5 2.6 scatter-add.34
  29.1 1.3 fusion.2
  30.3 1.3 fusion.3
  31.6 1.3 scatter-add.36
  33.0 1.3 fusion.4
  34.2 1.3 scatter-add.39
  35.6 1.3 fusion.6
  36.8 1.2 fusion.7
  38.1 1.3 scatter-add.41
  39.4 1.3 fusion.8
  40.7 1.3 scatter-add.44
  42.0 1.1 slice.398
  44.7 6.8 %bitcast_multiply_fusion = f32[9216,128]{1,0:T(8,128)} fusion(f32[1024,128]{1,0:T(8,128)S(1)} %broadcast_multiply_fusion.3, bf16[9,1024,128]{2,1,0:T(8,128)(2,1)} %param.29), kind=kLoop, calls=%fused_computation.1 | loop fusion | flops 3538944 | bytes 7602176 | tf_op jit(solution)/shard_map/mul | solution.py:84
  51.5 9.4 %reduce-scatter.13.cloned.1.call-done = f32[128,1]{1,0:T(8,128)} async-done(((f32[1024,1]{1,0:T(8,128)}), f32[128,1]{1,0:T(8,128)}) %reduce-scatter.13.cloned.1.call-update) | async-done | bytes 528
  61.8 45.3 %reduce-scatter.11.cloned.1.call-done = f32[1,16,16,128]{3,2,1,0:T(8,128)} async-done(((f32[1,16,16,1024]{3,2,1,0:T(8,128)}), f32[1,16,16,128]{3,2,1,0:T(8,128)}) %reduce-scatter.11.cloned.1.call-update) | async-done | bytes 131088 | tf_op jit(solution)/shard_map/reduce_scatter | solution.py:68
  107.1 1.6 multiply_reduce_fusion.1
  109.3 19.0 %all-to-all-start = ((f32[96,1,128]{2,1,0:T(1,128)}), f32[96,1,128]{2,1,0:T(1,128)S(1)}, u32[]{:S(2)}, u32[]{:S(2)}) async-start(f32[96,1,128]{2,1,0:T(1,128)} %bitcast.58), calls=%async_computation.2 | async-start | bytes 98304 | tf_op jit(solution)/shard_map/all_to_all | solution.py:93
  128.4 12.0 %all-to-all-done = f32[96,1,128]{2,1,0:T(1,128)S(1)} async-done(((f32[96,1,128]{2,1,0:T(1,128)}), f32[96,1,128]{2,1,0:T(1,128)S(1)}, u32[]{:S(2)}, u32[]{:S(2)}) %all-to-all-start) | async-done | bytes 49184 | tf_op jit(solution)/shard_map/all_to_all | solution.py:93
  140.6 1.3 convolution_bitcast_fusion.9
  143.0 26.7 %reduce-scatter.15.cloned.1.call-done = f32[128,1]{1,0:T(8,128)} async-done(((f32[1024,1]{1,0:T(8,128)}), f32[128,1]{1,0:T(8,128)}) %reduce-scatter.15.cloned.1.call-update) | async-done | bytes 528
  171.7 7.4 %convolution_add_fusion = f32[9216,128]{1,0:T(8,128)} fusion(f32[9216,128]{1,0:T(8,128)} %bitcast_multiply_fusion, bf16[256,9216]{1,0:T(8,128)(2,1)} %copy-done.2, bf16[256,128]{1,0:T(8,128)(2,1)S(1)} %fusion.31), kind=kOutput, calls=%fused_computation | convolution fusion | flops 605159424 | bytes 14221312 | tf_op jit(solution)/shard_map/dot_general | solution.py:80
  179.1 274.9 %all-reduce.5.cloned.1.call-done = (f32[1024,128]{1,0:T(8,128)}, f32[1024,128]{1,0:T(8,128)}) async-done(((f32[1024,128]{1,0:T(8,128)}, f32[1024,128]{1,0:T(8,128)}), (f32[1024,128]{1,0:T(8,128)}, f32[1024,128]{1,0:T(8,128)})) %all-reduce.5.cloned.1.call-update) | async-done | bytes 1048592 | tf_op jit(solution)/shard_map/psum | solution.py:109
  454.1 2.3 broadcast_multiply_fusion
  456.3 208.1 %reduce-scatter.9.cloned.1.call-done = f32[96,128]{1,0:T(8,128)} async-done(((f32[9216,128]{1,0:T(8,128)}), f32[96,128]{1,0:T(8,128)}) %reduce-scatter.9.cloned.1.call-update) | async-done | bytes 49168 | tf_op jit(solution)/shard_map/reduce_scatter | solution.py:83
  664.4 1.4 broadcast_multiply_fusion.5
  (59 shorter events, 9.9 us)
Async XLA Ops:
  7.2 133.4 %copy-start = (f32[1024,128]{1,0:T(8,128)S(1)}, f32[1024,128]{1,0:T(8,128)}, u32[]{:S(2)}) copy-start(f32[1024,128]{1,0:T(8,128)} %param.35) | copy-start | bytes 1572868
  7.2 2.0 copy-start.1
  7.2 53.7 %reduce-scatter.13.cloned.1.call-start = ((), (), s32[]{:S(2)}) async-start(), calls=%async_computation.7 | async-start | bytes 589824
  9.7 2.5 copy-start.3
  10.0 3.7 copy-start.4
  10.1 2.1 copy-start.2
  13.7 6.3 copy-start.7
  15.6 91.4 %reduce-scatter.11.cloned.1.call-start = ((), (), s32[]{:S(2)}) async-start(), calls=%async_computation.6 | async-start | bytes 1179648 | tf_op jit(solution)/shard_map/reduce_scatter | solution.py:68
  43.1 85.3 %copy-start.5 = (f32[1,1024]{1,0:T(1,128)S(1)}, f32[1,1024]{1,0:T(1,128)}, u32[]{:S(2)}) copy-start(f32[1,1024]{1,0:T(1,128)} %param.34) | copy-start | bytes 12292
  44.7 126.0 %copy-start.6 = (f32[1,1024]{1,0:T(1,128)S(1)}, f32[1,1024]{1,0:T(1,128)}, u32[]{:S(2)}) copy-start(f32[1,1024]{1,0:T(1,128)} %param.33) | copy-start | bytes 12292
  109.3 31.1 %all-to-all-start = ((f32[96,1,128]{2,1,0:T(1,128)}), f32[96,1,128]{2,1,0:T(1,128)S(1)}, u32[]{:S(2)}, u32[]{:S(2)}) async-start(f32[96,1,128]{2,1,0:T(1,128)} %bitcast.58), calls=%async_computation.2 | async-start | bytes 98304 | tf_op jit(solution)/shard_map/all_to_all | solution.py:93
  128.3 41.4 %reduce-scatter.15.cloned.1.call-start = ((), (), s32[]{:S(2)}) async-start(), calls=%async_computation.8 | async-start | bytes 589824
  141.9 312.1 %all-reduce.5.cloned.1.call-start = ((), (), s32[]{:S(2)}) async-start(), calls=%async_computation.9 | async-start | bytes 2097152 | tf_op jit(solution)/shard_map/psum | solution.py:109
  171.7 492.7 %reduce-scatter.9.cloned.1.call-start = ((), (), s32[]{:S(2)}) async-start(), calls=%async_computation.5 | async-start | bytes 4767744 | tf_op jit(solution)/shard_map/reduce_scatter | solution.py:83
Sparse Core Ops, SparseCore 0:
  15.8 45.0 reduce-scatter.12
  64.3 42.7 reduce-scatter.10
  142.0 27.6 reduce-scatter.14
  173.7 280.2 all-reduce.4
  459.2 205.1 reduce-scatter.8
where the time goes:
time: 681 us; the launch traced here: 672 us
  waiting for transfers between devices  576 us (85%)
  matrix products  24.6 us (4%)
  starting transfers between devices  19.2 us (3%)
  local copies, waits for them, and re-layouts  18.9 us (3%)
  other arithmetic  17.6 us (3%)
  between operations  15.5 us (2%)
    psum x1, waiting for transfers between devices, local(): map_out_sum, map_in_sum = lax.psum((map_out_part, map_in_part), 'dp')  275 us
    reduce_scatter x1, waiting for transfers between devices, local(): lax.psum_scatter(product_rows + 2.0 * weight_part * tiled_factor, 'dp', s...  208 us
    reduce_scatter x1, waiting for transfers between devices, local(): lax.psum_scatter(inner_part, 'chan', scatter_dimension=3, tiled=True)  45.3 us
    unnamed x7, waiting for transfers between devices  36.2 us
    all_to_all x1, starting transfers between devices, local(): lax.all_to_all(send_rows.reshape(dp_count, samples, cols_dev), 'dp', spli...  19 us
  transfers between devices with their start and end apart: 6, of which 6 were waited for; matrix products, arithmetic and copies ran while one was open for 7% of the time, Pallas kernels for 0%

commit v1 on v0

v1 whole, which is shorter than its diff:
```python
import jax
import jax.numpy as jnp
from jax import lax
from jax.sharding import Mesh, PartitionSpec as P

KTAPS = 9
LAYER = 6
LANES = 128

highest = lax.Precision.HIGHEST


def dp_axes(dp_count):
    return (4, 12, 2) if dp_count == 96 else (2, dp_count // 4, 2)


def tap_window(padded, row_off, col_off, side_len):
    return padded[:, row_off : row_off + side_len, col_off : col_off + side_len, :]


def exchange(blocks, axes):
    return lax.all_to_all(blocks, axes, 0, 0, tiled=True)


def local(
    features, styles, conv_weight, grad_out, crossover, partner, latents, map_pre, map_weight
):
    samples, side_len, _, channels = features.shape
    cols_dev = conv_weight.shape[2]
    pixels = samples * side_len * side_len
    nx, nz, ncore, nchan = (lax.axis_size(name) for name in ("x", "z", "core", "chan"))
    batch_size = nx * nz * ncore
    rows_dev = KTAPS * channels // batch_size
    chan_id = lax.axis_index("chan")
    dp_id = (lax.axis_index("x") * nz + lax.axis_index("z")) * ncore + lax.axis_index("core")

    own_rows = jnp.concatenate(
        [latents.reshape(1, -1, LANES), map_pre.reshape(1, -1, LANES)], axis=1
    )
    gathered = exchange(
        jnp.broadcast_to(own_rows, (batch_size,) + own_rows.shape[1:]), ("x", "z", "core")
    )
    map_rows = exchange(map_weight.reshape(nchan, -1, cols_dev), "chan")

    scaled = (features.astype(jnp.float32) * styles[:, None, None, :]).astype(jnp.bfloat16)
    weight_sq = jnp.sum(jnp.square(conv_weight.astype(jnp.float32)), axis=0)
    style_sq = styles * styles
    demodulate = lax.rsqrt(jnp.dot(style_sq, weight_sq, precision=highest) + 1e-08)
    padded = jnp.pad(scaled, ((0, 0), (1, 1), (1, 1), (0, 0)))
    patches = jnp.concatenate(
        [
            tap_window(padded, tap // 3, tap % 3, side_len).reshape(pixels, channels)
            for tap in range(KTAPS)
        ],
        axis=1,
    )
    weight_flat = conv_weight.reshape(KTAPS * channels, cols_dev)
    conv_out = jnp.dot(patches, weight_flat, preferred_element_type=jnp.float32)
    grad_wide = grad_out.astype(jnp.float32).reshape(pixels, cols_dev)
    demod_grad = jnp.sum(grad_wide * conv_out, axis=0, keepdims=True)
    square_grad = -0.5 * demodulate**3 * demod_grad
    grad_scaled = (grad_wide * demodulate).astype(jnp.bfloat16)
    grad_padded = jnp.pad(
        grad_scaled.reshape(samples, side_len, side_len, cols_dev), ((0, 0), (1, 1), (1, 1), (0, 0))
    )
    inner_part = jnp.zeros((pixels, channels), jnp.float32)
    for tap in range(KTAPS):
        inner_part = inner_part + lax.dot_general(
            tap_window(grad_padded, 2 - tap // 3, 2 - tap % 3, side_len).reshape(pixels, cols_dev),
            conv_weight[tap],
            (((1,), (1,)), ((), ())),
            preferred_element_type=jnp.float32,
        )
    style_part = jnp.sum(
        inner_part * features.reshape(pixels, channels).astype(jnp.float32), axis=0
    ) + (2.0 * styles * jnp.dot(square_grad, weight_sq.T, precision=highest)).reshape(channels)

    grad_inner = lax.psum_scatter(inner_part, "chan", scatter_dimension=1, tiled=True)
    style_cols = lax.dynamic_slice_in_dim(styles, chan_id * cols_dev, cols_dev, 1)
    grad_input = (grad_inner * style_cols).astype(jnp.bfloat16)

    tile = style_part.reshape(1, -1, LANES)
    parts = exchange(
        jnp.broadcast_to(tile, (ncore * nchan,) + tile.shape[1:]), ("core", "chan")
    )
    style_grad = jnp.sum(parts.reshape(ncore, nchan, -1, LANES), axis=1)
    hidden_cols = jnp.sum(
        lax.dot_general(
            map_rows,
            style_grad.reshape(ncore, nchan, cols_dev),
            (((2,), (2,)), ((0,), (1,))),
            precision=highest,
        ),
        axis=0,
    ).T
    style_own = lax.dynamic_slice_in_dim(
        style_grad.reshape(ncore, nchan, cols_dev), chan_id, 1, 1
    ).reshape(ncore, cols_dev)
    source = jnp.where(crossover <= LAYER, partner, dp_id).astype(jnp.float32)
    source = lax.all_gather(
        jnp.broadcast_to(source[:, None], (1, cols_dev)), "core", axis=0, tiled=True
    )

    style_factor = jnp.dot(style_sq.T, square_grad, precision=highest)
    product_rows = lax.dot_general(
        patches, grad_scaled, (((0,), (0,)), ((), ())), preferred_element_type=jnp.float32
    ) + 2.0 * weight_flat.astype(jnp.float32) * jnp.tile(style_factor, (KTAPS, 1))
    pieces = product_rows.reshape(nx * nz, ncore, rows_dev, cols_dev).transpose(1, 0, 2, 3)
    pieces = jnp.sum(exchange(pieces, "core"), axis=0)
    pieces = pieces.reshape(nx, nz * rows_dev, cols_dev)
    pad_rows = jnp.zeros((8 - 3 * ncore, cols_dev), jnp.float32)
    riders = jnp.concatenate([style_own, hidden_cols, source, pad_rows], axis=0)
    moved = exchange(
        jnp.concatenate([pieces, jnp.broadcast_to(riders[None], (nx,) + riders.shape)], axis=1), "x"
    )
    pieces = jnp.sum(moved[:, : nz * rows_dev], axis=0).reshape(nz, rows_dev, cols_dev)
    riders = jnp.concatenate(
        [
            moved[:, nz * rows_dev + kind * ncore : nz * rows_dev + (kind + 1) * ncore].reshape(
                nx * ncore, cols_dev
            )
            for kind in range(3)
        ],
        axis=0,
    )
    moved = exchange(
        jnp.concatenate([pieces, jnp.broadcast_to(riders[None], (nz,) + riders.shape)], axis=1), "z"
    )
    grad_weight = jnp.sum(moved[:, :rows_dev], axis=0) / batch_size

    per = nx * ncore
    style_all, hidden_all, source_all = (
        moved[:, rows_dev + kind * per : rows_dev + (kind + 1) * per].reshape(batch_size, cols_dev)
        for kind in range(3)
    )
    matches = (
        source_all[:, :1] == lax.broadcasted_iota(jnp.int32, (1, batch_size), 1).astype(jnp.float32)
    ).astype(jnp.float32)
    received = lax.dot_general(
        matches,
        jnp.concatenate([style_all, hidden_all], axis=1),
        (((0,), (0,)), ((), ())),
        precision=highest,
    )
    incoming, hidden_grad = received[:, :cols_dev], received[:, cols_dev:]
    half = channels // LANES
    all_latents = gathered[:, :half].reshape(batch_size, -1)
    all_pre = gathered[:, half:].reshape(batch_size, -1)
    hidden = jnp.where(all_pre > 0, all_pre, 0.2 * all_pre)
    grad_map_out = (
        lax.dot_general(hidden, incoming, (((0,), (0,)), ((), ())), precision=highest) / batch_size
    )
    pre_cols = lax.dynamic_slice_in_dim(all_pre, chan_id * cols_dev, cols_dev, 1)
    pre_grad = hidden_grad * jnp.where(pre_cols > 0, 1.0, 0.2)
    grad_map_in = (
        lax.dot_general(all_latents, pre_grad, (((0,), (0,)), ((), ())), precision=highest)
        / batch_size
    )
    return (
        grad_weight,
        grad_input.reshape(samples, side_len, side_len, cols_dev),
        grad_map_out,
        grad_map_in,
    )


def solution(mesh):
    dp_count, chan_count = mesh.devices.shape
    split = Mesh(
        mesh.devices.reshape(dp_axes(dp_count) + (chan_count,)), ("x", "z", "core", "chan")
    )
    dp = ("x", "z", "core")
    in_specs = (
        P(dp, None, None, None),
        P(dp, None),
        P(None, None, "chan"),
        P(dp, None, None, "chan"),
        P(dp),
        P(dp),
        P(dp, None),
        P(dp, None),
        P(None, "chan"),
    )
    out_specs = (P(dp, "chan"), P(dp, None, None, "chan"), P(None, "chan"), P(None, "chan"))
    return jax.shard_map(local, mesh=split, in_specs=in_specs, out_specs=out_specs, check_vma=False)
```

time: 681 us -> 200 us (0.29)
  waiting for transfers between devices: 576 us -> 94.5 us
  starting transfers between devices: 19.2 us -> 42.2 us
  blocking collectives: 0 us -> 13 us
  matrix products: 24.6 us -> 11.9 us
  local copies, waits for them, and re-layouts: 18.9 us -> 6.69 us
    psum x1 -> x0, waiting for transfers between devices: 275 us -> none  [local(): map_out_sum, map_in_sum = lax.psum((map_out_part, map_in_part), 'dp')]
    reduce_scatter x2 -> x1, waiting for transfers between devices: 253 us -> 1.41 us  [local(): lax.psum_scatter(inner_part, 'chan', scatter_dimension=1, tiled=True)]
    all_to_all x1 -> x5, waiting for transfers between devices: 12 us -> 92.5 us  [exchange(): return lax.all_to_all(blocks, axes, 0, 0, tiled=True)]
    unnamed x7 -> x1, waiting for transfers between devices: 36.2 us -> 0.5 us
    all_to_all x1 -> x5, starting transfers between devices: 19 us -> 42 us  [exchange(): return lax.all_to_all(blocks, axes, 0, 0, tiled=True)]
    scatter-add x7 -> x0, local copies, waits for them, and re-layouts: 10.8 us -> none  [local(): accumulated = accumulated.at[:, row_off:row_off + side_len, col_off:col_o...]
    all_to_all x0 -> x1, blocking collectives: none -> 9.98 us  [exchange(): return lax.all_to_all(blocks, axes, 0, 0, tiled=True)]
  transfers between devices with their start and end apart: 6 -> 6, of which waited for: 6 -> 6; matrix products, arithmetic and copies ran while one was open for 7% -> 6% of each run, Pallas kernels for 0% -> 0%
where the time goes in v1:
time: 200 us; the launch traced here: 196 us
  waiting for transfers between devices  94.5 us (47%)
  starting transfers between devices  42.2 us (21%)
  between operations  15.8 us (8%)
  blocking collectives  13 us (6%)
  other arithmetic  12.3 us (6%)
  matrix products  11.9 us (6%)
  local copies, waits for them, and re-layouts  6.69 us (3%)
    all_to_all x5, waiting for transfers between devices, exchange(): return lax.all_to_all(blocks, axes, 0, 0, tiled=True)  92.5 us
    all_to_all x5, starting transfers between devices, exchange(): return lax.all_to_all(blocks, axes, 0, 0, tiled=True)  42 us
    all_to_all x1, blocking collectives, exchange(): return lax.all_to_all(blocks, axes, 0, 0, tiled=True)  9.98 us
  transfers between devices with their start and end apart: 6, of which 6 were waited for; matrix products, arithmetic and copies ran while one was open for 6% of the time, Pallas kernels for 0%

profile of v1, /device:TPU:1, one launch (start us, length us, event | category | flops | bytes accessed | tf_op | source)
XLA Modules:
  0.0 196.3 jit_solution(3683031929984550784)
XLA Ops:
  7.2 0.9 mul.95
  8.0 1.2 multiply_convert_fusion
  9.2 0.6 pad_slice_fusion
  11.2 1.4 fusion
  13.3 0.9 bitcast_multiply_fusion
  14.2 1.4 convolution_add_fusion
  15.7 2.5 %copy.30 = f32[48,2,96,128]{3,2,0,1:T(8,128)} copy(f32[48,2,96,128]{3,2,1,0:T(8,128)S(1)} %bitcast.138) | data formatting | bytes 9437184 | tf_op jit(solution)/shard_map/reshape | solution.py:108
  18.2 16.3 %all-to-all-start = ((f32[2,48,96,128]{3,2,1,0:T(8,128)}), f32[2,48,96,128]{3,2,1,0:T(8,128)}, u32[]{:S(2)}, u32[]{:S(2)}) async-start(f32[2,48,96,128]{3,2,1,0:T(8,128)} %bitcast.139), calls=%async_computation | async-start | bytes 9437184 | tf_op jit(solution)/shard_map/all_to_all | solution.py:22
  34.5 0.5 convolution_multiply_fusion.3
  37.6 1.3 fusion.3
  39.0 10.0 %all_to_all.30 = f32[16,8,128]{2,1,0:T(8,128)S(1)} all-to-all(f32[16,8,128]{2,1,0:T(8,128)S(1)} %broadcast_in_dim.49), channel_id=1, replica_groups=mesh['x'=4,'z'=12,'core'=2,'chan'=8] {'core','chan'}, dimensions={0} | all-to-all | bytes 131072 | tf_op jit(solution)/shard_map/all_to_all | solution.py:22
  49.0 3.5 %all-to-all-start.2 = ((f32[8,128,128]{2,1,0:T(8,128)}), f32[8,128,128]{2,1,0:T(8,128)S(1)}, u32[]{:S(2)}, u32[]{:S(2)}) async-start(f32[8,128,128]{2,1,0:T(8,128)} %bitcast.44), calls=%async_computation.2 | async-start | bytes 1048576 | tf_op jit(solution)/shard_map/all_to_all | solution.py:22
  53.8 1.3 dynamic-slice
  55.0 0.7 fusion.47
  55.8 3.0 %all-reduce.2 = f32[2]{0:T(128)S(1)} all-reduce(f32[2]{0:T(128)S(1)} %fusion.47), channel_id=3, replica_groups=mesh['x'=4,'z'=12,'core'=2,'chan'=8] {'core'}, use_global_device_ids=true, to_apply=%add.2 | all-reduce | flops 2 | bytes 16
  58.9 3.0 %reduce_sum.71 = f32[48,96,128]{2,1,0:T(8,128)S(1)} reduce(f32[2,48,96,128]{3,2,1,0:T(8,128)} %all-to-all-done, f32[]{:T(128)} %constant.22.clone.1), dimensions={0}, to_apply=%region_2.3 | reduce | flops 589824 | bytes 7077892 | tf_op jit(solution)/shard_map/reduce_sum | solution.py:109
  61.9 8.4 %all-to-all-done.2 = f32[8,128,128]{2,1,0:T(8,128)S(1)} async-done(((f32[8,128,128]{2,1,0:T(8,128)}), f32[8,128,128]{2,1,0:T(8,128)S(1)}, u32[]{:S(2)}, u32[]{:S(2)}) %all-to-all-start.2) | async-done | bytes 524320 | tf_op jit(solution)/shard_map/all_to_all | solution.py:22
  70.3 0.5 convolution_bitcast_fusion
  70.9 1.6 pad_maximum_fusion
  72.5 3.6 %all-to-all-start.3 = ((f32[4,1160,128]{2,1,0:T(8,128)}), f32[4,1160,128]{2,1,0:T(8,128)S(1)}, u32[]{:S(2)}, u32[]{:S(2)}) async-start(f32[4,1160,128]{2,1,0:T(8,128)} %pad_maximum_fusion), calls=%async_computation.3 | async-start | bytes 4751360 | tf_op jit(solution)/shard_map/all_to_all | solution.py:22
  76.2 28.9 %all-to-all-done.3 = f32[4,1160,128]{2,1,0:T(8,128)S(1)} async-done(((f32[4,1160,128]{2,1,0:T(8,128)}), f32[4,1160,128]{2,1,0:T(8,128)S(1)}, u32[]{:S(2)}, u32[]{:S(2)}) %all-to-all-start.3) | async-done | bytes 2375712 | tf_op jit(solution)/shard_map/all_to_all | solution.py:22
  105.0 0.9 broadcast_in_dim.57
  106.0 13.9 %all-to-all-start.5 = ((f32[96,16,128]{2,1,0:T(8,128)}), f32[96,16,128]{2,1,0:T(8,128)S(1)}, u32[]{:S(2)}, u32[]{:S(2)}) async-start(f32[96,16,128]{2,1,0:T(8,128)} %broadcast_in_dim.57), calls=%async_computation.6 | async-start | bytes 1572864 | tf_op jit(solution)/shard_map/all_to_all | solution.py:22
  120.7 0.9 pad_maximum_fusion.1
  121.7 31.4 %all-to-all-done.5 = f32[96,16,128]{2,1,0:T(8,128)S(1)} async-done(((f32[96,16,128]{2,1,0:T(8,128)}), f32[96,16,128]{2,1,0:T(8,128)S(1)}, u32[]{:S(2)}, u32[]{:S(2)}) %all-to-all-start.5) | async-done | bytes 786464 | tf_op jit(solution)/shard_map/all_to_all | solution.py:22
  153.1 4.7 %all-to-all-start.4 = ((f32[12,120,128]{2,1,0:T(8,128)}), f32[12,120,128]{2,1,0:T(8,128)S(1)}, u32[]{:S(2)}, u32[]{:S(2)}) async-start(f32[12,120,128]{2,1,0:T(8,128)} %pad_maximum_fusion.1), calls=%async_computation.4 | async-start | bytes 1474560 | tf_op jit(solution)/shard_map/all_to_all | solution.py:22
  157.9 1.4 reduce-scatter.2.cloned.1.call-done
  159.3 1.5 multiply_convert_fusion.1
  160.9 23.8 %all-to-all-done.4 = f32[12,120,128]{2,1,0:T(8,128)S(1)} async-done(((f32[12,120,128]{2,1,0:T(8,128)}), f32[12,120,128]{2,1,0:T(8,128)S(1)}, u32[]{:S(2)}, u32[]{:S(2)}) %all-to-all-start.4) | async-done | bytes 737312 | tf_op jit(solution)/shard_map/all_to_all | solution.py:22
  185.2 1.8 convolution_multiply_fusion.1
  187.0 0.6 broadcast_multiply_fusion.1
  187.6 1.8 convolution_multiply_fusion
  (61 shorter events, 6.3 us)
Async XLA Ops:
  7.2 2.7 %copy-start = (bf16[9,1024,128]{2,1,0:T(8,128)(2,1)S(1)}, bf16[9,1024,128]{2,1,0:T(8,128)(2,1)}, u32[]{:S(2)}) copy-start(bf16[9,1024,128]{2,1,0:T(8,128)(2,1)} %param.11) | copy-start | bytes 7077892
  10.4 0.8 copy-start.2
  10.7 2.0 %copy-start.3 = (f32[1,1024]{1,0:T(1,128)S(1)}, f32[1,1024]{1,0:T(1,128)}, u32[]{:S(2)}) copy-start(f32[1,1024]{1,0:T(1,128)} %param.10) | copy-start | bytes 12292
  18.2 20.8 %all-to-all-start = ((f32[2,48,96,128]{3,2,1,0:T(8,128)}), f32[2,48,96,128]{3,2,1,0:T(8,128)}, u32[]{:S(2)}, u32[]{:S(2)}) async-start(f32[2,48,96,128]{3,2,1,0:T(8,128)} %bitcast.139), calls=%async_computation | async-start | bytes 9437184 | tf_op jit(solution)/shard_map/all_to_all | solution.py:22
  36.3 1.2 copy-start.1
  49.0 21.4 %all-to-all-start.2 = ((f32[8,128,128]{2,1,0:T(8,128)}), f32[8,128,128]{2,1,0:T(8,128)S(1)}, u32[]{:S(2)}, u32[]{:S(2)}) async-start(f32[8,128,128]{2,1,0:T(8,128)} %bitcast.44), calls=%async_computation.2 | async-start | bytes 1048576 | tf_op jit(solution)/shard_map/all_to_all | solution.py:22
  70.9 5.2 %copy-start.4 = (f32[1,1024]{1,0:T(1,128)S(1)}, f32[1,1024]{1,0:T(1,128)}, u32[]{:S(2)}) copy-start(f32[1,1024]{1,0:T(1,128)} %param.16) | copy-start | bytes 12292
  70.9 5.2 %copy-start.5 = (f32[1,1024]{1,0:T(1,128)S(1)}, f32[1,1024]{1,0:T(1,128)}, u32[]{:S(2)}) copy-start(f32[1,1024]{1,0:T(1,128)} %param.15) | copy-start | bytes 12292
  72.5 32.5 %all-to-all-start.3 = ((f32[4,1160,128]{2,1,0:T(8,128)}), f32[4,1160,128]{2,1,0:T(8,128)S(1)}, u32[]{:S(2)}, u32[]{:S(2)}) async-start(f32[4,1160,128]{2,1,0:T(8,128)} %pad_maximum_fusion), calls=%async_computation.3 | async-start | bytes 4751360 | tf_op jit(solution)/shard_map/all_to_all | solution.py:22
  106.0 47.1 %all-to-all-start.5 = ((f32[96,16,128]{2,1,0:T(8,128)}), f32[96,16,128]{2,1,0:T(8,128)S(1)}, u32[]{:S(2)}, u32[]{:S(2)}) async-start(f32[96,16,128]{2,1,0:T(8,128)} %broadcast_in_dim.57), calls=%async_computation.6 | async-start | bytes 1572864 | tf_op jit(solution)/shard_map/all_to_all | solution.py:22
  119.8 39.4 %reduce-scatter.2.cloned.1.call-start = ((), (), s32[]{:S(2)}) async-start(), calls=%async_computation.7 | async-start | bytes 1179648 | tf_op jit(solution)/shard_map/reduce_scatter | solution.py:78
  153.1 31.6 %all-to-all-start.4 = ((f32[12,120,128]{2,1,0:T(8,128)}), f32[12,120,128]{2,1,0:T(8,128)S(1)}, u32[]{:S(2)}, u32[]{:S(2)}) async-start(f32[12,120,128]{2,1,0:T(8,128)} %pad_maximum_fusion.1), calls=%async_computation.4 | async-start | bytes 1474560 | tf_op jit(solution)/shard_map/all_to_all | solution.py:22
Sparse Core Ops, SparseCore 0:
  123.8 35.4 reduce-scatter.1

commit v2 on v1

--- a/solution.py
+++ b/solution.py
@@ -1,5 +1,6 @@
 import jax
 import jax.numpy as jnp
+import numpy as np
 from jax import lax
 from jax.sharding import Mesh, PartitionSpec as P
 
@@ -34,12 +35,29 @@
     chan_id = lax.axis_index("chan")
     dp_id = (lax.axis_index("x") * nz + lax.axis_index("z")) * ncore + lax.axis_index("core")
 
-    own_rows = jnp.concatenate(
+    gathered = jnp.concatenate(
         [latents.reshape(1, -1, LANES), map_pre.reshape(1, -1, LANES)], axis=1
     )
-    gathered = exchange(
-        jnp.broadcast_to(own_rows, (batch_size,) + own_rows.shape[1:]), ("x", "z", "core")
-    )
+    offsets = np.zeros((3, 1), np.int32)
+    for name, axis in (("z", 1), ("core", 2), ("x", 0)):
+        size, have = lax.axis_size(name), 1
+        per = gathered.shape[0]
+        unit = (np.arange(3) == axis).astype(np.int32)[:, None]
+        while have < size:
+            extra = min(have, size - have)
+            coming = lax.ppermute(
+                gathered[: extra * per],
+                name,
+                [(sender, (sender + have) % size) for sender in range(size)],
+            )
+            gathered = jnp.concatenate([gathered, coming], axis=0)
+            offsets = np.concatenate([offsets, offsets[:, : extra * per] + have * unit], axis=1)
+            have += extra
+    spots = [
+        (lax.axis_index(name) + lax.axis_size(name) - offsets[axis]) % lax.axis_size(name)
+        for axis, name in enumerate(("x", "z", "core"))
+    ]
+    row_ids = ((spots[0] * nz + spots[1]) * ncore + spots[2]).astype(jnp.float32)
     map_rows = exchange(map_weight.reshape(nchan, -1, cols_dev), "chan")
 
     scaled = (features.astype(jnp.float32) * styles[:, None, None, :]).astype(jnp.bfloat16)
@@ -79,11 +97,20 @@
     style_cols = lax.dynamic_slice_in_dim(styles, chan_id * cols_dev, cols_dev, 1)
     grad_input = (grad_inner * style_cols).astype(jnp.bfloat16)
 
-    tile = style_part.reshape(1, -1, LANES)
+    source = jnp.where(crossover <= LAYER, partner, dp_id).astype(jnp.float32)
+    tile = jnp.concatenate(
+        [
+            style_part.reshape(1, -1, LANES),
+            jnp.broadcast_to(source[:, None, None], (1, 8, LANES)),
+        ],
+        axis=1,
+    )
+    tile, map_rows = lax.optimization_barrier((tile, map_rows))
     parts = exchange(
         jnp.broadcast_to(tile, (ncore * nchan,) + tile.shape[1:]), ("core", "chan")
-    )
-    style_grad = jnp.sum(parts.reshape(ncore, nchan, -1, LANES), axis=1)
+    ).reshape(ncore, nchan, -1, LANES)
+    style_grad = jnp.sum(parts[:, :, :-8], axis=1)
+    source = parts[:, 0, -1]
     hidden_cols = jnp.sum(
         lax.dot_general(
             map_rows,
@@ -96,16 +123,13 @@
     style_own = lax.dynamic_slice_in_dim(
         style_grad.reshape(ncore, nchan, cols_dev), chan_id, 1, 1
     ).reshape(ncore, cols_dev)
-    source = jnp.where(crossover <= LAYER, partner, dp_id).astype(jnp.float32)
-    source = lax.all_gather(
-        jnp.broadcast_to(source[:, None], (1, cols_dev)), "core", axis=0, tiled=True
-    )
 
     style_factor = jnp.dot(style_sq.T, square_grad, precision=highest)
     product_rows = lax.dot_general(
         patches, grad_scaled, (((0,), (0,)), ((), ())), preferred_element_type=jnp.float32
     ) + 2.0 * weight_flat.astype(jnp.float32) * jnp.tile(style_factor, (KTAPS, 1))
     pieces = product_rows.reshape(nx * nz, ncore, rows_dev, cols_dev).transpose(1, 0, 2, 3)
+    pieces, parts = lax.optimization_barrier((pieces, parts))
     pieces = jnp.sum(exchange(pieces, "core"), axis=0)
     pieces = pieces.reshape(nx, nz * rows_dev, cols_dev)
     pad_rows = jnp.zeros((8 - 3 * ncore, cols_dev), jnp.float32)
@@ -134,7 +158,7 @@
         for kind in range(3)
     )
     matches = (
-        source_all[:, :1] == lax.broadcasted_iota(jnp.int32, (1, batch_size), 1).astype(jnp.float32)
+        source_all[:, :1] == row_ids[None, :]
     ).astype(jnp.float32)
     received = lax.dot_general(
         matches,

time: 200 us -> 195 us (0.975)
  waiting for transfers between devices: 94.5 us -> 62.1 us
  starting transfers between devices: 42.2 us -> 63.9 us
  blocking collectives: 13 us -> 0 us
  matrix products: 11.9 us -> 18.8 us
  local copies, waits for them, and re-layouts: 6.69 us -> 13.5 us
  other arithmetic: 12.3 us -> 17.4 us
    all_to_all x5, waiting for transfers between devices: 92.5 us -> 20.2 us  [exchange(): return lax.all_to_all(blocks, axes, 0, 0, tiled=True)]
    ppermute x0 -> x7, waiting for transfers between devices: none -> 41.9 us  [local(): lax.ppermute(gathered[:extra * per], name, [(sender, (sender + have) % si...]
    ppermute x0 -> x7, starting transfers between devices: none -> 23.5 us  [local(): lax.ppermute(gathered[:extra * per], name, [(sender, (sender + have) % si...]
    all_to_all x1 -> x0, blocking collectives: 9.98 us -> none  [exchange(): return lax.all_to_all(blocks, axes, 0, 0, tiled=True)]
    dot_general x1, matrix products: 1.45 us -> 7.42 us  [local(): lax.dot_general(patches, grad_scaled, (((0,), (0,)), ((), ())), preferred...]
    mul x1, other arithmetic: 0.9 us -> 4.47 us  [local(): 2.0 * weight_flat.astype(jnp.float32) * jnp.tile(style_factor, (KTAPS, 1))]
    unnamed x24 -> x50, local copies, waits for them, and re-layouts: 2.13 us -> 5.56 us
    unnamed x1 -> x0, blocking collectives: 2.98 us -> none
  transfers between devices with their start and end apart: 6 -> 13, of which waited for: 6 -> 8; matrix products, arithmetic and copies ran while one was open for 6% -> 19% of each run, Pallas kernels for 0% -> 0%
where the time goes in v2:
time: 195 us; the launch traced here: 192 us
  starting transfers between devices  63.9 us (33%)
  waiting for transfers between devices  62.1 us (32%)
  matrix products  18.8 us (10%)
  other arithmetic  17.4 us (9%)
  between operations  16 us (8%)
  local copies, waits for them, and re-layouts  13.5 us (7%)
    ppermute x7, waiting for transfers between devices, local(): lax.ppermute(gathered[:extra * per], name, [(sender, (sender + have) % si...  41.9 us
    all_to_all x5, starting transfers between devices, exchange(): return lax.all_to_all(blocks, axes, 0, 0, tiled=True)  40.3 us
    ppermute x7, starting transfers between devices, local(): lax.ppermute(gathered[:extra * per], name, [(sender, (sender + have) % si...  23.5 us
    all_to_all x5, waiting for transfers between devices, exchange(): return lax.all_to_all(blocks, axes, 0, 0, tiled=True)  20.2 us
    dot_general x1, matrix products, local(): lax.dot_general(patches, grad_scaled, (((0,), (0,)), ((), ())), preferred...  7.42 us
    unnamed x50, local copies, waits for them, and re-layouts  5.56 us
    reshape x1, local copies, waits for them, and re-layouts, local(): product_rows.reshape(nx * nz, ncore, rows_dev, cols_dev)  4.87 us
    dot_general x9, matrix products, local(): lax.dot_general(tap_window(grad_padded, 2 - tap // 3, 2 - tap % 3, side_l...  4.67 us
  transfers between devices with their start and end apart: 13, of which 8 were waited for; matrix products, arithmetic and copies ran while one was open for 19% of the time, Pallas kernels for 0%

profile of v2, /device:TPU:1, one launch (start us, length us, event | category | flops | bytes accessed | tf_op | source)
XLA Modules:
  0.0 191.7 jit_solution(4734044038252527468)
XLA Ops:
  7.2 7.7 %all-to-all-start = ((f32[8,128,128]{2,1,0:T(8,128)}), f32[8,128,128]{2,1,0:T(8,128)S(1)}, u32[]{:S(2)}, u32[]{:S(2)}) async-start(f32[8,128,128]{2,1,0:T(8,128)} %bitcast.157), calls=%async_computation | async-start | bytes 1048576 | tf_op jit(solution)/shard_map/all_to_all | solution.py:23
  14.8 2.2 %multiply_reduce_fusion = f32[1024,128]{1,0:T(8,128)S(1)} fusion(bf16[9,1024,128]{2,1,0:T(8,128)(2,1)} %param.14), kind=kLoop, calls=%fused_computation.3 | loop fusion | flops 3407872 | bytes 2883584 | tf_op jit(solution)/shard_map/reduce_sum | solution.py:64
  20.0 1.9 copy-done
  21.9 1.4 fusion
  24.5 1.3 fusion.14
  27.4 4.5 %bitcast_multiply_fusion = f32[9216,128]{1,0:T(8,128)} fusion(f32[1024,128]{1,0:T(8,128)S(1)} %broadcast_multiply_fusion, bf16[9,1024,128]{2,1,0:T(8,128)(2,1)S(1)} %copy-done), kind=kLoop, calls=%fused_computation.1 | loop fusion | flops 3538944 | bytes 7602176 | tf_op jit(solution)/shard_map/mul | solution.py:130
  34.6 1.3 fusion.3
  36.6 13.5 %all-to-all-start.1 = ((f32[16,16,128]{2,1,0:T(8,128)}), f32[16,16,128]{2,1,0:T(8,128)S(1)}, u32[]{:S(2)}, u32[]{:S(2)}) async-start(f32[16,16,128]{2,1,0:T(8,128)} %broadcast_in_dim.46), calls=%async_computation.1 | async-start | bytes 262144 | tf_op jit(solution)/shard_map/all_to_all | solution.py:23
  50.1 7.4 %convolution_add_fusion = f32[9216,128]{1,0:T(8,128)} fusion(f32[9216,128]{1,0:T(8,128)} %bitcast_multiply_fusion, bf16[256,9216]{1,0:T(8,128)(2,1)} %copy-done.1, bf16[256,128]{1,0:T(8,128)(2,1)S(1)} %fusion.27), kind=kOutput, calls=%fused_computation | convolution fusion | flops 605159424 | bytes 14221312 | tf_op jit(solution)/shard_map/dot_general | solution.py:128
  57.6 4.9 %copy.36 = f32[48,2,96,128]{3,2,0,1:T(8,128)} copy(f32[48,2,96,128]{3,2,1,0:T(8,128)} %bitcast.139) | data formatting | bytes 9437184 | tf_op jit(solution)/shard_map/reshape | solution.py:131
  63.1 5.9 %all-to-all-start.2 = ((f32[2,48,96,128]{3,2,1,0:T(8,128)}), f32[2,48,96,128]{3,2,1,0:T(8,128)}, u32[]{:S(2)}, u32[]{:S(2)}) async-start(f32[2,48,96,128]{3,2,1,0:T(8,128)} %bitcast.140), calls=%async_computation.2 | async-start | bytes 9437184 | tf_op jit(solution)/shard_map/all_to_all | solution.py:23
  69.0 4.4 %all-to-all-done.2 = f32[2,48,96,128]{3,2,1,0:T(8,128)} async-done(((f32[2,48,96,128]{3,2,1,0:T(8,128)}), f32[2,48,96,128]{3,2,1,0:T(8,128)}, u32[]{:S(2)}, u32[]{:S(2)}) %all-to-all-start.2) | async-done | bytes 4718624 | tf_op jit(solution)/shard_map/all_to_all | solution.py:23
  73.4 3.0 %reduce_sum.73 = f32[48,96,128]{2,1,0:T(8,128)S(1)} reduce(f32[2,48,96,128]{3,2,1,0:T(8,128)} %all-to-all-done.2, f32[]{:T(128)} %constant.35.clone.1), dimensions={0}, to_apply=%region_3.4 | reduce | flops 589824 | bytes 7077892 | tf_op jit(solution)/shard_map/reduce_sum | solution.py:133
  76.5 1.6 pad_maximum_fusion
  78.1 3.6 %all-to-all-start.3 = ((f32[4,1160,128]{2,1,0:T(8,128)}), f32[4,1160,128]{2,1,0:T(8,128)S(1)}, u32[]{:S(2)}, u32[]{:S(2)}) async-start(f32[4,1160,128]{2,1,0:T(8,128)} %pad_maximum_fusion), calls=%async_computation.3 | async-start | bytes 4751360 | tf_op jit(solution)/shard_map/all_to_all | solution.py:23
  82.4 1.9 collective-permute-start
  84.4 8.7 %collective-permute-done = f32[1,16,128]{2,1,0:T(8,128)S(1)} collective-permute-done((f32[1,16,128]{2,1,0:T(8,128)S(1)}, f32[1,16,128]{2,1,0:T(8,128)S(1)}, u32[]{:S(2)}, u32[]{:S(2)}) %collective-permute-start) | collective-permute-done | bytes 8224 | tf_op jit(solution)/shard_map/ppermute | solution.py:48
  93.1 1.9 collective-permute-start.1
  95.0 15.8 %all-to-all-done.3 = f32[4,1160,128]{2,1,0:T(8,128)S(1)} async-done(((f32[4,1160,128]{2,1,0:T(8,128)}), f32[4,1160,128]{2,1,0:T(8,128)S(1)}, u32[]{:S(2)}, u32[]{:S(2)}) %all-to-all-start.3) | async-done | bytes 2375712 | tf_op jit(solution)/shard_map/all_to_all | solution.py:23
  111.8 9.6 %all-to-all-start.4 = ((f32[12,120,128]{2,1,0:T(8,128)}), f32[12,120,128]{2,1,0:T(8,128)S(1)}, u32[]{:S(2)}, u32[]{:S(2)}) async-start(f32[12,120,128]{2,1,0:T(8,128)} %pad_maximum_fusion.1), calls=%async_computation.4 | async-start | bytes 1474560 | tf_op jit(solution)/shard_map/all_to_all | solution.py:23
  122.1 7.2 %collective-permute-start.2 = (f32[4,16,128]{2,1,0:T(8,128)S(1)}, f32[4,16,128]{2,1,0:T(8,128)S(1)}, u32[]{:S(2)}, u32[]{:S(2)}) collective-permute-start(f32[4,16,128]{2,1,0:T(8,128)S(1)} %pad_maximum_fusion.2), channel_id=1, source_target_pairs={{0,64},{16,80},{32,96},{48,112},{64,128},{80,144},{96,160},{112,17... | collective-permute-start | bytes 98312 | tf_op jit(solution)/shard_map/ppermute | solution.py:48
  129.3 2.0 %collective-permute-start.3 = (f32[4,16,128]{2,1,0:T(8,128)S(1)}, f32[4,16,128]{2,1,0:T(8,128)S(1)}, u32[]{:S(2)}, u32[]{:S(2)}) collective-permute-start(f32[4,16,128]{2,1,0:T(8,128)S(1)} %pad_maximum_fusion.2), channel_id=1, source_target_pairs={{0,128},{16,144},{32,160},{48,176},{64,0},{80,16},{96,32},{112,48}... | collective-permute-start | bytes 98312 | tf_op jit(solution)/shard_map/ppermute | solution.py:48
  131.9 8.3 %collective-permute-done.2 = f32[4,16,128]{2,1,0:T(8,128)S(1)} collective-permute-done((f32[4,16,128]{2,1,0:T(8,128)S(1)}, f32[4,16,128]{2,1,0:T(8,128)S(1)}, u32[]{:S(2)}, u32[]{:S(2)}) %collective-permute-start.2) | collective-permute-done | bytes 32800 | tf_op jit(solution)/shard_map/ppermute | solution.py:48
  140.8 6.0 %collective-permute-done.3 = f32[4,16,128]{2,1,0:T(8,128)S(1)} collective-permute-done((f32[4,16,128]{2,1,0:T(8,128)S(1)}, f32[4,16,128]{2,1,0:T(8,128)S(1)}, u32[]{:S(2)}, u32[]{:S(2)}) %collective-permute-start.3) | collective-permute-done | bytes 32800 | tf_op jit(solution)/shard_map/ppermute | solution.py:48
  147.5 6.1 %collective-permute-start.4 = (f32[12,16,128]{2,1,0:T(8,128)S(1)}, f32[12,16,128]{2,1,0:T(8,128)S(1)}, u32[]{:S(2)}, u32[]{:S(2)}) collective-permute-start(f32[12,16,128]{2,1,0:T(8,128)S(1)} %get-tuple-element.42), channel_id=1, source_target_pairs={{0,8},{8,0},{1,9},{9,1},{2,10},{10,2},{3,11},{11,3},{4,12},{12,4},... | collective-permute-start | bytes 294920 | tf_op jit(solution)/shard_map/ppermute | solution.py:48
  155.2 2.3 %collective-permute-start.5 = (f32[24,16,128]{2,1,0:T(8,128)}, f32[24,16,128]{2,1,0:T(8,128)S(1)}, u32[]{:S(2)}, u32[]{:S(2)}) collective-permute-start(f32[24,16,128]{2,1,0:T(8,128)} %get-tuple-element.30), channel_id=1, source_target_pairs={{0,192},{192,384},{384,576},{576,0},{1,193},{193,385},{385,577},{5... | collective-permute-start | bytes 589832 | tf_op jit(solution)/shard_map/ppermute | solution.py:48
  157.5 7.1 %collective-permute-done.5 = f32[24,16,128]{2,1,0:T(8,128)S(1)} collective-permute-done((f32[24,16,128]{2,1,0:T(8,128)}, f32[24,16,128]{2,1,0:T(8,128)S(1)}, u32[]{:S(2)}, u32[]{:S(2)}) %collective-permute-start.5) | collective-permute-done | bytes 196640 | tf_op jit(solution)/shard_map/ppermute | solution.py:48
  165.3 2.1 %collective-permute-start.6 = (f32[48,16,128]{2,1,0:T(8,128)}, f32[48,16,128]{2,1,0:T(8,128)S(1)}, u32[]{:S(2)}, u32[]{:S(2)}) collective-permute-start(f32[48,16,128]{2,1,0:T(8,128)} %get-tuple-element.26), channel_id=1, source_target_pairs={{0,384},{192,576},{384,0},{576,192},{1,385},{193,577},{385,1},{577... | collective-permute-start | bytes 1179656 | tf_op jit(solution)/shard_map/ppermute | solution.py:48
  167.5 10.8 %collective-permute-done.6 = f32[48,16,128]{2,1,0:T(8,128)S(1)} collective-permute-done((f32[48,16,128]{2,1,0:T(8,128)}, f32[48,16,128]{2,1,0:T(8,128)S(1)}, u32[]{:S(2)}, u32[]{:S(2)}) %collective-permute-start.6) | collective-permute-done | bytes 393248 | tf_op jit(solution)/shard_map/ppermute | solution.py:48
  178.6 1.5 multiply_convert_fusion.1
  181.2 1.8 convolution_multiply_fusion.1
  183.0 1.8 convolution_multiply_fusion
  (103 shorter events, 16.2 us)
Async XLA Ops:
  7.2 28.8 %all-to-all-start = ((f32[8,128,128]{2,1,0:T(8,128)}), f32[8,128,128]{2,1,0:T(8,128)S(1)}, u32[]{:S(2)}, u32[]{:S(2)}) async-start(f32[8,128,128]{2,1,0:T(8,128)} %bitcast.157), calls=%async_computation | async-start | bytes 1048576 | tf_op jit(solution)/shard_map/all_to_all | solution.py:23
  19.6 2.3 %copy-start = (bf16[9,1024,128]{2,1,0:T(8,128)(2,1)S(1)}, bf16[9,1024,128]{2,1,0:T(8,128)(2,1)}, u32[]{:S(2)}) copy-start(bf16[9,1024,128]{2,1,0:T(8,128)(2,1)} %param.14) | copy-start | bytes 7077892
  19.6 2.3 %copy-start.4 = (bf16[1,16,16,128]{3,2,1,0:T(8,128)(2,1)S(1)}, bf16[1,16,16,128]{3,2,1,0:T(8,128)(2,1)}, u32[]{:S(2)}) copy-start(bf16[1,16,16,128]{3,2,1,0:T(8,128)(2,1)} %param.15) | copy-start | bytes 196612
  19.9 3.4 %copy-start.12 = (f32[1,1024]{1,0:T(1,128)S(1)}, f32[1,1024]{1,0:T(1,128)}, u32[]{:S(2)}) copy-start(f32[1,1024]{1,0:T(1,128)} %param.13) | copy-start | bytes 12292
  20.0 5.8 %copy-start.1 = (bf16[256,9216]{1,0:T(8,128)(2,1)}, bf16[256,9216]{1,0:T(8,128)(2,1)S(1)}, u32[]{:S(2)}) copy-start(bf16[256,9216]{1,0:T(8,128)(2,1)S(1)} %constant_dynamic-update-slice_fusion) | copy-start | bytes 14155780
  27.1 4.7 %copy-start.2 = (f32[256,1024]{1,0:T(8,128)S(1)}, f32[256,1024]{1,0:T(8,128)}, u32[]{:S(2)}) copy-start(f32[256,1024]{1,0:T(8,128)} %fusion.14) | copy-start | bytes 3145732
  27.1 4.7 %copy-start.11 = (bf16[1,16,16,128]{3,2,1,0:T(8,128)(2,1)S(1)}, bf16[1,16,16,128]{3,2,1,0:T(8,128)(2,1)}, u32[]{:S(2)}) copy-start(bf16[1,16,16,128]{3,2,1,0:T(8,128)(2,1)} %get-tuple-element.32) | copy-start | bytes 196612
  27.4 4.8 %copy-start.10 = (bf16[1,16,16,128]{3,2,1,0:T(8,128)(2,1)S(1)}, bf16[1,16,16,128]{3,2,1,0:T(8,128)(2,1)}, u32[]{:S(2)}) copy-start(bf16[1,16,16,128]{3,2,1,0:T(8,128)(2,1)} %get-tuple-element.33) | copy-start | bytes 196612
  27.4 5.1 %copy-start.9 = (bf16[1,16,16,128]{3,2,1,0:T(8,128)(2,1)S(1)}, bf16[1,16,16,128]{3,2,1,0:T(8,128)(2,1)}, u32[]{:S(2)}) copy-start(bf16[1,16,16,128]{3,2,1,0:T(8,128)(2,1)} %get-tuple-element.34) | copy-start | bytes 196612
  31.9 1.3 copy-start.8
  32.2 1.3 copy-start.7
  32.5 1.3 copy-start.6
  32.8 1.8 copy-start.3
  32.8 1.8 copy-start.5
  36.6 25.9 %all-to-all-start.1 = ((f32[16,16,128]{2,1,0:T(8,128)}), f32[16,16,128]{2,1,0:T(8,128)S(1)}, u32[]{:S(2)}, u32[]{:S(2)}) async-start(f32[16,16,128]{2,1,0:T(8,128)} %broadcast_in_dim.46), calls=%async_computation.1 | async-start | bytes 262144 | tf_op jit(solution)/shard_map/all_to_all | solution.py:23
  63.1 10.4 %all-to-all-start.2 = ((f32[2,48,96,128]{3,2,1,0:T(8,128)}), f32[2,48,96,128]{3,2,1,0:T(8,128)}, u32[]{:S(2)}, u32[]{:S(2)}) async-start(f32[2,48,96,128]{3,2,1,0:T(8,128)} %bitcast.140), calls=%async_computation.2 | async-start | bytes 9437184 | tf_op jit(solution)/shard_map/all_to_all | solution.py:23
  76.4 5.4 %copy-start.13 = (f32[1,1024]{1,0:T(1,128)S(1)}, f32[1,1024]{1,0:T(1,128)}, u32[]{:S(2)}) copy-start(f32[1,1024]{1,0:T(1,128)} %param.19) | copy-start | bytes 12292
  76.4 5.4 %copy-start.14 = (f32[1,1024]{1,0:T(1,128)S(1)}, f32[1,1024]{1,0:T(1,128)}, u32[]{:S(2)}) copy-start(f32[1,1024]{1,0:T(1,128)} %param.18) | copy-start | bytes 12292
  78.1 32.7 %all-to-all-start.3 = ((f32[4,1160,128]{2,1,0:T(8,128)}), f32[4,1160,128]{2,1,0:T(8,128)S(1)}, u32[]{:S(2)}, u32[]{:S(2)}) async-start(f32[4,1160,128]{2,1,0:T(8,128)} %pad_maximum_fusion), calls=%async_computation.3 | async-start | bytes 4751360 | tf_op jit(solution)/shard_map/all_to_all | solution.py:23
  81.7 85.8 %copy-start.15 = (s32[96]{0:T(128)S(1)}, s32[96]{0:T(128)}, u32[]{:S(2)}) copy-start(s32[96]{0:T(128)} %constant.112) | copy-start | bytes 1156
  81.7 85.8 %copy-start.16 = (s32[96]{0:T(128)S(1)}, s32[96]{0:T(128)}, u32[]{:S(2)}) copy-start(s32[96]{0:T(128)} %constant.110) | copy-start | bytes 1156
  81.7 85.8 %copy-start.17 = (s32[96]{0:T(128)S(1)}, s32[96]{0:T(128)}, u32[]{:S(2)}) copy-start(s32[96]{0:T(128)} %constant.111) | copy-start | bytes 1156
  81.7 96.8 %reduce-scatter.2.cloned.1.call-start = ((), (), s32[]{:S(2)}) async-start(), calls=%async_computation.6 | async-start | bytes 1179648 | tf_op jit(solution)/shard_map/reduce_scatter | solution.py:96
  82.4 10.6 %collective-permute-start = (f32[1,16,128]{2,1,0:T(8,128)S(1)}, f32[1,16,128]{2,1,0:T(8,128)S(1)}, u32[]{:S(2)}, u32[]{:S(2)}) collective-permute-start(f32[1,16,128]{2,1,0:T(8,128)S(1)} %get-tuple-element.59), channel_id=1, source_target_pairs={{0,16},{16,32},{32,48},{48,64},{64,80},{80,96},{96,112},{112,128},... | collective-permute-start | bytes 24584 | tf_op jit(solution)/shard_map/ppermute | solution.py:48
  93.1 29.0 %collective-permute-start.1 = (f32[2,16,128]{2,1,0:T(8,128)S(1)}, f32[2,16,128]{2,1,0:T(8,128)S(1)}, u32[]{:S(2)}, u32[]{:S(2)}) collective-permute-start(f32[2,16,128]{2,1,0:T(8,128)S(1)} %pad_maximum_fusion.3), channel_id=1, source_target_pairs={{0,32},{16,48},{32,64},{48,80},{64,96},{80,112},{96,128},{112,144}... | collective-permute-start | bytes 49160 | tf_op jit(solution)/shard_map/ppermute | solution.py:48
  111.8 68.3 %all-to-all-start.4 = ((f32[12,120,128]{2,1,0:T(8,128)}), f32[12,120,128]{2,1,0:T(8,128)S(1)}, u32[]{:S(2)}, u32[]{:S(2)}) async-start(f32[12,120,128]{2,1,0:T(8,128)} %pad_maximum_fusion.1), calls=%async_computation.4 | async-start | bytes 1474560 | tf_op jit(solution)/shard_map/all_to_all | solution.py:23
  122.1 18.1 %collective-permute-start.2 = (f32[4,16,128]{2,1,0:T(8,128)S(1)}, f32[4,16,128]{2,1,0:T(8,128)S(1)}, u32[]{:S(2)}, u32[]{:S(2)}) collective-permute-start(f32[4,16,128]{2,1,0:T(8,128)S(1)} %pad_maximum_fusion.2), channel_id=1, source_target_pairs={{0,64},{16,80},{32,96},{48,112},{64,128},{80,144},{96,160},{112,17... | collective-permute-start | bytes 98312 | tf_op jit(solution)/shard_map/ppermute | solution.py:48
  129.3 17.5 %collective-permute-start.3 = (f32[4,16,128]{2,1,0:T(8,128)S(1)}, f32[4,16,128]{2,1,0:T(8,128)S(1)}, u32[]{:S(2)}, u32[]{:S(2)}) collective-permute-start(f32[4,16,128]{2,1,0:T(8,128)S(1)} %pad_maximum_fusion.2), channel_id=1, source_target_pairs={{0,128},{16,144},{32,160},{48,176},{64,0},{80,16},{96,32},{112,48}... | collective-permute-start | bytes 98312 | tf_op jit(solution)/shard_map/ppermute | solution.py:48
  147.5 7.0 %collective-permute-start.4 = (f32[12,16,128]{2,1,0:T(8,128)S(1)}, f32[12,16,128]{2,1,0:T(8,128)S(1)}, u32[]{:S(2)}, u32[]{:S(2)}) collective-permute-start(f32[12,16,128]{2,1,0:T(8,128)S(1)} %get-tuple-element.42), channel_id=1, source_target_pairs={{0,8},{8,0},{1,9},{9,1},{2,10},{10,2},{3,11},{11,3},{4,12},{12,4},... | collective-permute-start | bytes 294920 | tf_op jit(solution)/shard_map/ppermute | solution.py:48
  155.2 9.4 %collective-permute-start.5 = (f32[24,16,128]{2,1,0:T(8,128)}, f32[24,16,128]{2,1,0:T(8,128)S(1)}, u32[]{:S(2)}, u32[]{:S(2)}) collective-permute-start(f32[24,16,128]{2,1,0:T(8,128)} %get-tuple-element.30), channel_id=1, source_target_pairs={{0,192},{192,384},{384,576},{576,0},{1,193},{193,385},{385,577},{5... | collective-permute-start | bytes 589832 | tf_op jit(solution)/shard_map/ppermute | solution.py:48
  165.3 13.0 %collective-permute-start.6 = (f32[48,16,128]{2,1,0:T(8,128)}, f32[48,16,128]{2,1,0:T(8,128)S(1)}, u32[]{:S(2)}, u32[]{:S(2)}) collective-permute-start(f32[48,16,128]{2,1,0:T(8,128)} %get-tuple-element.26), channel_id=1, source_target_pairs={{0,384},{192,576},{384,0},{576,192},{1,385},{193,577},{385,1},{577... | collective-permute-start | bytes 1179656 | tf_op jit(solution)/shard_map/ppermute | solution.py:48
Sparse Core Ops, SparseCore 0:
  85.7 41.7 reduce-scatter.1

commit v3 on v1

--- a/solution.py
+++ b/solution.py
@@ -1,5 +1,6 @@
 import jax
 import jax.numpy as jnp
+import numpy as np
 from jax import lax
 from jax.sharding import Mesh, PartitionSpec as P
 
@@ -16,6 +17,21 @@
 
 def tap_window(padded, row_off, col_off, side_len):
     return padded[:, row_off : row_off + side_len, col_off : col_off + side_len, :]
+
+
+def doubled(rows, name, have):
+    size = lax.axis_size(name)
+    extra = min(have, size - have)
+    per = rows.shape[0] // have
+    coming = lax.ppermute(
+        rows[: extra * per], name, [(sender, (sender + have) % size) for sender in range(size)]
+    )
+    return jnp.concatenate([rows, coming], axis=0)
+
+
+def flipped_sum(rows, bit):
+    size = lax.axis_size("chan")
+    return rows + lax.ppermute(rows, "chan", [(sender, sender ^ bit) for sender in range(size)])
 
 
 def exchange(blocks, axes):
@@ -37,9 +53,7 @@
     own_rows = jnp.concatenate(
         [latents.reshape(1, -1, LANES), map_pre.reshape(1, -1, LANES)], axis=1
     )
-    gathered = exchange(
-        jnp.broadcast_to(own_rows, (batch_size,) + own_rows.shape[1:]), ("x", "z", "core")
-    )
+    rows_z2 = doubled(own_rows, "z", 1)
     map_rows = exchange(map_weight.reshape(nchan, -1, cols_dev), "chan")
 
     scaled = (features.astype(jnp.float32) * styles[:, None, None, :]).astype(jnp.bfloat16)
@@ -79,53 +93,74 @@
     style_cols = lax.dynamic_slice_in_dim(styles, chan_id * cols_dev, cols_dev, 1)
     grad_input = (grad_inner * style_cols).astype(jnp.bfloat16)
 
-    tile = style_part.reshape(1, -1, LANES)
-    parts = exchange(
-        jnp.broadcast_to(tile, (ncore * nchan,) + tile.shape[1:]), ("core", "chan")
-    )
-    style_grad = jnp.sum(parts.reshape(ncore, nchan, -1, LANES), axis=1)
-    hidden_cols = jnp.sum(
-        lax.dot_general(
-            map_rows,
-            style_grad.reshape(ncore, nchan, cols_dev),
-            (((2,), (2,)), ((0,), (1,))),
-            precision=highest,
-        ),
-        axis=0,
-    ).T
-    style_own = lax.dynamic_slice_in_dim(
-        style_grad.reshape(ncore, nchan, cols_dev), chan_id, 1, 1
-    ).reshape(ncore, cols_dev)
-    source = jnp.where(crossover <= LAYER, partner, dp_id).astype(jnp.float32)
-    source = lax.all_gather(
-        jnp.broadcast_to(source[:, None], (1, cols_dev)), "core", axis=0, tiled=True
-    )
-
     style_factor = jnp.dot(style_sq.T, square_grad, precision=highest)
     product_rows = lax.dot_general(
         patches, grad_scaled, (((0,), (0,)), ((), ())), preferred_element_type=jnp.float32
     ) + 2.0 * weight_flat.astype(jnp.float32) * jnp.tile(style_factor, (KTAPS, 1))
     pieces = product_rows.reshape(nx * nz, ncore, rows_dev, cols_dev).transpose(1, 0, 2, 3)
-    pieces = jnp.sum(exchange(pieces, "core"), axis=0)
-    pieces = pieces.reshape(nx, nz * rows_dev, cols_dev)
-    pad_rows = jnp.zeros((8 - 3 * ncore, cols_dev), jnp.float32)
-    riders = jnp.concatenate([style_own, hidden_cols, source, pad_rows], axis=0)
-    moved = exchange(
-        jnp.concatenate([pieces, jnp.broadcast_to(riders[None], (nx,) + riders.shape)], axis=1), "x"
-    )
-    pieces = jnp.sum(moved[:, : nz * rows_dev], axis=0).reshape(nz, rows_dev, cols_dev)
+    tile = style_part.reshape(channels // LANES, LANES)
+    pieces, tile, map_rows, rows_z2 = lax.optimization_barrier((pieces, tile, map_rows, rows_z2))
+    pieces = jnp.sum(exchange(pieces, "core"), axis=0).reshape(nx, nz * rows_dev, cols_dev)
+    tile = flipped_sum(tile, 1)
+    rows_z4 = doubled(rows_z2, "z", 2)
+    pieces, tile, rows_z4 = lax.optimization_barrier((pieces, tile, rows_z4))
+    pieces = jnp.sum(exchange(pieces, "x"), axis=0).reshape(nz, rows_dev, cols_dev)
+    bit = 2
+    while bit < nchan:
+        tile = flipped_sum(tile, bit)
+        bit *= 2
+    hidden_row = jnp.sum(
+        lax.dot_general(
+            map_rows,
+            tile.reshape(nchan, cols_dev),
+            (((2,), (1,)), ((0,), (0,))),
+            precision=highest,
+        ),
+        axis=0,
+        keepdims=True,
+    )
+    style_row = lax.dynamic_slice_in_dim(tile.reshape(nchan, cols_dev), chan_id, 1, 0)
+    source = jnp.where(crossover <= LAYER, partner, dp_id).astype(jnp.float32)
+    own = (style_row, hidden_row, jnp.broadcast_to(source[:, None], (1, cols_dev)))
+    others = lax.ppermute(
+        jnp.concatenate(own + (jnp.zeros((5, cols_dev), jnp.float32),), axis=0),
+        "core",
+        [(core, (core + 1) % ncore) for core in range(ncore)],
+    )
+    chip = jnp.concatenate(
+        [part for kind in range(3) for part in (own[kind], others[kind : kind + 1])]
+        + [jnp.zeros((2, cols_dev), jnp.float32)],
+        axis=0,
+    )
+    chips = [chip] + [
+        lax.ppermute(chip, "x", [(sender, (sender + hop) % nx) for sender in range(nx)])
+        for hop in range(1, nx)
+    ]
     riders = jnp.concatenate(
-        [
-            moved[:, nz * rows_dev + kind * ncore : nz * rows_dev + (kind + 1) * ncore].reshape(
-                nx * ncore, cols_dev
-            )
-            for kind in range(3)
-        ],
-        axis=0,
-    )
+        [one[kind * ncore : (kind + 1) * ncore] for kind in range(3) for one in chips], axis=0
+    )
+    have = 4
+    rows_z = rows_z4
+    while have < nz:
+        rows_z = doubled(rows_z, "z", have)
+        have = min(2 * have, nz)
+    pieces, riders, rows_z = lax.optimization_barrier((pieces, riders, rows_z))
     moved = exchange(
         jnp.concatenate([pieces, jnp.broadcast_to(riders[None], (nz,) + riders.shape)], axis=1), "z"
     )
+    gathered = doubled(rows_z, "core", 1)
+    have = 1
+    while have < nx:
+        gathered = doubled(gathered, "x", have)
+        have *= 2
+    back_x, back_core, back_z = np.meshgrid(
+        np.arange(nx), np.arange(ncore), np.arange(nz), indexing="ij"
+    )
+    spots = [
+        (lax.axis_index(name) + lax.axis_size(name) - back.reshape(-1)) % lax.axis_size(name)
+        for name, back in (("x", back_x), ("z", back_z), ("core", back_core))
+    ]
+    row_ids = ((spots[0] * nz + spots[1]) * ncore + spots[2]).astype(jnp.float32)
     grad_weight = jnp.sum(moved[:, :rows_dev], axis=0) / batch_size
 
     per = nx * ncore
@@ -134,7 +169,7 @@
         for kind in range(3)
     )
     matches = (
-        source_all[:, :1] == lax.broadcasted_iota(jnp.int32, (1, batch_size), 1).astype(jnp.float32)
+        source_all[:, :1] == row_ids[None, :]
     ).astype(jnp.float32)
     received = lax.dot_general(
         matches,

time: 200 us -> 166 us (0.83)
  waiting for transfers between devices: 94.5 us -> 24.6 us
  starting transfers between devices: 42.2 us -> 78.6 us
  local copies, waits for them, and re-layouts: 6.69 us -> 4.58 us
    all_to_all x5 -> x3, waiting for transfers between devices: 92.5 us -> 0.01 us  [exchange(): return lax.all_to_all(blocks, axes, 0, 0, tiled=True)]
    ppermute x0 -> x14, starting transfers between devices: none -> 60.2 us  [the longest x7 34.6 us: doubled(): lax.ppermute(rows[:extra * per], name, [(sender, (sender + have) % size)...]
    ppermute x0 -> x14, waiting for transfers between devices: none -> 24.5 us  [the longest x7 17.3 us: doubled(): lax.ppermute(rows[:extra * per], name, [(sender, (sender + have) % size)...]
    all_to_all x5 -> x3, starting transfers between devices: 42 us -> 18.3 us  [exchange(): return lax.all_to_all(blocks, axes, 0, 0, tiled=True)]
    all_to_all x1, blocking collectives: 9.98 us -> 14.6 us  [exchange(): return lax.all_to_all(blocks, axes, 0, 0, tiled=True)]
    unnamed x1 -> x0, blocking collectives: 2.98 us -> none
    reduce_sum x3 -> x2, other arithmetic: 3.09 us -> 4.59 us  [the longest x1 4.42 us: local(): jnp.sum(exchange(pieces, 'core'), axis=0)]
  transfers between devices with their start and end apart: 6 -> 18, of which waited for: 6 -> 8; matrix products, arithmetic and copies ran while one was open for 6% -> 14% of each run, Pallas kernels for 0% -> 0%
where the time goes in v3:
time: 166 us; the launch traced here: 163 us
  starting transfers between devices  78.6 us (47%)
  waiting for transfers between devices  24.6 us (15%)
  between operations  16 us (10%)
  blocking collectives  14.6 us (9%)
  other arithmetic  12.3 us (7%)
  matrix products  11.9 us (7%)
  local copies, waits for them, and re-layouts  4.58 us (3%)
    ppermute x7, starting transfers between devices, doubled(): lax.ppermute(rows[:extra * per], name, [(sender, (sender + have) % size)...  34.6 us
    all_to_all x3, starting transfers between devices, exchange(): return lax.all_to_all(blocks, axes, 0, 0, tiled=True)  18.3 us
    ppermute x7, waiting for transfers between devices, doubled(): lax.ppermute(rows[:extra * per], name, [(sender, (sender + have) % size)...  17.3 us
    all_to_all x1, blocking collectives, exchange(): return lax.all_to_all(blocks, axes, 0, 0, tiled=True)  14.6 us
    ppermute x3, starting transfers between devices, flipped_sum(): lax.ppermute(rows, 'chan', [(sender, sender ^ bit) for sender in range(si...  11.2 us
    ppermute x3, starting transfers between devices, local(): lax.ppermute(chip, 'x', [(sender, (sender + hop) % nx) for sender in rang...  9.82 us
    ppermute x1, starting transfers between devices, local(): lax.ppermute(jnp.concatenate(own + (jnp.zeros((5, cols_dev), jnp.float32)...  4.56 us
    reduce_sum x1, other arithmetic, local(): jnp.sum(exchange(pieces, 'core'), axis=0)  4.42 us
  transfers between devices with their start and end apart: 18, of which 8 were waited for; matrix products, arithmetic and copies ran while one was open for 14% of the time, Pallas kernels for 0%

profile of v3, /device:TPU:1, one launch (start us, length us, event | category | flops | bytes accessed | tf_op | source)
XLA Modules:
  0.0 162.5 jit_solution(9604359096955315858)
XLA Ops:
  8.0 4.8 %collective-permute-start = (f32[1,16,128]{2,1,0:T(8,128)S(1)}, f32[1,16,128]{2,1,0:T(8,128)S(1)}, u32[]{:S(2)}, u32[]{:S(2)}) collective-permute-start(f32[1,16,128]{2,1,0:T(8,128)S(1)} %pad_maximum_fusion.6), channel_id=1, source_target_pairs={{0,16},{16,32},{32,48},{48,64},{64,80},{80,96},{96,112},{112,128},... | collective-permute-start | bytes 24584 | tf_op jit(solution)/shard_map/ppermute | solution.py:26
  12.9 6.8 %all-to-all-start = ((f32[8,128,128]{2,1,0:T(8,128)}), f32[8,128,128]{2,1,0:T(8,128)S(1)}, u32[]{:S(2)}, u32[]{:S(2)}) async-start(f32[8,128,128]{2,1,0:T(8,128)} %bitcast.153), calls=%async_computation | async-start | bytes 1048576 | tf_op jit(solution)/shard_map/all_to_all | solution.py:38
  20.5 1.2 multiply_convert_fusion
  23.6 1.4 fusion
  29.7 1.3 fusion.3
  31.0 1.4 convolution_add_fusion
  32.5 2.5 %copy.36 = f32[48,2,96,128]{3,2,0,1:T(8,128)} copy(f32[48,2,96,128]{3,2,1,0:T(8,128)S(1)} %bitcast.136) | data formatting | bytes 9437184 | tf_op jit(solution)/shard_map/reshape | solution.py:100
  35.0 7.5 %collective-permute-start.2 = (f32[2,16,128]{2,1,0:T(8,128)S(1)}, f32[2,16,128]{2,1,0:T(8,128)S(1)}, u32[]{:S(2)}, u32[]{:S(2)}) collective-permute-start(f32[2,16,128]{2,1,0:T(8,128)S(1)} %pad_maximum_fusion.5), channel_id=1, source_target_pairs={{0,32},{16,48},{32,64},{48,80},{64,96},{80,112},{96,128},{112,144}... | collective-permute-start | bytes 49160 | tf_op jit(solution)/shard_map/ppermute | solution.py:26
  42.5 1.9 %collective-permute-start.1 = (f32[8,128]{1,0:T(8,128)S(1)}, f32[8,128]{1,0:T(8,128)S(1)}, u32[]{:S(2)}, u32[]{:S(2)}) collective-permute-start(f32[8,128]{1,0:T(8,128)S(1)} %bitcast_add_fusion), channel_id=1, source_target_pairs={{0,1},{1,0},{2,3},{3,2},{4,5},{5,4},{6,7},{7,6},{8,9},{9,8},{10,11... | collective-permute-start | bytes 12296 | tf_op jit(solution)/shard_map/ppermute | solution.py:34
  44.5 14.6 %all_to_all.20 = f32[2,48,96,128]{3,2,1,0:T(8,128)} all-to-all(f32[2,48,96,128]{3,2,1,0:T(8,128)} %bitcast.137), channel_id=1, replica_groups=mesh['x'=4,'z'=12,'core'=2,'chan'=8] {'core'}, dimensions={0} | all-to-all | bytes 9437184 | tf_op jit(solution)/shard_map/all_to_all | solution.py:38
  59.1 4.4 %reduce_sum.64 = f32[48,96,128]{2,1,0:T(8,128)} reduce(f32[2,48,96,128]{3,2,1,0:T(8,128)} %all_to_all.20, f32[]{:T(128)} %constant.35.clone.1), dimensions={0}, to_apply=%region_3.4 | reduce | flops 589824 | bytes 7077892 | tf_op jit(solution)/shard_map/reduce_sum | solution.py:103
  63.5 4.0 %all-to-all-start.2 = ((f32[4,1152,128]{2,1,0:T(8,128)}), f32[4,1152,128]{2,1,0:T(8,128)S(1)}, u32[]{:S(2)}, u32[]{:S(2)}) async-start(f32[4,1152,128]{2,1,0:T(8,128)} %bitcast.44), calls=%async_computation.2 | async-start | bytes 4718592 | tf_op jit(solution)/shard_map/all_to_all | solution.py:38
  67.6 3.6 %collective-permute-start.3 = (f32[8,128]{1,0:T(8,128)S(1)}, f32[8,128]{1,0:T(8,128)S(1)}, u32[]{:S(2)}, u32[]{:S(2)}) collective-permute-start(f32[8,128]{1,0:T(8,128)S(1)} %add.109), channel_id=1, source_target_pairs={{0,2},{1,3},{2,0},{3,1},{4,6},{5,7},{6,4},{7,5},{8,10},{9,11},{10,... | collective-permute-start | bytes 12296 | tf_op jit(solution)/shard_map/ppermute | solution.py:34
  71.2 1.9 %collective-permute-done.3 = f32[8,128]{1,0:T(8,128)S(1)} collective-permute-done((f32[8,128]{1,0:T(8,128)S(1)}, f32[8,128]{1,0:T(8,128)S(1)}, u32[]{:S(2)}, u32[]{:S(2)}) %collective-permute-start.3) | collective-permute-done | bytes 4128 | tf_op jit(solution)/shard_map/ppermute | solution.py:34
  73.1 5.7 %collective-permute-start.4 = (f32[8,128]{1,0:T(8,128)S(1)}, f32[8,128]{1,0:T(8,128)S(1)}, u32[]{:S(2)}, u32[]{:S(2)}) collective-permute-start(f32[8,128]{1,0:T(8,128)S(1)} %add.110), channel_id=1, source_target_pairs={{0,4},{1,5},{2,6},{3,7},{4,0},{5,1},{6,2},{7,3},{8,12},{9,13},{10,... | collective-permute-start | bytes 12296 | tf_op jit(solution)/shard_map/ppermute | solution.py:34
  80.2 1.1 collective-permute-done.4
  82.0 4.6 %collective-permute-start.5 = (f32[8,128]{1,0:T(8,128)S(1)}, f32[8,128]{1,0:T(8,128)S(1)}, u32[]{:S(2)}, u32[]{:S(2)}) collective-permute-start(f32[8,128]{1,0:T(8,128)S(1)} %maximum_maximum_fusion), channel_id=1, source_target_pairs={{0,8},{8,0},{1,9},{9,1},{2,10},{10,2},{3,11},{11,3},{4,12},{12,4},... | collective-permute-start | bytes 12296 | tf_op jit(solution)/shard_map/ppermute | solution.py:125
  87.4 4.9 %collective-permute-start.8 = (f32[8,128]{1,0:T(8,128)S(1)}, f32[8,128]{1,0:T(8,128)S(1)}, u32[]{:S(2)}, u32[]{:S(2)}) collective-permute-start(f32[8,128]{1,0:T(8,128)S(1)} %concatenate.52), channel_id=1, source_target_pairs={{0,576},{192,0},{384,192},{576,384},{1,577},{193,1},{385,193},{577... | collective-permute-start | bytes 12296 | tf_op jit(solution)/shard_map/ppermute | solution.py:136
  92.2 11.6 %collective-permute-start.10 = (f32[4,16,128]{2,1,0:T(8,128)S(1)}, f32[4,16,128]{2,1,0:T(8,128)S(1)}, u32[]{:S(2)}, u32[]{:S(2)}) collective-permute-start(f32[4,16,128]{2,1,0:T(8,128)S(1)} %pad_maximum_fusion.4), channel_id=1, source_target_pairs={{0,128},{16,144},{32,160},{48,176},{64,0},{80,16},{96,32},{112,48}... | collective-permute-start | bytes 98312 | tf_op jit(solution)/shard_map/ppermute | solution.py:26
  103.8 1.9 %collective-permute-start.9 = (f32[4,16,128]{2,1,0:T(8,128)S(1)}, f32[4,16,128]{2,1,0:T(8,128)S(1)}, u32[]{:S(2)}, u32[]{:S(2)}) collective-permute-start(f32[4,16,128]{2,1,0:T(8,128)S(1)} %pad_maximum_fusion.4), channel_id=1, source_target_pairs={{0,64},{16,80},{32,96},{48,112},{64,128},{80,144},{96,160},{112,17... | collective-permute-start | bytes 98312 | tf_op jit(solution)/shard_map/ppermute | solution.py:26
  105.8 2.5 %collective-permute-start.7 = (f32[8,128]{1,0:T(8,128)S(1)}, f32[8,128]{1,0:T(8,128)S(1)}, u32[]{:S(2)}, u32[]{:S(2)}) collective-permute-start(f32[8,128]{1,0:T(8,128)S(1)} %concatenate.52), channel_id=1, source_target_pairs={{0,384},{192,576},{384,0},{576,192},{1,385},{193,577},{385,1},{577... | collective-permute-start | bytes 12296 | tf_op jit(solution)/shard_map/ppermute | solution.py:136
  108.2 2.5 %collective-permute-start.6 = (f32[8,128]{1,0:T(8,128)S(1)}, f32[8,128]{1,0:T(8,128)S(1)}, u32[]{:S(2)}, u32[]{:S(2)}) collective-permute-start(f32[8,128]{1,0:T(8,128)S(1)} %concatenate.52), channel_id=1, source_target_pairs={{0,192},{192,384},{384,576},{576,0},{1,193},{193,385},{385,577},{5... | collective-permute-start | bytes 12296 | tf_op jit(solution)/shard_map/ppermute | solution.py:136
  111.6 2.6 %collective-permute-done.6 = f32[8,128]{1,0:T(8,128)S(1)} collective-permute-done((f32[8,128]{1,0:T(8,128)S(1)}, f32[8,128]{1,0:T(8,128)S(1)}, u32[]{:S(2)}, u32[]{:S(2)}) %collective-permute-start.6) | collective-permute-done | bytes 4128 | tf_op jit(solution)/shard_map/ppermute | solution.py:136
  115.5 7.5 %all-to-all-start.3 = ((f32[12,120,128]{2,1,0:T(8,128)}), f32[12,120,128]{2,1,0:T(8,128)S(1)}, u32[]{:S(2)}, u32[]{:S(2)}) async-start(f32[12,120,128]{2,1,0:T(8,128)} %pad_maximum_fusion), calls=%async_computation.3 | async-start | bytes 1474560 | tf_op jit(solution)/shard_map/all_to_all | solution.py:38
  122.9 4.8 %collective-permute-start.11 = (f32[12,16,128]{2,1,0:T(8,128)S(1)}, f32[12,16,128]{2,1,0:T(8,128)S(1)}, u32[]{:S(2)}, u32[]{:S(2)}) collective-permute-start(f32[12,16,128]{2,1,0:T(8,128)S(1)} %pad_maximum_fusion.3), channel_id=1, source_target_pairs={{0,8},{8,0},{1,9},{9,1},{2,10},{10,2},{3,11},{11,3},{4,12},{12,4},... | collective-permute-start | bytes 294920 | tf_op jit(solution)/shard_map/ppermute | solution.py:26
  128.7 1.9 %collective-permute-start.12 = (f32[24,16,128]{2,1,0:T(8,128)S(1)}, f32[24,16,128]{2,1,0:T(8,128)S(1)}, u32[]{:S(2)}, u32[]{:S(2)}) collective-permute-start(f32[24,16,128]{2,1,0:T(8,128)S(1)} %pad_maximum_fusion.2), channel_id=1, source_target_pairs={{0,192},{192,384},{384,576},{576,0},{1,193},{193,385},{385,577},{5... | collective-permute-start | bytes 589832 | tf_op jit(solution)/shard_map/ppermute | solution.py:26
  130.7 7.2 %collective-permute-done.12 = f32[24,16,128]{2,1,0:T(8,128)S(1)} collective-permute-done((f32[24,16,128]{2,1,0:T(8,128)S(1)}, f32[24,16,128]{2,1,0:T(8,128)S(1)}, u32[]{:S(2)}, u32[]{:S(2)}) %collective-permute-start.12) | collective-permute-done | bytes 196640 | tf_op jit(solution)/shard_map/ppermute | solution.py:26
  138.0 2.1 %collective-permute-start.13 = (f32[48,16,128]{2,1,0:T(8,128)S(1)}, f32[48,16,128]{2,1,0:T(8,128)S(1)}, u32[]{:S(2)}, u32[]{:S(2)}) collective-permute-start(f32[48,16,128]{2,1,0:T(8,128)S(1)} %pad_maximum_fusion.1), channel_id=1, source_target_pairs={{0,384},{192,576},{384,0},{576,192},{1,385},{193,577},{385,1},{577... | collective-permute-start | bytes 1179656 | tf_op jit(solution)/shard_map/ppermute | solution.py:26
  140.1 1.5 multiply_convert_fusion.1
  141.7 9.1 %collective-permute-done.13 = f32[48,16,128]{2,1,0:T(8,128)S(1)} collective-permute-done((f32[48,16,128]{2,1,0:T(8,128)S(1)}, f32[48,16,128]{2,1,0:T(8,128)S(1)}, u32[]{:S(2)}, u32[]{:S(2)}) %collective-permute-start.13) | collective-permute-done | bytes 393248 | tf_op jit(solution)/shard_map/ppermute | solution.py:26
  151.4 1.8 %convolution_multiply_fusion.1 = f32[1024,128]{1,0:T(8,128)} fusion(f32[96,256]{1,0:T(8,128)S(1)} %fusion.28, f32[12,8,8,128]{3,2,1,0:T(8,128)S(1)} %bitcast.140), kind=kOutput, calls=%fused_computation.21 | convolution fusion | flops 151420928 | bytes 966656 | tf_op jit(solution)/shard_map/dot_general | solution.py:186
  153.9 1.8 %convolution_multiply_fusion = f32[1024,128]{1,0:T(8,128)} fusion(f32[12,8,8,128]{3,2,1,0:T(8,128)S(1)} %bitcast.150, f32[96,256]{1,0:T(8,128)S(1)} %fusion.28, f32[96,1024]{1,0:T(8,128)S(1)} %bitcast.154, s32[]{:T(128)S(6)} %select_n.36), kind=kOutput, calls=%fused_computation.20 | convolution fusion | flops 151162880 | bytes 1015812 | tf_op jit(solution)/shard_map/dot_general | solution.py:191
  (100 shorter events, 13.9 us)
Async XLA Ops:
  7.2 15.1 %copy-start = (bf16[9,1024,128]{2,1,0:T(8,128)(2,1)S(1)}, bf16[9,1024,128]{2,1,0:T(8,128)(2,1)}, u32[]{:S(2)}) copy-start(bf16[9,1024,128]{2,1,0:T(8,128)(2,1)} %param.14) | copy-start | bytes 7077892
  8.0 27.0 %collective-permute-start = (f32[1,16,128]{2,1,0:T(8,128)S(1)}, f32[1,16,128]{2,1,0:T(8,128)S(1)}, u32[]{:S(2)}, u32[]{:S(2)}) collective-permute-start(f32[1,16,128]{2,1,0:T(8,128)S(1)} %pad_maximum_fusion.6), channel_id=1, source_target_pairs={{0,16},{16,32},{32,48},{48,64},{64,80},{80,96},{96,112},{112,128},... | collective-permute-start | bytes 24584 | tf_op jit(solution)/shard_map/ppermute | solution.py:26
  12.9 22.2 %all-to-all-start = ((f32[8,128,128]{2,1,0:T(8,128)}), f32[8,128,128]{2,1,0:T(8,128)S(1)}, u32[]{:S(2)}, u32[]{:S(2)}) async-start(f32[8,128,128]{2,1,0:T(8,128)} %bitcast.153), calls=%async_computation | async-start | bytes 1048576 | tf_op jit(solution)/shard_map/all_to_all | solution.py:38
  22.8 0.8 copy-start.2
  23.1 2.0 %copy-start.3 = (f32[1,1024]{1,0:T(1,128)S(1)}, f32[1,1024]{1,0:T(1,128)}, u32[]{:S(2)}) copy-start(f32[1,1024]{1,0:T(1,128)} %param.13) | copy-start | bytes 12292
  28.4 1.3 copy-start.1
  32.5 2.6 %copy-start.4 = (f32[1,1024]{1,0:T(1,128)S(1)}, f32[1,1024]{1,0:T(1,128)}, u32[]{:S(2)}) copy-start(f32[1,1024]{1,0:T(1,128)} %param.19) | copy-start | bytes 12292
  32.5 2.6 %copy-start.5 = (f32[1,1024]{1,0:T(1,128)S(1)}, f32[1,1024]{1,0:T(1,128)}, u32[]{:S(2)}) copy-start(f32[1,1024]{1,0:T(1,128)} %param.18) | copy-start | bytes 12292
  35.0 28.4 %collective-permute-start.2 = (f32[2,16,128]{2,1,0:T(8,128)S(1)}, f32[2,16,128]{2,1,0:T(8,128)S(1)}, u32[]{:S(2)}, u32[]{:S(2)}) collective-permute-start(f32[2,16,128]{2,1,0:T(8,128)S(1)} %pad_maximum_fusion.5), channel_id=1, source_target_pairs={{0,32},{16,48},{32,64},{48,80},{64,96},{80,112},{96,128},{112,144}... | collective-permute-start | bytes 49160 | tf_op jit(solution)/shard_map/ppermute | solution.py:26
  42.5 20.9 %collective-permute-start.1 = (f32[8,128]{1,0:T(8,128)S(1)}, f32[8,128]{1,0:T(8,128)S(1)}, u32[]{:S(2)}, u32[]{:S(2)}) collective-permute-start(f32[8,128]{1,0:T(8,128)S(1)} %bitcast_add_fusion), channel_id=1, source_target_pairs={{0,1},{1,0},{2,3},{3,2},{4,5},{5,4},{6,7},{7,6},{8,9},{9,8},{10,11... | collective-permute-start | bytes 12296 | tf_op jit(solution)/shard_map/ppermute | solution.py:34
  63.5 50.8 %all-to-all-start.2 = ((f32[4,1152,128]{2,1,0:T(8,128)}), f32[4,1152,128]{2,1,0:T(8,128)S(1)}, u32[]{:S(2)}, u32[]{:S(2)}) async-start(f32[4,1152,128]{2,1,0:T(8,128)} %bitcast.44), calls=%async_computation.2 | async-start | bytes 4718592 | tf_op jit(solution)/shard_map/all_to_all | solution.py:38
  67.5 63.1 %copy-start.6 = (s32[96]{0:T(128)S(1)}, s32[96]{0:T(128)}, u32[]{:S(2)}) copy-start(s32[96]{0:T(128)} %constant.111) | copy-start | bytes 1156
  67.5 63.1 %copy-start.7 = (s32[96]{0:T(128)S(1)}, s32[96]{0:T(128)}, u32[]{:S(2)}) copy-start(s32[96]{0:T(128)} %constant.112) | copy-start | bytes 1156
  67.5 63.1 %copy-start.8 = (s32[96]{0:T(128)S(1)}, s32[96]{0:T(128)}, u32[]{:S(2)}) copy-start(s32[96]{0:T(128)} %constant.113) | copy-start | bytes 1156
  67.5 72.6 %reduce-scatter.2.cloned.1.call-start = ((), (), s32[]{:S(2)}) async-start(), calls=%async_computation.5 | async-start | bytes 1179648 | tf_op jit(solution)/shard_map/reduce_scatter | solution.py:92
  67.6 5.5 %collective-permute-start.3 = (f32[8,128]{1,0:T(8,128)S(1)}, f32[8,128]{1,0:T(8,128)S(1)}, u32[]{:S(2)}, u32[]{:S(2)}) collective-permute-start(f32[8,128]{1,0:T(8,128)S(1)} %add.109), channel_id=1, source_target_pairs={{0,2},{1,3},{2,0},{3,1},{4,6},{5,7},{6,4},{7,5},{8,10},{9,11},{10,... | collective-permute-start | bytes 12296 | tf_op jit(solution)/shard_map/ppermute | solution.py:34
  73.1 8.2 %collective-permute-start.4 = (f32[8,128]{1,0:T(8,128)S(1)}, f32[8,128]{1,0:T(8,128)S(1)}, u32[]{:S(2)}, u32[]{:S(2)}) collective-permute-start(f32[8,128]{1,0:T(8,128)S(1)} %add.110), channel_id=1, source_target_pairs={{0,4},{1,5},{2,6},{3,7},{4,0},{5,1},{6,2},{7,3},{8,12},{9,13},{10,... | collective-permute-start | bytes 12296 | tf_op jit(solution)/shard_map/ppermute | solution.py:34
  82.0 5.4 %collective-permute-start.5 = (f32[8,128]{1,0:T(8,128)S(1)}, f32[8,128]{1,0:T(8,128)S(1)}, u32[]{:S(2)}, u32[]{:S(2)}) collective-permute-start(f32[8,128]{1,0:T(8,128)S(1)} %maximum_maximum_fusion), channel_id=1, source_target_pairs={{0,8},{8,0},{1,9},{9,1},{2,10},{10,2},{3,11},{11,3},{4,12},{12,4},... | collective-permute-start | bytes 12296 | tf_op jit(solution)/shard_map/ppermute | solution.py:125
  87.4 23.4 %collective-permute-start.8 = (f32[8,128]{1,0:T(8,128)S(1)}, f32[8,128]{1,0:T(8,128)S(1)}, u32[]{:S(2)}, u32[]{:S(2)}) collective-permute-start(f32[8,128]{1,0:T(8,128)S(1)} %concatenate.52), channel_id=1, source_target_pairs={{0,576},{192,0},{384,192},{576,384},{1,577},{193,1},{385,193},{577... | collective-permute-start | bytes 12296 | tf_op jit(solution)/shard_map/ppermute | solution.py:136
  92.2 22.0 %collective-permute-start.10 = (f32[4,16,128]{2,1,0:T(8,128)S(1)}, f32[4,16,128]{2,1,0:T(8,128)S(1)}, u32[]{:S(2)}, u32[]{:S(2)}) collective-permute-start(f32[4,16,128]{2,1,0:T(8,128)S(1)} %pad_maximum_fusion.4), channel_id=1, source_target_pairs={{0,128},{16,144},{32,160},{48,176},{64,0},{80,16},{96,32},{112,48}... | collective-permute-start | bytes 98312 | tf_op jit(solution)/shard_map/ppermute | solution.py:26
  103.8 10.5 %collective-permute-start.9 = (f32[4,16,128]{2,1,0:T(8,128)S(1)}, f32[4,16,128]{2,1,0:T(8,128)S(1)}, u32[]{:S(2)}, u32[]{:S(2)}) collective-permute-start(f32[4,16,128]{2,1,0:T(8,128)S(1)} %pad_maximum_fusion.4), channel_id=1, source_target_pairs={{0,64},{16,80},{32,96},{48,112},{64,128},{80,144},{96,160},{112,17... | collective-permute-start | bytes 98312 | tf_op jit(solution)/shard_map/ppermute | solution.py:26
  105.8 5.9 %collective-permute-start.7 = (f32[8,128]{1,0:T(8,128)S(1)}, f32[8,128]{1,0:T(8,128)S(1)}, u32[]{:S(2)}, u32[]{:S(2)}) collective-permute-start(f32[8,128]{1,0:T(8,128)S(1)} %concatenate.52), channel_id=1, source_target_pairs={{0,384},{192,576},{384,0},{576,192},{1,385},{193,577},{385,1},{577... | collective-permute-start | bytes 12296 | tf_op jit(solution)/shard_map/ppermute | solution.py:136
  108.2 6.0 %collective-permute-start.6 = (f32[8,128]{1,0:T(8,128)S(1)}, f32[8,128]{1,0:T(8,128)S(1)}, u32[]{:S(2)}, u32[]{:S(2)}) collective-permute-start(f32[8,128]{1,0:T(8,128)S(1)} %concatenate.52), channel_id=1, source_target_pairs={{0,192},{192,384},{384,576},{576,0},{1,193},{193,385},{385,577},{5... | collective-permute-start | bytes 12296 | tf_op jit(solution)/shard_map/ppermute | solution.py:136
  115.5 35.5 %all-to-all-start.3 = ((f32[12,120,128]{2,1,0:T(8,128)}), f32[12,120,128]{2,1,0:T(8,128)S(1)}, u32[]{:S(2)}, u32[]{:S(2)}) async-start(f32[12,120,128]{2,1,0:T(8,128)} %pad_maximum_fusion), calls=%async_computation.3 | async-start | bytes 1474560 | tf_op jit(solution)/shard_map/all_to_all | solution.py:38
  122.9 5.7 %collective-permute-start.11 = (f32[12,16,128]{2,1,0:T(8,128)S(1)}, f32[12,16,128]{2,1,0:T(8,128)S(1)}, u32[]{:S(2)}, u32[]{:S(2)}) collective-permute-start(f32[12,16,128]{2,1,0:T(8,128)S(1)} %pad_maximum_fusion.3), channel_id=1, source_target_pairs={{0,8},{8,0},{1,9},{9,1},{2,10},{10,2},{3,11},{11,3},{4,12},{12,4},... | collective-permute-start | bytes 294920 | tf_op jit(solution)/shard_map/ppermute | solution.py:26
  128.7 9.2 %collective-permute-start.12 = (f32[24,16,128]{2,1,0:T(8,128)S(1)}, f32[24,16,128]{2,1,0:T(8,128)S(1)}, u32[]{:S(2)}, u32[]{:S(2)}) collective-permute-start(f32[24,16,128]{2,1,0:T(8,128)S(1)} %pad_maximum_fusion.2), channel_id=1, source_target_pairs={{0,192},{192,384},{384,576},{576,0},{1,193},{193,385},{385,577},{5... | collective-permute-start | bytes 589832 | tf_op jit(solution)/shard_map/ppermute | solution.py:26
  138.0 12.8 %collective-permute-start.13 = (f32[48,16,128]{2,1,0:T(8,128)S(1)}, f32[48,16,128]{2,1,0:T(8,128)S(1)}, u32[]{:S(2)}, u32[]{:S(2)}) collective-permute-start(f32[48,16,128]{2,1,0:T(8,128)S(1)} %pad_maximum_fusion.1), channel_id=1, source_target_pairs={{0,384},{192,576},{384,0},{576,192},{1,385},{193,577},{385,1},{577... | collective-permute-start | bytes 1179656 | tf_op jit(solution)/shard_map/ppermute | solution.py:26
Sparse Core Ops, SparseCore 0:
  86.7 41.1 reduce-scatter.1

commit v4 on v3

--- a/solution.py
+++ b/solution.py
@@ -27,11 +27,6 @@
         rows[: extra * per], name, [(sender, (sender + have) % size) for sender in range(size)]
     )
     return jnp.concatenate([rows, coming], axis=0)
-
-
-def flipped_sum(rows, bit):
-    size = lax.axis_size("chan")
-    return rows + lax.ppermute(rows, "chan", [(sender, sender ^ bit) for sender in range(size)])
 
 
 def exchange(blocks, axes):
@@ -97,53 +92,71 @@
     product_rows = lax.dot_general(
         patches, grad_scaled, (((0,), (0,)), ((), ())), preferred_element_type=jnp.float32
     ) + 2.0 * weight_flat.astype(jnp.float32) * jnp.tile(style_factor, (KTAPS, 1))
-    pieces = product_rows.reshape(nx * nz, ncore, rows_dev, cols_dev).transpose(1, 0, 2, 3)
-    tile = style_part.reshape(channels // LANES, LANES)
-    pieces, tile, map_rows, rows_z2 = lax.optimization_barrier((pieces, tile, map_rows, rows_z2))
-    pieces = jnp.sum(exchange(pieces, "core"), axis=0).reshape(nx, nz * rows_dev, cols_dev)
-    tile = flipped_sum(tile, 1)
+    source = jnp.where(crossover <= LAYER, partner, dp_id).astype(jnp.float32)
+    tile = jnp.concatenate(
+        [
+            style_part.reshape(-1, LANES),
+            jnp.broadcast_to(source[:, None], (8, LANES)),
+        ],
+        axis=0,
+    )
+    tile, product_rows, map_rows, rows_z2 = lax.optimization_barrier(
+        (tile, product_rows, map_rows, rows_z2)
+    )
+    parts = exchange(
+        jnp.broadcast_to(tile[None], (ncore * nchan,) + tile.shape), ("core", "chan")
+    ).reshape(ncore, nchan, -1, LANES)
+    pieces = product_rows.reshape(nx, nz, ncore, rows_dev, cols_dev)
+    core_id = lax.axis_index("core")
+    coming = lax.ppermute(
+        lax.dynamic_index_in_dim(pieces, ncore - 1 - core_id, 2, keepdims=False),
+        "core",
+        [(core, ncore - 1 - core) for core in range(ncore)],
+    )
     rows_z4 = doubled(rows_z2, "z", 2)
-    pieces, tile, rows_z4 = lax.optimization_barrier((pieces, tile, rows_z4))
-    pieces = jnp.sum(exchange(pieces, "x"), axis=0).reshape(nz, rows_dev, cols_dev)
-    bit = 2
-    while bit < nchan:
-        tile = flipped_sum(tile, bit)
-        bit *= 2
-    hidden_row = jnp.sum(
+    style_grad = jnp.sum(parts[:, :, :-8], axis=1)
+    hidden_rows = jnp.sum(
         lax.dot_general(
             map_rows,
-            tile.reshape(nchan, cols_dev),
-            (((2,), (1,)), ((0,), (0,))),
+            style_grad.reshape(ncore, nchan, cols_dev),
+            (((2,), (2,)), ((0,), (1,))),
             precision=highest,
         ),
         axis=0,
-        keepdims=True,
-    )
-    style_row = lax.dynamic_slice_in_dim(tile.reshape(nchan, cols_dev), chan_id, 1, 0)
-    source = jnp.where(crossover <= LAYER, partner, dp_id).astype(jnp.float32)
-    own = (style_row, hidden_row, jnp.broadcast_to(source[:, None], (1, cols_dev)))
-    others = lax.ppermute(
-        jnp.concatenate(own + (jnp.zeros((5, cols_dev), jnp.float32),), axis=0),
-        "core",
-        [(core, (core + 1) % ncore) for core in range(ncore)],
-    )
-    chip = jnp.concatenate(
-        [part for kind in range(3) for part in (own[kind], others[kind : kind + 1])]
-        + [jnp.zeros((2, cols_dev), jnp.float32)],
-        axis=0,
-    )
-    chips = [chip] + [
-        lax.ppermute(chip, "x", [(sender, (sender + hop) % nx) for sender in range(nx)])
-        for hop in range(1, nx)
-    ]
+    ).T
+    style_rows = lax.dynamic_slice_in_dim(
+        style_grad.reshape(ncore, nchan, cols_dev), chan_id, 1, 1
+    ).reshape(ncore, cols_dev)
     riders = jnp.concatenate(
-        [one[kind * ncore : (kind + 1) * ncore] for kind in range(3) for one in chips], axis=0
+        [style_rows, hidden_rows, parts[:, 0, -1], jnp.zeros((8 - 3 * ncore, cols_dev))], axis=0
+    )
+    coming, riders, rows_z4 = lax.optimization_barrier((coming, riders, rows_z4))
+    pieces = lax.dynamic_index_in_dim(pieces, core_id, 2, keepdims=False) + coming
+    moved = exchange(
+        jnp.concatenate(
+            [
+                pieces.reshape(nx, nz * rows_dev, cols_dev),
+                jnp.broadcast_to(riders[None], (nx,) + riders.shape),
+            ],
+            axis=1,
+        ),
+        "x",
     )
     have = 4
     rows_z = rows_z4
     while have < nz:
         rows_z = doubled(rows_z, "z", have)
         have = min(2 * have, nz)
+    pieces = jnp.sum(moved[:, : nz * rows_dev], axis=0).reshape(nz, rows_dev, cols_dev)
+    riders = jnp.concatenate(
+        [
+            moved[:, nz * rows_dev + kind * ncore : nz * rows_dev + (kind + 1) * ncore].reshape(
+                nx * ncore, cols_dev
+            )
+            for kind in range(3)
+        ],
+        axis=0,
+    )
     pieces, riders, rows_z = lax.optimization_barrier((pieces, riders, rows_z))
     moved = exchange(
         jnp.concatenate([pieces, jnp.broadcast_to(riders[None], (nz,) + riders.shape)], axis=1), "z"

time: 166 us -> 151 us (0.910)
  the two profiles are of different devices: /device:TPU:1 before, /device:TPU:72 now
where the time goes in v4:
time: 151 us
  starting transfers between devices  58.2 us (39%)
  waiting for transfers between devices  45.2 us (30%)
  between operations  15.9 us (11%)
  matrix products  14.1 us (9%)
  other arithmetic  11.4 us (8%)
  local copies, waits for them, and re-layouts  5.87 us (4%)
    ppermute x7, waiting for transfers between devices, doubled(): lax.ppermute(rows[:extra * per], name, [(sender, (sender + have) % size)...  30.7 us
    all_to_all x4, starting transfers between devices, exchange(): return lax.all_to_all(blocks, axes, 0, 0, tiled=True)  28.3 us
    ppermute x7, starting transfers between devices, doubled(): lax.ppermute(rows[:extra * per], name, [(sender, (sender + have) % size)...  27.9 us
    all_to_all x4, waiting for transfers between devices, exchange(): return lax.all_to_all(blocks, axes, 0, 0, tiled=True)  13.8 us
    dot_general x9, matrix products, local(): lax.dot_general(tap_window(grad_padded, 2 - tap // 3, 2 - tap % 3, side_l...  3.71 us
    dot_general x1, matrix products, local(): lax.dot_general(patches, grad_scaled, (((0,), (0,)), ((), ())), preferred...  3.59 us
    squeeze x1, local copies, waits for them, and re-layouts, local(): lax.dynamic_index_in_dim(pieces, ncore - 1 - core_id, 2, keepdims=False)  3.26 us
  transfers between devices with their start and end apart: 13, of which 7 were waited for; matrix products, arithmetic and copies ran while one was open for 12% of the time, Pallas kernels for 0%

profile of v4, /device:TPU:72, one launch (start us, length us, event | category | flops | bytes accessed | tf_op | source)
XLA Modules:
  0.0 150.6 jit_solution(15784809709272127021)
XLA Ops:
  7.2 0.9 pad_maximum_fusion.8
  8.0 4.3 %collective-permute-start = (f32[1,16,128]{2,1,0:T(8,128)S(1)}, f32[1,16,128]{2,1,0:T(8,128)S(1)}, u32[]{:S(2)}, u32[]{:S(2)}) collective-permute-start(f32[1,16,128]{2,1,0:T(8,128)S(1)} %pad_maximum_fusion.8), channel_id=1, source_target_pairs={{0,16},{16,32},{32,48},{48,64},{64,80},{80,96},{96,112},{112,128},... | collective-permute-start | bytes 24584 | tf_op jit(solution)/shard_map/ppermute | solution.py:26
  12.3 7.6 %all-to-all-start = ((f32[8,128,128]{2,1,0:T(8,128)}), f32[8,128,128]{2,1,0:T(8,128)S(1)}, u32[]{:S(2)}, u32[]{:S(2)}) async-start(f32[8,128,128]{2,1,0:T(8,128)} %bitcast.157), calls=%async_computation | async-start | bytes 1048576 | tf_op jit(solution)/shard_map/all_to_all | solution.py:33
  20.6 1.2 multiply_convert_fusion
  23.8 1.4 fusion
  26.8 0.8 bitcast_multiply_fusion
  29.9 1.3 fusion.3
  31.2 3.6 %convolution_add_fusion = f32[9216,128]{1,0:T(8,128)} fusion(f32[9216,128]{1,0:T(8,128)S(1)} %bitcast_multiply_fusion, bf16[256,9216]{1,0:T(8,128)(2,1)S(1)} %constant_dynamic-update-slice_fusion, bf16[256,128]{1,0:T(8,128)(2,1)S(1)} %fusion.27), kind=kOutput, calls=%fused_computation | convolution fusion | flops 605159424 | bytes 14221312 | tf_op jit(solution)/shard_map/dot_general | solution.py:92
  36.1 3.3 %dynamic-slice_bitcast_fusion = f32[4,12,96,128]{3,2,1,0:T(8,128)} fusion(f32[4,12,2,96,128]{4,3,2,1,0:T(8,128)} %bitcast.139, s32[]{:T(128)S(6)} %select_n.43), kind=kLoop, calls=%fused_computation.6 | loop fusion | bytes 4718596 | tf_op jit(solution)/shard_map/jit(dynamic_index_in_dim)/squeeze | solution.py:112
  39.4 1.9 %collective-permute-start.1 = (f32[4,12,96,128]{3,2,1,0:T(8,128)}, f32[4,12,96,128]{3,2,1,0:T(8,128)S(1)}, u32[]{:S(2)}, u32[]{:S(2)}) collective-permute-start(f32[4,12,96,128]{3,2,1,0:T(8,128)} %dynamic-slice_bitcast_fusion), channel_id=1, source_target_pairs={{0,8},{8,0},{1,9},{9,1},{2,10},{10,2},{3,11},{11,3},{4,12},{12,4},... | collective-permute-start | bytes 7077896 | tf_op jit(solution)/shard_map/ppermute | solution.py:111
  42.0 7.3 %all-to-all-start.1 = ((f32[16,16,128]{2,1,0:T(8,128)}), f32[16,16,128]{2,1,0:T(8,128)S(1)}, u32[]{:S(2)}, u32[]{:S(2)}) async-start(f32[16,16,128]{2,1,0:T(8,128)} %broadcast_in_dim.22), calls=%async_computation.1 | async-start | bytes 262144 | tf_op jit(solution)/shard_map/all_to_all | solution.py:33
  49.3 7.3 %collective-permute-start.2 = (f32[2,16,128]{2,1,0:T(8,128)S(1)}, f32[2,16,128]{2,1,0:T(8,128)S(1)}, u32[]{:S(2)}, u32[]{:S(2)}) collective-permute-start(f32[2,16,128]{2,1,0:T(8,128)S(1)} %pad_maximum_fusion.6), channel_id=1, source_target_pairs={{0,32},{16,48},{32,64},{48,80},{64,96},{80,112},{96,128},{112,144}... | collective-permute-start | bytes 49160 | tf_op jit(solution)/shard_map/ppermute | solution.py:26
  56.7 5.6 %collective-permute-done.2 = f32[2,16,128]{2,1,0:T(8,128)S(1)} collective-permute-done((f32[2,16,128]{2,1,0:T(8,128)S(1)}, f32[2,16,128]{2,1,0:T(8,128)S(1)}, u32[]{:S(2)}, u32[]{:S(2)}) %collective-permute-start.2) | collective-permute-done | bytes 16416 | tf_op jit(solution)/shard_map/ppermute | solution.py:26
  63.0 2.1 %bitcast_add_fusion = f32[4,12,96,128]{3,2,1,0:T(8,128)S(1)} fusion(f32[4,12,96,128]{3,2,1,0:T(8,128)S(1)} %collective-permute-done.1, f32[4,12,2,96,128]{4,3,2,1,0:T(8,128)} %bitcast.140, s32[]{:T(128)S(6)} %select_n.42), kind=kLoop, calls=%fused_computation.5 | loop fusion | flops 589824 | bytes 7077892 | tf_op jit(solution)/shard_map/add | solution.py:134
  65.0 1.6 %pad_maximum_fusion = f32[4,1160,128]{2,1,0:T(8,128)} fusion(f32[4,8,128]{2,1,0:T(8,128)S(1)} %broadcast_in_dim.46, f32[4,1152,128]{2,1,0:T(8,128)S(1)} %bitcast.141), kind=kLoop, calls=%fused_computation.3 | loop fusion | flops 593920 | bytes 4751360 | tf_op jit(solution)/shard_map/concatenate | solution.py:136
  66.6 4.3 %all-to-all-start.2 = ((f32[4,1160,128]{2,1,0:T(8,128)}), f32[4,1160,128]{2,1,0:T(8,128)S(1)}, u32[]{:S(2)}, u32[]{:S(2)}) async-start(f32[4,1160,128]{2,1,0:T(8,128)} %pad_maximum_fusion), calls=%async_computation.2 | async-start | bytes 4751360 | tf_op jit(solution)/shard_map/all_to_all | solution.py:33
  71.6 6.1 %collective-permute-start.3 = (f32[4,16,128]{2,1,0:T(8,128)S(1)}, f32[4,16,128]{2,1,0:T(8,128)S(1)}, u32[]{:S(2)}, u32[]{:S(2)}) collective-permute-start(f32[4,16,128]{2,1,0:T(8,128)S(1)} %pad_maximum_fusion.5), channel_id=1, source_target_pairs={{0,64},{16,80},{32,96},{48,112},{64,128},{80,144},{96,160},{112,17... | collective-permute-start | bytes 98312 | tf_op jit(solution)/shard_map/ppermute | solution.py:26
  77.8 3.8 %collective-permute-start.4 = (f32[4,16,128]{2,1,0:T(8,128)S(1)}, f32[4,16,128]{2,1,0:T(8,128)S(1)}, u32[]{:S(2)}, u32[]{:S(2)}) collective-permute-start(f32[4,16,128]{2,1,0:T(8,128)S(1)} %pad_maximum_fusion.5), channel_id=1, source_target_pairs={{0,128},{16,144},{32,160},{48,176},{64,0},{80,16},{96,32},{112,48}... | collective-permute-start | bytes 98312 | tf_op jit(solution)/shard_map/ppermute | solution.py:26
  81.5 6.3 %collective-permute-done.4 = f32[4,16,128]{2,1,0:T(8,128)S(1)} collective-permute-done((f32[4,16,128]{2,1,0:T(8,128)S(1)}, f32[4,16,128]{2,1,0:T(8,128)S(1)}, u32[]{:S(2)}, u32[]{:S(2)}) %collective-permute-start.4) | collective-permute-done | bytes 32800 | tf_op jit(solution)/shard_map/ppermute | solution.py:26
  87.8 11.8 %all-to-all-done.2 = f32[4,1160,128]{2,1,0:T(8,128)S(1)} async-done(((f32[4,1160,128]{2,1,0:T(8,128)}), f32[4,1160,128]{2,1,0:T(8,128)S(1)}, u32[]{:S(2)}, u32[]{:S(2)}) %all-to-all-start.2) | async-done | bytes 2375712 | tf_op jit(solution)/shard_map/all_to_all | solution.py:33
  99.8 0.9 pad_maximum_fusion.1
  100.7 9.1 %all-to-all-start.3 = ((f32[12,120,128]{2,1,0:T(8,128)}), f32[12,120,128]{2,1,0:T(8,128)S(1)}, u32[]{:S(2)}, u32[]{:S(2)}) async-start(f32[12,120,128]{2,1,0:T(8,128)} %pad_maximum_fusion.1), calls=%async_computation.3 | async-start | bytes 1474560 | tf_op jit(solution)/shard_map/all_to_all | solution.py:33
  109.9 1.9 %collective-permute-start.5 = (f32[12,16,128]{2,1,0:T(8,128)S(1)}, f32[12,16,128]{2,1,0:T(8,128)S(1)}, u32[]{:S(2)}, u32[]{:S(2)}) collective-permute-start(f32[12,16,128]{2,1,0:T(8,128)S(1)} %pad_maximum_fusion.4), channel_id=1, source_target_pairs={{0,8},{8,0},{1,9},{9,1},{2,10},{10,2},{3,11},{11,3},{4,12},{12,4},... | collective-permute-start | bytes 294920 | tf_op jit(solution)/shard_map/ppermute | solution.py:26
  111.8 1.2 collective-permute-done.5
  113.1 2.5 %collective-permute-start.6 = (f32[24,16,128]{2,1,0:T(8,128)S(1)}, f32[24,16,128]{2,1,0:T(8,128)S(1)}, u32[]{:S(2)}, u32[]{:S(2)}) collective-permute-start(f32[24,16,128]{2,1,0:T(8,128)S(1)} %pad_maximum_fusion.3), channel_id=1, source_target_pairs={{0,192},{192,384},{384,576},{576,0},{1,193},{193,385},{385,577},{5... | collective-permute-start | bytes 589832 | tf_op jit(solution)/shard_map/ppermute | solution.py:26
  115.6 7.5 %collective-permute-done.6 = f32[24,16,128]{2,1,0:T(8,128)S(1)} collective-permute-done((f32[24,16,128]{2,1,0:T(8,128)S(1)}, f32[24,16,128]{2,1,0:T(8,128)S(1)}, u32[]{:S(2)}, u32[]{:S(2)}) %collective-permute-start.6) | collective-permute-done | bytes 196640 | tf_op jit(solution)/shard_map/ppermute | solution.py:26
  123.2 2.1 %collective-permute-start.7 = (f32[48,16,128]{2,1,0:T(8,128)S(1)}, f32[48,16,128]{2,1,0:T(8,128)S(1)}, u32[]{:S(2)}, u32[]{:S(2)}) collective-permute-start(f32[48,16,128]{2,1,0:T(8,128)S(1)} %pad_maximum_fusion.2), channel_id=1, source_target_pairs={{0,384},{192,576},{384,0},{576,192},{1,385},{193,577},{385,1},{577... | collective-permute-start | bytes 1179656 | tf_op jit(solution)/shard_map/ppermute | solution.py:26
  125.3 1.5 %multiply_convert_fusion.1 = bf16[256,128]{1,0:T(8,128)(2,1)} fusion(f32[256,128]{1,0:T(8,128)} %reduce-scatter.2.cloned.1.call-done, f32[128]{0:T(128)S(1)} %fusion.52), kind=kLoop, calls=%fused_computation.75 | loop fusion | flops 65536 | bytes 197120 | tf_op jit(solution)/shard_map/convert_element_type | solution.py:89
  126.9 10.0 %collective-permute-done.7 = f32[48,16,128]{2,1,0:T(8,128)S(1)} collective-permute-done((f32[48,16,128]{2,1,0:T(8,128)S(1)}, f32[48,16,128]{2,1,0:T(8,128)S(1)}, u32[]{:S(2)}, u32[]{:S(2)}) %collective-permute-start.7) | collective-permute-done | bytes 393248 | tf_op jit(solution)/shard_map/ppermute | solution.py:26
  137.1 2.0 %all-to-all-done.3 = f32[12,120,128]{2,1,0:T(8,128)S(1)} async-done(((f32[12,120,128]{2,1,0:T(8,128)}), f32[12,120,128]{2,1,0:T(8,128)S(1)}, u32[]{:S(2)}, u32[]{:S(2)}) %all-to-all-start.3) | async-done | bytes 737312 | tf_op jit(solution)/shard_map/all_to_all | solution.py:33
  139.5 1.8 %convolution_multiply_fusion.1 = f32[1024,128]{1,0:T(8,128)} fusion(f32[96,256]{1,0:T(8,128)S(1)} %fusion.28, f32[12,8,8,128]{3,2,1,0:T(8,128)S(1)} %bitcast.144), kind=kOutput, calls=%fused_computation.24 | convolution fusion | flops 151420928 | bytes 966656 | tf_op jit(solution)/shard_map/dot_general | solution.py:199
  142.0 1.8 %convolution_multiply_fusion = f32[1024,128]{1,0:T(8,128)} fusion(f32[12,8,8,128]{3,2,1,0:T(8,128)S(1)} %bitcast.154, f32[96,256]{1,0:T(8,128)S(1)} %fusion.28, f32[96,1024]{1,0:T(8,128)S(1)} %bitcast.158, s32[]{:T(128)S(6)} %select_n.45), kind=kOutput, calls=%fused_computation.23 | convolution fusion | flops 151162880 | bytes 1015812 | tf_op jit(solution)/shard_map/dot_general | solution.py:204
  (85 shorter events, 10.0 us)
Async XLA Ops:
  7.2 15.3 %copy-start = (bf16[9,1024,128]{2,1,0:T(8,128)(2,1)S(1)}, bf16[9,1024,128]{2,1,0:T(8,128)(2,1)}, u32[]{:S(2)}) copy-start(bf16[9,1024,128]{2,1,0:T(8,128)(2,1)} %param.14) | copy-start | bytes 7077892
  8.0 28.0 %collective-permute-start = (f32[1,16,128]{2,1,0:T(8,128)S(1)}, f32[1,16,128]{2,1,0:T(8,128)S(1)}, u32[]{:S(2)}, u32[]{:S(2)}) collective-permute-start(f32[1,16,128]{2,1,0:T(8,128)S(1)} %pad_maximum_fusion.8), channel_id=1, source_target_pairs={{0,16},{16,32},{32,48},{48,64},{64,80},{80,96},{96,112},{112,128},... | collective-permute-start | bytes 24584 | tf_op jit(solution)/shard_map/ppermute | solution.py:26
  12.3 23.8 %all-to-all-start = ((f32[8,128,128]{2,1,0:T(8,128)}), f32[8,128,128]{2,1,0:T(8,128)S(1)}, u32[]{:S(2)}, u32[]{:S(2)}) async-start(f32[8,128,128]{2,1,0:T(8,128)} %bitcast.157), calls=%async_computation | async-start | bytes 1048576 | tf_op jit(solution)/shard_map/all_to_all | solution.py:33
  23.0 0.8 copy-start.2
  23.3 2.0 %copy-start.3 = (f32[1,1024]{1,0:T(1,128)S(1)}, f32[1,1024]{1,0:T(1,128)}, u32[]{:S(2)}) copy-start(f32[1,1024]{1,0:T(1,128)} %param.13) | copy-start | bytes 12292
  28.6 1.3 copy-start.1
  31.1 4.9 %copy-start.4 = (f32[1,1024]{1,0:T(1,128)S(1)}, f32[1,1024]{1,0:T(1,128)}, u32[]{:S(2)}) copy-start(f32[1,1024]{1,0:T(1,128)} %param.19) | copy-start | bytes 12292
  31.2 4.9 %copy-start.5 = (f32[1,1024]{1,0:T(1,128)S(1)}, f32[1,1024]{1,0:T(1,128)}, u32[]{:S(2)}) copy-start(f32[1,1024]{1,0:T(1,128)} %param.18) | copy-start | bytes 12292
  39.4 23.6 %collective-permute-start.1 = (f32[4,12,96,128]{3,2,1,0:T(8,128)}, f32[4,12,96,128]{3,2,1,0:T(8,128)S(1)}, u32[]{:S(2)}, u32[]{:S(2)}) collective-permute-start(f32[4,12,96,128]{3,2,1,0:T(8,128)} %dynamic-slice_bitcast_fusion), channel_id=1, source_target_pairs={{0,8},{8,0},{1,9},{9,1},{2,10},{10,2},{3,11},{11,3},{4,12},{12,4},... | collective-permute-start | bytes 7077896 | tf_op jit(solution)/shard_map/ppermute | solution.py:111
  42.0 20.3 %all-to-all-start.1 = ((f32[16,16,128]{2,1,0:T(8,128)}), f32[16,16,128]{2,1,0:T(8,128)S(1)}, u32[]{:S(2)}, u32[]{:S(2)}) async-start(f32[16,16,128]{2,1,0:T(8,128)} %broadcast_in_dim.22), calls=%async_computation.1 | async-start | bytes 262144 | tf_op jit(solution)/shard_map/all_to_all | solution.py:33
  49.3 13.0 %collective-permute-start.2 = (f32[2,16,128]{2,1,0:T(8,128)S(1)}, f32[2,16,128]{2,1,0:T(8,128)S(1)}, u32[]{:S(2)}, u32[]{:S(2)}) collective-permute-start(f32[2,16,128]{2,1,0:T(8,128)S(1)} %pad_maximum_fusion.6), channel_id=1, source_target_pairs={{0,32},{16,48},{32,64},{48,80},{64,96},{80,112},{96,128},{112,144}... | collective-permute-start | bytes 49160 | tf_op jit(solution)/shard_map/ppermute | solution.py:26
  66.6 33.0 %all-to-all-start.2 = ((f32[4,1160,128]{2,1,0:T(8,128)}), f32[4,1160,128]{2,1,0:T(8,128)S(1)}, u32[]{:S(2)}, u32[]{:S(2)}) async-start(f32[4,1160,128]{2,1,0:T(8,128)} %pad_maximum_fusion), calls=%async_computation.2 | async-start | bytes 4751360 | tf_op jit(solution)/shard_map/all_to_all | solution.py:33
  70.9 44.6 %copy-start.6 = (s32[96]{0:T(128)S(1)}, s32[96]{0:T(128)}, u32[]{:S(2)}) copy-start(s32[96]{0:T(128)} %constant.118) | copy-start | bytes 1156
  70.9 44.7 %copy-start.7 = (s32[96]{0:T(128)S(1)}, s32[96]{0:T(128)}, u32[]{:S(2)}) copy-start(s32[96]{0:T(128)} %constant.119) | copy-start | bytes 1156
  70.9 44.7 %copy-start.8 = (s32[96]{0:T(128)S(1)}, s32[96]{0:T(128)}, u32[]{:S(2)}) copy-start(s32[96]{0:T(128)} %constant.120) | copy-start | bytes 1156
  70.9 54.4 %reduce-scatter.2.cloned.1.call-start = ((), (), s32[]{:S(2)}) async-start(), calls=%async_computation.5 | async-start | bytes 1179648 | tf_op jit(solution)/shard_map/reduce_scatter | solution.py:87
  71.6 9.9 %collective-permute-start.3 = (f32[4,16,128]{2,1,0:T(8,128)S(1)}, f32[4,16,128]{2,1,0:T(8,128)S(1)}, u32[]{:S(2)}, u32[]{:S(2)}) collective-permute-start(f32[4,16,128]{2,1,0:T(8,128)S(1)} %pad_maximum_fusion.5), channel_id=1, source_target_pairs={{0,64},{16,80},{32,96},{48,112},{64,128},{80,144},{96,160},{112,17... | collective-permute-start | bytes 98312 | tf_op jit(solution)/shard_map/ppermute | solution.py:26
  77.8 10.1 %collective-permute-start.4 = (f32[4,16,128]{2,1,0:T(8,128)S(1)}, f32[4,16,128]{2,1,0:T(8,128)S(1)}, u32[]{:S(2)}, u32[]{:S(2)}) collective-permute-start(f32[4,16,128]{2,1,0:T(8,128)S(1)} %pad_maximum_fusion.5), channel_id=1, source_target_pairs={{0,128},{16,144},{32,160},{48,176},{64,0},{80,16},{96,32},{112,48}... | collective-permute-start | bytes 98312 | tf_op jit(solution)/shard_map/ppermute | solution.py:26
  100.7 38.4 %all-to-all-start.3 = ((f32[12,120,128]{2,1,0:T(8,128)}), f32[12,120,128]{2,1,0:T(8,128)S(1)}, u32[]{:S(2)}, u32[]{:S(2)}) async-start(f32[12,120,128]{2,1,0:T(8,128)} %pad_maximum_fusion.1), calls=%async_computation.3 | async-start | bytes 1474560 | tf_op jit(solution)/shard_map/all_to_all | solution.py:33
  109.9 3.2 %collective-permute-start.5 = (f32[12,16,128]{2,1,0:T(8,128)S(1)}, f32[12,16,128]{2,1,0:T(8,128)S(1)}, u32[]{:S(2)}, u32[]{:S(2)}) collective-permute-start(f32[12,16,128]{2,1,0:T(8,128)S(1)} %pad_maximum_fusion.4), channel_id=1, source_target_pairs={{0,8},{8,0},{1,9},{9,1},{2,10},{10,2},{3,11},{11,3},{4,12},{12,4},... | collective-permute-start | bytes 294920 | tf_op jit(solution)/shard_map/ppermute | solution.py:26
  113.1 10.1 %collective-permute-start.6 = (f32[24,16,128]{2,1,0:T(8,128)S(1)}, f32[24,16,128]{2,1,0:T(8,128)S(1)}, u32[]{:S(2)}, u32[]{:S(2)}) collective-permute-start(f32[24,16,128]{2,1,0:T(8,128)S(1)} %pad_maximum_fusion.3), channel_id=1, source_target_pairs={{0,192},{192,384},{384,576},{576,0},{1,193},{193,385},{385,577},{5... | collective-permute-start | bytes 589832 | tf_op jit(solution)/shard_map/ppermute | solution.py:26
  123.2 13.7 %collective-permute-start.7 = (f32[48,16,128]{2,1,0:T(8,128)S(1)}, f32[48,16,128]{2,1,0:T(8,128)S(1)}, u32[]{:S(2)}, u32[]{:S(2)}) collective-permute-start(f32[48,16,128]{2,1,0:T(8,128)S(1)} %pad_maximum_fusion.2), channel_id=1, source_target_pairs={{0,384},{192,576},{384,0},{576,192},{1,385},{193,577},{385,1},{577... | collective-permute-start | bytes 1179656 | tf_op jit(solution)/shard_map/ppermute | solution.py:26
Sparse Core Ops, SparseCore 0:
  74.8 42.1 reduce-scatter.1

commit v5 on v4

--- a/solution.py
+++ b/solution.py
@@ -27,6 +27,17 @@
         rows[: extra * per], name, [(sender, (sender + have) % size) for sender in range(size)]
     )
     return jnp.concatenate([rows, coming], axis=0)
+
+
+def halved(blocks, bit):
+    side = (lax.axis_index("chan") // bit) % 2
+    pairs = blocks.reshape((-1, 2) + blocks.shape[1:])
+    coming = lax.ppermute(
+        lax.dynamic_index_in_dim(pairs, 1 - side, 1, keepdims=False),
+        "chan",
+        [(sender, sender ^ bit) for sender in range(lax.axis_size("chan"))],
+    )
+    return lax.dynamic_index_in_dim(pairs, side, 1, keepdims=False) + coming
 
 
 def exchange(blocks, axes):
@@ -84,9 +95,7 @@
         inner_part * features.reshape(pixels, channels).astype(jnp.float32), axis=0
     ) + (2.0 * styles * jnp.dot(square_grad, weight_sq.T, precision=highest)).reshape(channels)
 
-    grad_inner = lax.psum_scatter(inner_part, "chan", scatter_dimension=1, tiled=True)
-    style_cols = lax.dynamic_slice_in_dim(styles, chan_id * cols_dev, cols_dev, 1)
-    grad_input = (grad_inner * style_cols).astype(jnp.bfloat16)
+    inner_part = inner_part.reshape(pixels, nchan, cols_dev).transpose(1, 0, 2)
 
     style_factor = jnp.dot(style_sq.T, square_grad, precision=highest)
     product_rows = lax.dot_general(
@@ -100,9 +109,7 @@
         ],
         axis=0,
     )
-    tile, product_rows, map_rows, rows_z2 = lax.optimization_barrier(
-        (tile, product_rows, map_rows, rows_z2)
-    )
+    tile, map_rows, rows_z2 = lax.optimization_barrier((tile, map_rows, rows_z2))
     parts = exchange(
         jnp.broadcast_to(tile[None], (ncore * nchan,) + tile.shape), ("core", "chan")
     ).reshape(ncore, nchan, -1, LANES)
@@ -130,7 +137,9 @@
     riders = jnp.concatenate(
         [style_rows, hidden_rows, parts[:, 0, -1], jnp.zeros((8 - 3 * ncore, cols_dev))], axis=0
     )
-    coming, riders, rows_z4 = lax.optimization_barrier((coming, riders, rows_z4))
+    coming, riders, rows_z4, inner_part = lax.optimization_barrier(
+        (coming, riders, rows_z4, inner_part)
+    )
     pieces = lax.dynamic_index_in_dim(pieces, core_id, 2, keepdims=False) + coming
     moved = exchange(
         jnp.concatenate(
@@ -142,6 +151,7 @@
         ),
         "x",
     )
+    inner_half = halved(inner_part, 1)
     have = 4
     rows_z = rows_z4
     while have < nz:
@@ -157,7 +167,9 @@
         ],
         axis=0,
     )
-    pieces, riders, rows_z = lax.optimization_barrier((pieces, riders, rows_z))
+    pieces, riders, rows_z, inner_half = lax.optimization_barrier(
+        (pieces, riders, rows_z, inner_half)
+    )
     moved = exchange(
         jnp.concatenate([pieces, jnp.broadcast_to(riders[None], (nz,) + riders.shape)], axis=1), "z"
     )
@@ -174,6 +186,12 @@
         for name, back in (("x", back_x), ("z", back_z), ("core", back_core))
     ]
     row_ids = ((spots[0] * nz + spots[1]) * ncore + spots[2]).astype(jnp.float32)
+    bit = 2
+    while bit < nchan:
+        inner_half = halved(inner_half, bit)
+        bit *= 2
+    style_cols = lax.dynamic_slice_in_dim(styles, chan_id * cols_dev, cols_dev, 1)
+    grad_input = (inner_half[0] * style_cols).astype(jnp.bfloat16)
     grad_weight = jnp.sum(moved[:, :rows_dev], axis=0) / batch_size
 
     per = nx * ncore
@@ -196,12 +214,12 @@
     all_pre = gathered[:, half:].reshape(batch_size, -1)
     hidden = jnp.where(all_pre > 0, all_pre, 0.2 * all_pre)
     grad_map_out = (
-        lax.dot_general(hidden, incoming, (((0,), (0,)), ((), ())), precision=highest) / batch_size
+        lax.dot_general(hidden, incoming, (((0,), (0,)), ((), ())), precision=lax.Precision.HIGH) / batch_size
     )
     pre_cols = lax.dynamic_slice_in_dim(all_pre, chan_id * cols_dev, cols_dev, 1)
     pre_grad = hidden_grad * jnp.where(pre_cols > 0, 1.0, 0.2)
     grad_map_in = (
-        lax.dot_general(all_latents, pre_grad, (((0,), (0,)), ((), ())), precision=highest)
+        lax.dot_general(all_latents, pre_grad, (((0,), (0,)), ((), ())), precision=lax.Precision.HIGH)
         / batch_size
     )
     return (

time: 151 us -> 172 us (1.14)
  the two profiles are of different devices: /device:TPU:72 before, /device:TPU:1 now
where the time goes in v5:
time: 172 us; the launch traced here: 171 us
  starting transfers between devices  69.5 us (40%)
  waiting for transfers between devices  39.4 us (23%)
  local copies, waits for them, and re-layouts  22.7 us (13%)
  matrix products  19.4 us (11%)
  other arithmetic  17.5 us (10%)
  between operations  2.58 us (2%)
    ppermute x7, starting transfers between devices, doubled(): lax.ppermute(rows[:extra * per], name, [(sender, (sender + have) % size)...  25.3 us
    all_to_all x4, starting transfers between devices, exchange(): return lax.all_to_all(blocks, axes, 0, 0, tiled=True)  24.5 us
    ppermute x3, waiting for transfers between devices, halved(): lax.ppermute(lax.dynamic_index_in_dim(pairs, 1 - side, 1, keepdims=False)...  15.4 us
    ppermute x7, waiting for transfers between devices, doubled(): lax.ppermute(rows[:extra * per], name, [(sender, (sender + have) % size)...  15.1 us
    unnamed x36, local copies, waits for them, and re-layouts  13.2 us
    ppermute x3, starting transfers between devices, halved(): lax.ppermute(lax.dynamic_index_in_dim(pairs, 1 - side, 1, keepdims=False)...  12.9 us
    all_to_all x4, waiting for transfers between devices, exchange(): return lax.all_to_all(blocks, axes, 0, 0, tiled=True)  8.9 us
    dot_general x1, matrix products, local(): lax.dot_general(patches, grad_scaled, (((0,), (0,)), ((), ())), preferred...  7.39 us
  transfers between devices with their start and end apart: 15, of which 6 were waited for; matrix products, arithmetic and copies ran while one was open for 28% of the time, Pallas kernels for 0%

profile of v5, /device:TPU:1, one launch (start us, length us, event | category | flops | bytes accessed | tf_op | source)
XLA Modules:
  0.0 171.1 jit_solution(4332182255644436759)
XLA Ops:
  1.5 4.8 %collective-permute-start.1 = (f32[1,16,128]{2,1,0:T(8,128)S(1)}, f32[1,16,128]{2,1,0:T(8,128)S(1)}, u32[]{:S(2)}, u32[]{:S(2)}) collective-permute-start(f32[1,16,128]{2,1,0:T(8,128)S(1)} %pad_maximum_fusion.8), channel_id=1, source_target_pairs={{0,16},{16,32},{32,48},{48,64},{64,80},{80,96},{96,112},{112,128},... | collective-permute-start | bytes 24584 | tf_op jit(solution)/shard_map/ppermute | solution.py:26
  6.3 6.8 %all-to-all-start = ((f32[8,128,128]{2,1,0:T(8,128)}), f32[8,128,128]{2,1,0:T(8,128)}, u32[]{:S(2)}, u32[]{:S(2)}) async-start(f32[8,128,128]{2,1,0:T(8,128)} %bitcast.178), calls=%async_computation | async-start | bytes 1048576 | tf_op jit(solution)/shard_map/all_to_all | solution.py:44
  15.1 2.0 %pad_slice_fusion = (bf16[1,16,16,1024]{3,2,1,0:T(8,128)(2,1)}, bf16[1,16,16,1024]{3,2,1,0:T(8,128)(2,1)}, bf16[1,16,16,1024]{3,2,1,0:T(8,128)(2,1)}, bf16[1,16,...) fusion(bf16[1,16,16,1024]{3,2,1,0:T(8,128)(2,1)S(1)} %multiply_, ...), kind=kLoop, calls=%fused_computation.7 | loop fusion | bytes 4718592 | tf_op jit(solution)/shard_map/slice | solution.py:19
  18.6 2.0 %constant_dynamic-update-slice_fusion.7 = bf16[256,9216]{1,0:T(8,128)(2,1)} fusion(bf16[256,9216]{1,0:T(8,128)(2,1)} %constant_dynamic-update-slice_fusion.8, bf16[256,1024]{1,0:T(8,128)(2,1)} %bitcast.173), kind=kLoop, calls=%fused_computation.106 | loop fusion | bytes 1048576
  20.6 1.9 %constant_dynamic-update-slice_fusion.6 = bf16[256,9216]{1,0:T(8,128)(2,1)} fusion(bf16[256,9216]{1,0:T(8,128)(2,1)} %constant_dynamic-update-slice_fusion.7, bf16[256,1024]{1,0:T(8,128)(2,1)} %bitcast.172), kind=kLoop, calls=%fused_computation.105 | loop fusion | bytes 1048576
  22.5 1.9 %constant_dynamic-update-slice_fusion.5 = bf16[256,9216]{1,0:T(8,128)(2,1)} fusion(bf16[256,9216]{1,0:T(8,128)(2,1)} %constant_dynamic-update-slice_fusion.6, bf16[256,1024]{1,0:T(8,128)(2,1)} %bitcast.171), kind=kLoop, calls=%fused_computation.104 | loop fusion | bytes 1048576
  25.2 1.9 %constant_dynamic-update-slice_fusion.3 = bf16[256,9216]{1,0:T(8,128)(2,1)} fusion(bf16[256,9216]{1,0:T(8,128)(2,1)} %constant_dynamic-update-slice_fusion.4, bf16[256,1024]{1,0:T(8,128)(2,1)} %bitcast.170), kind=kLoop, calls=%fused_computation.102 | loop fusion | bytes 1048576
  29.7 3.7 %fusion = f32[128]{0:T(128)S(1)} fusion(bf16[256,9216]{1,0:T(8,128)(2,1)} %constant_dynamic-update-slice_fusion, bf16[9216,128]{1,0:T(8,128)(2,1)S(1)} %bitcast.155, bf16[256,128]{1,0:T(8,128)(2,1)S(1)} %bitcast.176), kind=kOutput, calls=%fused_computation.27 | convolution fusion | flops 604077952 | bytes 7143936 | tf_op jit(solution)/shard_map/dot_general | solution.py:78
  34.1 4.5 %bitcast_multiply_fusion = f32[9216,128]{1,0:T(8,128)} fusion(f32[1024,128]{1,0:T(8,128)S(1)} %broadcast_multiply_fusion, bf16[9,1024,128]{2,1,0:T(8,128)(2,1)S(1)} %copy-done), kind=kLoop, calls=%fused_computation.1 | loop fusion | flops 3538944 | bytes 7602176 | tf_op jit(solution)/shard_map/mul | solution.py:103
  38.5 7.4 %convolution_add_fusion = f32[9216,128]{1,0:T(8,128)} fusion(f32[9216,128]{1,0:T(8,128)} %bitcast_multiply_fusion, bf16[256,9216]{1,0:T(8,128)(2,1)} %constant_dynamic-update-slice_fusion, bf16[256,128]{1,0:T(8,128)(2,1)S(1)} %fusion.28), kind=kOutput, calls=%fused_computation | convolution fusion | flops 605159424 | bytes 14221312 | tf_op jit(solution)/shard_map/dot_general | solution.py:101
  45.9 3.2 %dynamic-slice_bitcast_fusion = f32[4,12,96,128]{3,2,1,0:T(8,128)} fusion(f32[4,12,2,96,128]{4,3,2,1,0:T(8,128)} %bitcast.156, s32[]{:T(128)S(6)} %select_n.85), kind=kLoop, calls=%fused_computation.6 | loop fusion | bytes 4718596 | tf_op jit(solution)/shard_map/jit(dynamic_index_in_dim)/squeeze | solution.py:119
  49.2 6.8 %collective-permute-start = (f32[4,12,96,128]{3,2,1,0:T(8,128)}, f32[4,12,96,128]{3,2,1,0:T(8,128)}, u32[]{:S(2)}, u32[]{:S(2)}) collective-permute-start(f32[4,12,96,128]{3,2,1,0:T(8,128)} %dynamic-slice_bitcast_fusion), channel_id=1, source_target_pairs={{0,8},{8,0},{1,9},{9,1},{2,10},{10,2},{3,11},{11,3},{4,12},{12,4},... | collective-permute-start | bytes 7077896 | tf_op jit(solution)/shard_map/ppermute | solution.py:118
  61.5 7.2 %all-to-all-start.1 = ((f32[16,16,128]{2,1,0:T(8,128)}), f32[16,16,128]{2,1,0:T(8,128)S(1)}, u32[]{:S(2)}, u32[]{:S(2)}) async-start(f32[16,16,128]{2,1,0:T(8,128)} %broadcast_in_dim.22), calls=%async_computation.1 | async-start | bytes 262144 | tf_op jit(solution)/shard_map/all_to_all | solution.py:44
  68.7 2.2 %collective-permute-start.2 = (f32[2,16,128]{2,1,0:T(8,128)S(1)}, f32[2,16,128]{2,1,0:T(8,128)S(1)}, u32[]{:S(2)}, u32[]{:S(2)}) collective-permute-start(f32[2,16,128]{2,1,0:T(8,128)S(1)} %pad_maximum_fusion.6), channel_id=1, source_target_pairs={{0,32},{16,48},{32,64},{48,80},{64,96},{80,112},{96,128},{112,144}... | collective-permute-start | bytes 49160 | tf_op jit(solution)/shard_map/ppermute | solution.py:26
  72.2 7.4 %collective-permute-done.2 = f32[2,16,128]{2,1,0:T(8,128)S(1)} collective-permute-done((f32[2,16,128]{2,1,0:T(8,128)S(1)}, f32[2,16,128]{2,1,0:T(8,128)S(1)}, u32[]{:S(2)}, u32[]{:S(2)}) %collective-permute-start.2) | collective-permute-done | bytes 16416 | tf_op jit(solution)/shard_map/ppermute | solution.py:26
  81.3 2.8 %bitcast_add_fusion = f32[4,12,96,128]{3,2,1,0:T(8,128)S(1)} fusion(f32[4,12,96,128]{3,2,1,0:T(8,128)} %collective-permute-done, f32[4,12,2,96,128]{4,3,2,1,0:T(8,128)} %bitcast.157, s32[]{:T(128)S(6)} %select_n.84), kind=kLoop, calls=%fused_computation.5 | loop fusion | flops 589824 | bytes 7077892 | tf_op jit(solution)/shard_map/add | solution.py:143
  85.7 4.0 %all-to-all-start.2 = ((f32[4,1160,128]{2,1,0:T(8,128)}), f32[4,1160,128]{2,1,0:T(8,128)S(1)}, u32[]{:S(2)}, u32[]{:S(2)}) async-start(f32[4,1160,128]{2,1,0:T(8,128)} %pad_maximum_fusion), calls=%async_computation.2 | async-start | bytes 4751360 | tf_op jit(solution)/shard_map/all_to_all | solution.py:44
  89.7 1.7 constant_dynamic-slice_fusion.3
  91.4 3.3 %collective-permute-start.5 = (f32[4,256,128]{2,1,0:T(8,128)S(1)}, f32[4,256,128]{2,1,0:T(8,128)S(1)}, u32[]{:S(2)}, u32[]{:S(2)}) collective-permute-start(f32[4,256,128]{2,1,0:T(8,128)S(1)} %bitcast.179), channel_id=1, source_target_pairs={{0,1},{1,0},{2,3},{3,2},{4,5},{5,4},{6,7},{7,6},{8,9},{9,8},{10,11... | collective-permute-start | bytes 1572872 | tf_op jit(solution)/shard_map/ppermute | solution.py:35
  94.7 3.5 %collective-permute-start.3 = (f32[4,16,128]{2,1,0:T(8,128)S(1)}, f32[4,16,128]{2,1,0:T(8,128)S(1)}, u32[]{:S(2)}, u32[]{:S(2)}) collective-permute-start(f32[4,16,128]{2,1,0:T(8,128)S(1)} %pad_maximum_fusion.5), channel_id=1, source_target_pairs={{0,64},{16,80},{32,96},{48,112},{64,128},{80,144},{96,160},{112,17... | collective-permute-start | bytes 98312 | tf_op jit(solution)/shard_map/ppermute | solution.py:26
  98.3 5.7 %collective-permute-start.4 = (f32[4,16,128]{2,1,0:T(8,128)S(1)}, f32[4,16,128]{2,1,0:T(8,128)}, u32[]{:S(2)}, u32[]{:S(2)}) collective-permute-start(f32[4,16,128]{2,1,0:T(8,128)S(1)} %pad_maximum_fusion.5), channel_id=1, source_target_pairs={{0,128},{16,144},{32,160},{48,176},{64,0},{80,16},{96,32},{112,48}... | collective-permute-start | bytes 98312 | tf_op jit(solution)/shard_map/ppermute | solution.py:26
  104.6 2.4 %collective-permute-done.4 = f32[4,16,128]{2,1,0:T(8,128)} collective-permute-done((f32[4,16,128]{2,1,0:T(8,128)S(1)}, f32[4,16,128]{2,1,0:T(8,128)}, u32[]{:S(2)}, u32[]{:S(2)}) %collective-permute-start.4) | collective-permute-done | bytes 32800 | tf_op jit(solution)/shard_map/ppermute | solution.py:26
  108.9 8.9 %all-to-all-done.2 = f32[4,1160,128]{2,1,0:T(8,128)S(1)} async-done(((f32[4,1160,128]{2,1,0:T(8,128)}), f32[4,1160,128]{2,1,0:T(8,128)S(1)}, u32[]{:S(2)}, u32[]{:S(2)}) %all-to-all-start.2) | async-done | bytes 2375712 | tf_op jit(solution)/shard_map/all_to_all | solution.py:44
  118.9 6.5 %all-to-all-start.3 = ((f32[12,120,128]{2,1,0:T(8,128)}), f32[12,120,128]{2,1,0:T(8,128)S(1)}, u32[]{:S(2)}, u32[]{:S(2)}) async-start(f32[12,120,128]{2,1,0:T(8,128)} %pad_maximum_fusion.1), calls=%async_computation.3 | async-start | bytes 1474560 | tf_op jit(solution)/shard_map/all_to_all | solution.py:44
  126.8 4.7 %collective-permute-start.8 = (f32[12,16,128]{2,1,0:T(8,128)S(1)}, f32[12,16,128]{2,1,0:T(8,128)S(1)}, u32[]{:S(2)}, u32[]{:S(2)}) collective-permute-start(f32[12,16,128]{2,1,0:T(8,128)S(1)} %pad_maximum_fusion.4), channel_id=1, source_target_pairs={{0,8},{8,0},{1,9},{9,1},{2,10},{10,2},{3,11},{11,3},{4,12},{12,4},... | collective-permute-start | bytes 294920 | tf_op jit(solution)/shard_map/ppermute | solution.py:26
  131.5 3.8 %collective-permute-start.6 = (f32[2,256,128]{2,1,0:T(8,128)S(1)}, f32[2,256,128]{2,1,0:T(8,128)S(1)}, u32[]{:S(2)}, u32[]{:S(2)}) collective-permute-start(f32[2,256,128]{2,1,0:T(8,128)S(1)} %dynamic-slice_bitcast_fusion.1), channel_id=1, source_target_pairs={{0,2},{1,3},{2,0},{3,1},{4,6},{5,7},{6,4},{7,5},{8,10},{9,11},{10,... | collective-permute-start | bytes 786440 | tf_op jit(solution)/shard_map/ppermute | solution.py:35
  135.4 2.2 %collective-permute-start.9 = (f32[24,16,128]{2,1,0:T(8,128)S(1)}, f32[24,16,128]{2,1,0:T(8,128)S(1)}, u32[]{:S(2)}, u32[]{:S(2)}) collective-permute-start(f32[24,16,128]{2,1,0:T(8,128)S(1)} %pad_maximum_fusion.3), channel_id=1, source_target_pairs={{0,192},{192,384},{384,576},{576,0},{1,193},{193,385},{385,577},{5... | collective-permute-start | bytes 589832 | tf_op jit(solution)/shard_map/ppermute | solution.py:26
  137.6 10.3 %collective-permute-done.6 = f32[2,256,128]{2,1,0:T(8,128)S(1)} collective-permute-done((f32[2,256,128]{2,1,0:T(8,128)S(1)}, f32[2,256,128]{2,1,0:T(8,128)S(1)}, u32[]{:S(2)}, u32[]{:S(2)}) %collective-permute-start.6) | collective-permute-done | bytes 262176 | tf_op jit(solution)/shard_map/ppermute | solution.py:35
  147.9 5.8 %collective-permute-start.7 = (f32[1,256,128]{2,1,0:T(8,128)S(1)}, f32[1,256,128]{2,1,0:T(8,128)S(1)}, u32[]{:S(2)}, u32[]{:S(2)}) collective-permute-start(f32[1,256,128]{2,1,0:T(8,128)S(1)} %constant_dynamic-slice_fusion.1), channel_id=1, source_target_pairs={{0,4},{1,5},{2,6},{3,7},{4,0},{5,1},{6,2},{7,3},{8,12},{9,13},{10,... | collective-permute-start | bytes 393224 | tf_op jit(solution)/shard_map/ppermute | solution.py:35
  153.7 2.2 %collective-permute-start.10 = (f32[48,16,128]{2,1,0:T(8,128)S(1)}, f32[48,16,128]{2,1,0:T(8,128)S(1)}, u32[]{:S(2)}, u32[]{:S(2)}) collective-permute-start(f32[48,16,128]{2,1,0:T(8,128)S(1)} %pad_maximum_fusion.2), channel_id=1, source_target_pairs={{0,384},{192,576},{384,0},{576,192},{1,385},{193,577},{385,1},{577... | collective-permute-start | bytes 1179656 | tf_op jit(solution)/shard_map/ppermute | solution.py:26
  155.9 5.2 %collective-permute-done.7 = f32[1,256,128]{2,1,0:T(8,128)S(1)} collective-permute-done((f32[1,256,128]{2,1,0:T(8,128)S(1)}, f32[1,256,128]{2,1,0:T(8,128)S(1)}, u32[]{:S(2)}, u32[]{:S(2)}) %collective-permute-start.7) | collective-permute-done | bytes 131104 | tf_op jit(solution)/shard_map/ppermute | solution.py:35
  161.8 5.2 %collective-permute-done.10 = f32[48,16,128]{2,1,0:T(8,128)S(1)} collective-permute-done((f32[48,16,128]{2,1,0:T(8,128)S(1)}, f32[48,16,128]{2,1,0:T(8,128)S(1)}, u32[]{:S(2)}, u32[]{:S(2)}) %collective-permute-start.10) | collective-permute-done | bytes 393248 | tf_op jit(solution)/shard_map/ppermute | solution.py:26
  (100 shorter events, 26.6 us)
Async XLA Ops:
  0.6 17.4 %copy-start = (bf16[9,1024,128]{2,1,0:T(8,128)(2,1)S(1)}, bf16[9,1024,128]{2,1,0:T(8,128)(2,1)}, u32[]{:S(2)}) copy-start(bf16[9,1024,128]{2,1,0:T(8,128)(2,1)} %param.14) | copy-start | bytes 7077892
  1.5 59.3 %collective-permute-start.1 = (f32[1,16,128]{2,1,0:T(8,128)S(1)}, f32[1,16,128]{2,1,0:T(8,128)S(1)}, u32[]{:S(2)}, u32[]{:S(2)}) collective-permute-start(f32[1,16,128]{2,1,0:T(8,128)S(1)} %pad_maximum_fusion.8), channel_id=1, source_target_pairs={{0,16},{16,32},{32,48},{48,64},{64,80},{80,96},{96,112},{112,128},... | collective-permute-start | bytes 24584 | tf_op jit(solution)/shard_map/ppermute | solution.py:26
  6.3 54.5 %all-to-all-start = ((f32[8,128,128]{2,1,0:T(8,128)}), f32[8,128,128]{2,1,0:T(8,128)}, u32[]{:S(2)}, u32[]{:S(2)}) async-start(f32[8,128,128]{2,1,0:T(8,128)} %bitcast.178), calls=%async_computation | async-start | bytes 1048576 | tf_op jit(solution)/shard_map/all_to_all | solution.py:44
  18.5 11.2 %copy-start.6 = (bf16[1,16,16,128]{3,2,1,0:T(8,128)(2,1)S(1)}, bf16[1,16,16,128]{3,2,1,0:T(8,128)(2,1)}, u32[]{:S(2)}) copy-start(bf16[1,16,16,128]{3,2,1,0:T(8,128)(2,1)} %param.15) | copy-start | bytes 196612
  18.5 8.6 %copy-start.4 = (bf16[1,16,16,1024]{3,2,1,0:T(8,128)(2,1)S(1)}, bf16[1,16,16,1024]{3,2,1,0:T(8,128)(2,1)}, u32[]{:S(2)}) copy-start(bf16[1,16,16,1024]{3,2,1,0:T(8,128)(2,1)} %get-tuple-element.41) | copy-start | bytes 1572868
  18.5 9.5 %copy-start.3 = (bf16[1,16,16,1024]{3,2,1,0:T(8,128)(2,1)S(1)}, bf16[1,16,16,1024]{3,2,1,0:T(8,128)(2,1)}, u32[]{:S(2)}) copy-start(bf16[1,16,16,1024]{3,2,1,0:T(8,128)(2,1)} %get-tuple-element.42) | copy-start | bytes 1572868
  18.5 10.3 %copy-start.2 = (bf16[1,16,16,1024]{3,2,1,0:T(8,128)(2,1)S(1)}, bf16[1,16,16,1024]{3,2,1,0:T(8,128)(2,1)}, u32[]{:S(2)}) copy-start(bf16[1,16,16,1024]{3,2,1,0:T(8,128)(2,1)} %get-tuple-element.36) | copy-start | bytes 1572868
  28.0 5.5 %copy-start.7 = (f32[1,1024]{1,0:T(1,128)S(1)}, f32[1,1024]{1,0:T(1,128)}, u32[]{:S(2)}) copy-start(f32[1,1024]{1,0:T(1,128)} %param.13) | copy-start | bytes 12292
  49.2 32.2 %collective-permute-start = (f32[4,12,96,128]{3,2,1,0:T(8,128)}, f32[4,12,96,128]{3,2,1,0:T(8,128)}, u32[]{:S(2)}, u32[]{:S(2)}) collective-permute-start(f32[4,12,96,128]{3,2,1,0:T(8,128)} %dynamic-slice_bitcast_fusion), channel_id=1, source_target_pairs={{0,8},{8,0},{1,9},{9,1},{2,10},{10,2},{3,11},{11,3},{4,12},{12,4},... | collective-permute-start | bytes 7077896 | tf_op jit(solution)/shard_map/ppermute | solution.py:118
  57.3 1.8 %copy-start.5 = (bf16[1,16,16,1024]{3,2,1,0:T(8,128)(2,1)S(1)}, bf16[1,16,16,1024]{3,2,1,0:T(8,128)(2,1)}, u32[]{:S(2)}) copy-start(bf16[1,16,16,1024]{3,2,1,0:T(8,128)(2,1)} %param.12) | copy-start | bytes 1572868
  58.2 2.6 %copy-start.9 = (f32[1,1024]{1,0:T(1,128)S(1)}, f32[1,1024]{1,0:T(1,128)}, u32[]{:S(2)}) copy-start(f32[1,1024]{1,0:T(1,128)} %param.19) | copy-start | bytes 12292
  58.2 2.6 %copy-start.10 = (f32[1,1024]{1,0:T(1,128)S(1)}, f32[1,1024]{1,0:T(1,128)}, u32[]{:S(2)}) copy-start(f32[1,1024]{1,0:T(1,128)} %param.18) | copy-start | bytes 12292
  61.5 18.1 %all-to-all-start.1 = ((f32[16,16,128]{2,1,0:T(8,128)}), f32[16,16,128]{2,1,0:T(8,128)S(1)}, u32[]{:S(2)}, u32[]{:S(2)}) async-start(f32[16,16,128]{2,1,0:T(8,128)} %broadcast_in_dim.22), calls=%async_computation.1 | async-start | bytes 262144 | tf_op jit(solution)/shard_map/all_to_all | solution.py:44
  68.7 10.9 %collective-permute-start.2 = (f32[2,16,128]{2,1,0:T(8,128)S(1)}, f32[2,16,128]{2,1,0:T(8,128)S(1)}, u32[]{:S(2)}, u32[]{:S(2)}) collective-permute-start(f32[2,16,128]{2,1,0:T(8,128)S(1)} %pad_maximum_fusion.6), channel_id=1, source_target_pairs={{0,32},{16,48},{32,64},{48,80},{64,96},{80,112},{96,128},{112,144}... | collective-permute-start | bytes 49160 | tf_op jit(solution)/shard_map/ppermute | solution.py:26
  84.1 5.6 %copy-start.1 = (f32[32,8,8,128]{3,2,1,0:T(8,128)S(1)}, f32[32,8,8,128]{3,2,1,0:T(8,128)}, u32[]{:S(2)}) copy-start(f32[32,8,8,128]{3,2,1,0:T(8,128)} %copy.31) | copy-start | bytes 3145732
  85.7 32.1 %all-to-all-start.2 = ((f32[4,1160,128]{2,1,0:T(8,128)}), f32[4,1160,128]{2,1,0:T(8,128)S(1)}, u32[]{:S(2)}, u32[]{:S(2)}) async-start(f32[4,1160,128]{2,1,0:T(8,128)} %pad_maximum_fusion), calls=%async_computation.2 | async-start | bytes 4751360 | tf_op jit(solution)/shard_map/all_to_all | solution.py:44
  91.4 16.4 %collective-permute-start.5 = (f32[4,256,128]{2,1,0:T(8,128)S(1)}, f32[4,256,128]{2,1,0:T(8,128)S(1)}, u32[]{:S(2)}, u32[]{:S(2)}) collective-permute-start(f32[4,256,128]{2,1,0:T(8,128)S(1)} %bitcast.179), channel_id=1, source_target_pairs={{0,1},{1,0},{2,3},{3,2},{4,5},{5,4},{6,7},{7,6},{8,9},{9,8},{10,11... | collective-permute-start | bytes 1572872 | tf_op jit(solution)/shard_map/ppermute | solution.py:35
  94.7 9.2 %collective-permute-start.3 = (f32[4,16,128]{2,1,0:T(8,128)S(1)}, f32[4,16,128]{2,1,0:T(8,128)S(1)}, u32[]{:S(2)}, u32[]{:S(2)}) collective-permute-start(f32[4,16,128]{2,1,0:T(8,128)S(1)} %pad_maximum_fusion.5), channel_id=1, source_target_pairs={{0,64},{16,80},{32,96},{48,112},{64,128},{80,144},{96,160},{112,17... | collective-permute-start | bytes 98312 | tf_op jit(solution)/shard_map/ppermute | solution.py:26
  98.3 8.7 %collective-permute-start.4 = (f32[4,16,128]{2,1,0:T(8,128)S(1)}, f32[4,16,128]{2,1,0:T(8,128)}, u32[]{:S(2)}, u32[]{:S(2)}) collective-permute-start(f32[4,16,128]{2,1,0:T(8,128)S(1)} %pad_maximum_fusion.5), channel_id=1, source_target_pairs={{0,128},{16,144},{32,160},{48,176},{64,0},{80,16},{96,32},{112,48}... | collective-permute-start | bytes 98312 | tf_op jit(solution)/shard_map/ppermute | solution.py:26
  104.0 0.6 copy-start.8
  118.9 48.3 %all-to-all-start.3 = ((f32[12,120,128]{2,1,0:T(8,128)}), f32[12,120,128]{2,1,0:T(8,128)S(1)}, u32[]{:S(2)}, u32[]{:S(2)}) async-start(f32[12,120,128]{2,1,0:T(8,128)} %pad_maximum_fusion.1), calls=%async_computation.3 | async-start | bytes 1474560 | tf_op jit(solution)/shard_map/all_to_all | solution.py:44
  126.8 8.5 %collective-permute-start.8 = (f32[12,16,128]{2,1,0:T(8,128)S(1)}, f32[12,16,128]{2,1,0:T(8,128)S(1)}, u32[]{:S(2)}, u32[]{:S(2)}) collective-permute-start(f32[12,16,128]{2,1,0:T(8,128)S(1)} %pad_maximum_fusion.4), channel_id=1, source_target_pairs={{0,8},{8,0},{1,9},{9,1},{2,10},{10,2},{3,11},{11,3},{4,12},{12,4},... | collective-permute-start | bytes 294920 | tf_op jit(solution)/shard_map/ppermute | solution.py:26
  131.5 16.3 %collective-permute-start.6 = (f32[2,256,128]{2,1,0:T(8,128)S(1)}, f32[2,256,128]{2,1,0:T(8,128)S(1)}, u32[]{:S(2)}, u32[]{:S(2)}) collective-permute-start(f32[2,256,128]{2,1,0:T(8,128)S(1)} %dynamic-slice_bitcast_fusion.1), channel_id=1, source_target_pairs={{0,2},{1,3},{2,0},{3,1},{4,6},{5,7},{6,4},{7,5},{8,10},{9,11},{10,... | collective-permute-start | bytes 786440 | tf_op jit(solution)/shard_map/ppermute | solution.py:35
  135.4 18.3 %collective-permute-start.9 = (f32[24,16,128]{2,1,0:T(8,128)S(1)}, f32[24,16,128]{2,1,0:T(8,128)S(1)}, u32[]{:S(2)}, u32[]{:S(2)}) collective-permute-start(f32[24,16,128]{2,1,0:T(8,128)S(1)} %pad_maximum_fusion.3), channel_id=1, source_target_pairs={{0,192},{192,384},{384,576},{576,0},{1,193},{193,385},{385,577},{5... | collective-permute-start | bytes 589832 | tf_op jit(solution)/shard_map/ppermute | solution.py:26
  147.9 13.2 %collective-permute-start.7 = (f32[1,256,128]{2,1,0:T(8,128)S(1)}, f32[1,256,128]{2,1,0:T(8,128)S(1)}, u32[]{:S(2)}, u32[]{:S(2)}) collective-permute-start(f32[1,256,128]{2,1,0:T(8,128)S(1)} %constant_dynamic-slice_fusion.1), channel_id=1, source_target_pairs={{0,4},{1,5},{2,6},{3,7},{4,0},{5,1},{6,2},{7,3},{8,12},{9,13},{10,... | collective-permute-start | bytes 393224 | tf_op jit(solution)/shard_map/ppermute | solution.py:35
  153.7 13.3 %collective-permute-start.10 = (f32[48,16,128]{2,1,0:T(8,128)S(1)}, f32[48,16,128]{2,1,0:T(8,128)S(1)}, u32[]{:S(2)}, u32[]{:S(2)}) collective-permute-start(f32[48,16,128]{2,1,0:T(8,128)S(1)} %pad_maximum_fusion.2), channel_id=1, source_target_pairs={{0,384},{192,576},{384,0},{576,192},{1,385},{193,577},{385,1},{577... | collective-permute-start | bytes 1179656 | tf_op jit(solution)/shard_map/ppermute | solution.py:26

commit v6 on v5

--- a/solution.py
+++ b/solution.py
@@ -1,7 +1,11 @@
+import functools
+
 import jax
 import jax.numpy as jnp
 import numpy as np
 from jax import lax
+from jax.experimental import pallas as pl
+from jax.experimental.pallas import tpu as pltpu
 from jax.sharding import Mesh, PartitionSpec as P
 
 KTAPS = 9
@@ -15,8 +19,149 @@
     return (4, 12, 2) if dp_count == 96 else (2, dp_count // 4, 2)
 
 
-def tap_window(padded, row_off, col_off, side_len):
-    return padded[:, row_off : row_off + side_len, col_off : col_off + side_len, :]
+def convolution_kernel(
+    side, core_ref, feat_ref, style_ref, weight_ref, grad_ref, source_ref,
+    sent_ref, kept_ref, inner_ref, tile_ref,
+    scaled_t, shifted, product, square, factor,
+):
+    pixels, channels = feat_ref.shape
+    cols = grad_ref.shape[1]
+    block = min(256, channels)
+    rows_dev = sent_ref.shape[1]
+    f32, bf16 = jnp.float32, jnp.bfloat16
+
+    for start in range(0, channels, LANES):
+        total = jnp.zeros((LANES, cols), f32)
+        for tap in range(KTAPS):
+            wide = weight_ref[tap * channels + start : tap * channels + start + LANES].astype(f32)
+            total = total + wide * wide
+        square[start : start + LANES] = total
+    style = style_ref[...]
+    style_sq = jnp.broadcast_to(style * style, (8, channels))
+    norm = jnp.dot(style_sq, square[...], precision=highest, preferred_element_type=f32)
+    demodulate = lax.rsqrt(norm[:1] + 1e-08)
+
+    grad_scaled = (grad_ref[...].astype(f32) * demodulate).astype(bf16).astype(f32)
+    place = lax.broadcasted_iota(jnp.int32, (pixels, cols), 0)
+    row, col = place // side, place % side
+    for tap in range(KTAPS):
+        down, right = tap // 3 - 1, tap % 3 - 1
+        moved = grad_scaled
+        if down or right:
+            moved = pltpu.roll(grad_scaled, (down * side + right) % pixels, 0)
+            inside = (
+                (row >= down) & (row < side + down) & (col >= right) & (col < side + right)
+            )
+            moved = jnp.where(inside, moved, 0.0)
+        shifted[:, tap * cols : (tap + 1) * cols] = moved.astype(bf16)
+
+    demod_grad = jnp.zeros((8, cols), f32)
+    for start in range(0, channels, block):
+        wide = feat_ref[:, start : start + block].astype(f32) * style[:, start : start + block]
+        scaled_t[start : start + block] = wide.astype(bf16).astype(f32).T.astype(bf16)
+        for tap in range(0, KTAPS, 2):
+            taps = min(2, KTAPS - tap)
+            result = jnp.dot(
+                scaled_t[start : start + block],
+                shifted[:, tap * cols : (tap + taps) * cols],
+                preferred_element_type=f32,
+            )
+            for own in range(taps):
+                first = (tap + own) * channels + start
+                part = result[:, own * cols : (own + 1) * cols]
+                product[first : first + block] = part
+                weighted = part * weight_ref[first : first + block].astype(f32)
+                demod_grad = demod_grad + jnp.sum(weighted.reshape(-1, 8, cols), axis=0)
+    demod_grad = jnp.sum(demod_grad, axis=0, keepdims=True) / demodulate
+    square_grad = -0.5 * demodulate * demodulate * demodulate * demod_grad
+
+    demod_part = lax.dot_general(
+        jnp.broadcast_to(square_grad, (8, cols)),
+        square[...],
+        (((1,), (1,)), ((), ())),
+        precision=highest,
+        preferred_element_type=f32,
+    )[:1]
+    style_rows = []
+    for start in range(0, channels, block):
+        kernel = jnp.concatenate(
+            [
+                weight_ref[tap * channels + start : tap * channels + start + block]
+                for tap in range(KTAPS)
+            ],
+            axis=1,
+        )
+        inner = lax.dot_general(
+            shifted[...], kernel, (((1,), (1,)), ((), ())), preferred_element_type=f32
+        )
+        total = jnp.sum(inner * feat_ref[:, start : start + block].astype(f32), axis=0, keepdims=True)
+        total = total + 2.0 * style[:, start : start + block] * demod_part[:, start : start + block]
+        for own in range(block // cols):
+            inner_ref[start // cols + own] = inner[:, own * cols : (own + 1) * cols]
+            style_rows.append(total[:, own * cols : (own + 1) * cols])
+    tile = jnp.concatenate(
+        style_rows + [jnp.broadcast_to(source_ref[...], (8, cols))], axis=0
+    )
+    for peer in range(tile_ref.shape[0]):
+        tile_ref[peer] = tile
+
+    for start in range(0, channels, LANES):
+        columns = jnp.broadcast_to(style_sq[:1, start : start + LANES], (LANES, LANES)).T
+        factor[start : start + LANES] = columns * (2.0 * square_grad)
+
+    def emit(even_ref, odd_ref):
+        total = KTAPS * channels
+        first = 0
+        while first < total:
+            chunk, at = divmod(first, rows_dev)
+            source = first % channels
+            size = min(rows_dev - at, channels - source)
+            target = odd_ref if chunk % 2 else even_ref
+            target[chunk // 2, at : at + size] = product[first : first + size] + weight_ref[
+                first : first + size
+            ].astype(f32) * factor[source : source + size]
+            first += size
+
+    @pl.when(core_ref[0] == 0)
+    def _():
+        emit(kept_ref, sent_ref)
+
+    @pl.when(core_ref[0] != 0)
+    def _():
+        emit(sent_ref, kept_ref)
+
+
+def convolution_part(core_id, features, styles, weight, grad_out, source, sizes):
+    chunks, rows_dev, peers = sizes
+    pixels, channels = features.shape
+    cols = grad_out.shape[1]
+    side = int(round(pixels**0.5))
+    f32 = jnp.float32
+    whole = pl.BlockSpec(memory_space=pltpu.VMEM)
+    tile_rows = channels // LANES + 8
+    return pl.pallas_call(
+        functools.partial(convolution_kernel, side),
+        out_shape=(
+            jax.ShapeDtypeStruct((chunks, rows_dev, cols), f32),
+            jax.ShapeDtypeStruct((chunks, rows_dev, cols), f32),
+            jax.ShapeDtypeStruct((channels // cols, pixels, cols), f32),
+            jax.ShapeDtypeStruct((peers, tile_rows, cols), f32),
+        ),
+        in_specs=[pl.BlockSpec(memory_space=pltpu.SMEM)] + [whole] * 5,
+        out_specs=[whole] * 4,
+        scratch_shapes=[
+            pltpu.VMEM((channels, pixels), jnp.bfloat16),
+            pltpu.VMEM((pixels, KTAPS * cols), jnp.bfloat16),
+            pltpu.VMEM((KTAPS * channels, cols), f32),
+            pltpu.VMEM((channels, cols), f32),
+            pltpu.VMEM((channels, cols), f32),
+        ],
+        compiler_params=pltpu.CompilerParams(vmem_limit_bytes=32 * 1024 * 1024),
+        cost_estimate=pl.CostEstimate(
+            flops=4 * pixels * KTAPS * channels * cols, transcendentals=0, bytes_accessed=12_000_000
+        ),
+        name="convolution_part",
+    )(core_id.astype(jnp.int32).reshape(1), features, styles, weight, grad_out, source)
 
 
 def doubled(rows, name, have):
@@ -62,64 +207,20 @@
     rows_z2 = doubled(own_rows, "z", 1)
     map_rows = exchange(map_weight.reshape(nchan, -1, cols_dev), "chan")
 
-    scaled = (features.astype(jnp.float32) * styles[:, None, None, :]).astype(jnp.bfloat16)
-    weight_sq = jnp.sum(jnp.square(conv_weight.astype(jnp.float32)), axis=0)
-    style_sq = styles * styles
-    demodulate = lax.rsqrt(jnp.dot(style_sq, weight_sq, precision=highest) + 1e-08)
-    padded = jnp.pad(scaled, ((0, 0), (1, 1), (1, 1), (0, 0)))
-    patches = jnp.concatenate(
-        [
-            tap_window(padded, tap // 3, tap % 3, side_len).reshape(pixels, channels)
-            for tap in range(KTAPS)
-        ],
-        axis=1,
-    )
-    weight_flat = conv_weight.reshape(KTAPS * channels, cols_dev)
-    conv_out = jnp.dot(patches, weight_flat, preferred_element_type=jnp.float32)
-    grad_wide = grad_out.astype(jnp.float32).reshape(pixels, cols_dev)
-    demod_grad = jnp.sum(grad_wide * conv_out, axis=0, keepdims=True)
-    square_grad = -0.5 * demodulate**3 * demod_grad
-    grad_scaled = (grad_wide * demodulate).astype(jnp.bfloat16)
-    grad_padded = jnp.pad(
-        grad_scaled.reshape(samples, side_len, side_len, cols_dev), ((0, 0), (1, 1), (1, 1), (0, 0))
-    )
-    inner_part = jnp.zeros((pixels, channels), jnp.float32)
-    for tap in range(KTAPS):
-        inner_part = inner_part + lax.dot_general(
-            tap_window(grad_padded, 2 - tap // 3, 2 - tap % 3, side_len).reshape(pixels, cols_dev),
-            conv_weight[tap],
-            (((1,), (1,)), ((), ())),
-            preferred_element_type=jnp.float32,
-        )
-    style_part = jnp.sum(
-        inner_part * features.reshape(pixels, channels).astype(jnp.float32), axis=0
-    ) + (2.0 * styles * jnp.dot(square_grad, weight_sq.T, precision=highest)).reshape(channels)
-
-    inner_part = inner_part.reshape(pixels, nchan, cols_dev).transpose(1, 0, 2)
-
-    style_factor = jnp.dot(style_sq.T, square_grad, precision=highest)
-    product_rows = lax.dot_general(
-        patches, grad_scaled, (((0,), (0,)), ((), ())), preferred_element_type=jnp.float32
-    ) + 2.0 * weight_flat.astype(jnp.float32) * jnp.tile(style_factor, (KTAPS, 1))
+    core_id = lax.axis_index("core")
     source = jnp.where(crossover <= LAYER, partner, dp_id).astype(jnp.float32)
-    tile = jnp.concatenate(
-        [
-            style_part.reshape(-1, LANES),
-            jnp.broadcast_to(source[:, None], (8, LANES)),
-        ],
-        axis=0,
-    )
-    tile, map_rows, rows_z2 = lax.optimization_barrier((tile, map_rows, rows_z2))
-    parts = exchange(
-        jnp.broadcast_to(tile[None], (ncore * nchan,) + tile.shape), ("core", "chan")
-    ).reshape(ncore, nchan, -1, LANES)
-    pieces = product_rows.reshape(nx, nz, ncore, rows_dev, cols_dev)
-    core_id = lax.axis_index("core")
-    coming = lax.ppermute(
-        lax.dynamic_index_in_dim(pieces, ncore - 1 - core_id, 2, keepdims=False),
-        "core",
-        [(core, ncore - 1 - core) for core in range(ncore)],
-    )
+    sent, kept, inner_part, tile = convolution_part(
+        core_id,
+        features.reshape(pixels, channels),
+        styles,
+        conv_weight.reshape(KTAPS * channels, cols_dev),
+        grad_out.reshape(pixels, cols_dev),
+        jnp.broadcast_to(source[:, None], (1, cols_dev)),
+        (nx * nz, rows_dev, ncore * nchan),
+    )
+    tile, sent, map_rows, rows_z2 = lax.optimization_barrier((tile, sent, map_rows, rows_z2))
+    parts = exchange(tile, ("core", "chan")).reshape(ncore, nchan, -1, LANES)
+    coming = lax.ppermute(sent, "core", [(core, ncore - 1 - core) for core in range(ncore)])
     rows_z4 = doubled(rows_z2, "z", 2)
     style_grad = jnp.sum(parts[:, :, :-8], axis=1)
     hidden_rows = jnp.sum(
@@ -140,7 +241,7 @@
     coming, riders, rows_z4, inner_part = lax.optimization_barrier(
         (coming, riders, rows_z4, inner_part)
     )
-    pieces = lax.dynamic_index_in_dim(pieces, core_id, 2, keepdims=False) + coming
+    pieces = kept + coming
     moved = exchange(
         jnp.concatenate(
             [
@@ -173,6 +274,8 @@
     moved = exchange(
         jnp.concatenate([pieces, jnp.broadcast_to(riders[None], (nz,) + riders.shape)], axis=1), "z"
     )
+    inner_half = halved(inner_half, 2)
+    inner_half, rows_z = lax.optimization_barrier((inner_half, rows_z))
     gathered = doubled(rows_z, "core", 1)
     have = 1
     while have < nx:
@@ -186,7 +289,7 @@
         for name, back in (("x", back_x), ("z", back_z), ("core", back_core))
     ]
     row_ids = ((spots[0] * nz + spots[1]) * ncore + spots[2]).astype(jnp.float32)
-    bit = 2
+    bit = 4
     while bit < nchan:
         inner_half = halved(inner_half, bit)
         bit *= 2

time: 172 us -> 143 us (0.83)
  matrix products: 19.4 us -> 4.66 us
  local copies, waits for them, and re-layouts: 22.7 us -> 8.77 us
  other arithmetic: 17.5 us -> 11.6 us
  Pallas kernels: 0 us -> 4.31 us
  waiting for transfers between devices: 39.4 us -> 42.1 us
    dot_general x13 -> x0, matrix products: 14.7 us -> none  [the longest x1 7.39 us: local(): lax.dot_general(patches, grad_scaled, (((0,), (0,)), ((), ())), preferred...]
    ppermute x7, waiting for transfers between devices: 15.1 us -> 27.3 us  [doubled(): lax.ppermute(rows[:extra * per], name, [(sender, (sender + have) % size)...]
    ppermute x3, waiting for transfers between devices: 15.4 us -> 5.2 us  [halved(): lax.ppermute(lax.dynamic_index_in_dim(pairs, 1 - side, 1, keepdims=False)...]
    unnamed x36 -> x32, local copies, waits for them, and re-layouts: 13.2 us -> 6.42 us
    mul x2 -> x0, other arithmetic: 5.22 us -> none  [the longest x1 4.45 us: local(): 2.0 * weight_flat.astype(jnp.float32) * jnp.tile(style_factor, (KTAPS, 1))]
    pallas_call x0 -> x1, Pallas kernels: none -> 4.31 us  [convolution_part(): pl.pallas_call(functools.partial(convolution_kernel, side), out_shape=(ja...]
    squeeze x1 -> x0, local copies, waits for them, and re-layouts: 3.23 us -> none  [local(): lax.dynamic_index_in_dim(pieces, ncore - 1 - core_id, 2, keepdims=False)]
    ppermute x7, starting transfers between devices: 25.3 us -> 22.7 us  [doubled(): lax.ppermute(rows[:extra * per], name, [(sender, (sender + have) % size)...]
  transfers between devices with their start and end apart: 15 -> 15, of which waited for: 6 -> 6; matrix products, arithmetic and copies ran while one was open for 28% -> 8% of each run, Pallas kernels for 0% -> 3%
where the time goes in v6:
time: 143 us; the launch traced here: 142 us
  starting transfers between devices  67.8 us (47%)
  waiting for transfers between devices  42.1 us (29%)
  other arithmetic  11.6 us (8%)
  local copies, waits for them, and re-layouts  8.77 us (6%)
  matrix products  4.66 us (3%)
  Pallas kernels  4.31 us (3%)
  between operations  2.39 us (2%)
    ppermute x7, waiting for transfers between devices, doubled(): lax.ppermute(rows[:extra * per], name, [(sender, (sender + have) % size)...  27.3 us
    all_to_all x4, starting transfers between devices, exchange(): return lax.all_to_all(blocks, axes, 0, 0, tiled=True)  24.3 us
    ppermute x7, starting transfers between devices, doubled(): lax.ppermute(rows[:extra * per], name, [(sender, (sender + have) % size)...  22.7 us
    ppermute x3, starting transfers between devices, halved(): lax.ppermute(lax.dynamic_index_in_dim(pairs, 1 - side, 1, keepdims=False)...  13.9 us
    all_to_all x4, waiting for transfers between devices, exchange(): return lax.all_to_all(blocks, axes, 0, 0, tiled=True)  9.61 us
    ppermute x1, starting transfers between devices, local(): lax.ppermute(sent, 'core', [(core, ncore - 1 - core) for core in range(nc...  6.83 us
    unnamed x32, local copies, waits for them, and re-layouts  6.42 us
    ppermute x3, waiting for transfers between devices, halved(): lax.ppermute(lax.dynamic_index_in_dim(pairs, 1 - side, 1, keepdims=False)...  5.2 us
  transfers between devices with their start and end apart: 15, of which 6 were waited for; matrix products, arithmetic and copies ran while one was open for 8% of the time, Pallas kernels for 3%

profile of v6, /device:TPU:1, one launch (start us, length us, event | category | flops | bytes accessed | tf_op | source)
XLA Modules:
  0.0 141.7 jit_solution(5709270414981936699)
XLA Ops:
  0.6 7.7 %all-to-all-start = ((f32[8,128,128]{2,1,0:T(8,128)}), f32[8,128,128]{2,1,0:T(8,128)}, u32[]{:S(2)}, u32[]{:S(2)}) async-start(f32[8,128,128]{2,1,0:T(8,128)} %bitcast.64), calls=%async_computation | async-start | bytes 1048576 | tf_op jit(solution)/shard_map/all_to_all | solution.py:189
  9.1 4.0 %collective-permute-start = (f32[1,16,128]{2,1,0:T(8,128)S(1)}, f32[1,16,128]{2,1,0:T(8,128)S(1)}, u32[]{:S(2)}, u32[]{:S(2)}) collective-permute-start(f32[1,16,128]{2,1,0:T(8,128)S(1)} %pad_maximum_fusion.8), channel_id=1, source_target_pairs={{0,16},{16,32},{32,48},{48,64},{64,80},{80,96},{96,112},{112,128},... | collective-permute-start | bytes 24584 | tf_op jit(solution)/shard_map/ppermute | solution.py:171
  14.4 1.7 %copy-done = bf16[9,1024,128]{2,1,0:T(8,128)(2,1)S(1)} copy-done((bf16[9,1024,128]{2,1,0:T(8,128)(2,1)S(1)}, bf16[9,1024,128]{2,1,0:T(8,128)(2,1)}, u32[]{:S(2)}) %copy-start) | copy-done | bytes 2359320
  16.1 1.0 copy-done.2
  18.6 4.3 %convolution_part.1 = (f32[48,96,128]{2,1,0:T(8,128)S(1)}, f32[48,96,128]{2,1,0:T(8,128)S(1)}, f32[8,256,128]{2,1,0:T(8,128)S(1)}, f32[16,16,128]{2,1,0:T(8,128)}) custom-call(s32[1]{0:T(128)} %bitcast.core_ref, bf16[256,1024]{1,0:T(8,128)(2,1)S(1)} %bitcast.55, f32[1,1024]{1,0:T(1,128)S(1)} %copy-done.4, bf16[9216,128]{1,0:T(8,128)(2,1)S(1)} %bitcast.54, ...), custom_call_target="tpu_custom_call" | custom-call | flops 1207959552 | bytes 12000000 | tf_op jit(solution)/shard_map/convolution_part/pallas_call | solution.py:142
  22.9 1.4 %copy-done.1 = f32[48,96,128]{2,1,0:T(8,128)} copy-done((f32[48,96,128]{2,1,0:T(8,128)}, f32[48,96,128]{2,1,0:T(8,128)S(1)}, u32[]{:S(2)}) %copy-start.1) | copy-done | bytes 2359320
  24.4 6.8 %collective-permute-start.1 = (f32[48,96,128]{2,1,0:T(8,128)}, f32[48,96,128]{2,1,0:T(8,128)}, u32[]{:S(2)}, u32[]{:S(2)}) collective-permute-start(f32[48,96,128]{2,1,0:T(8,128)} %copy-done.1), channel_id=1, source_target_pairs={{0,8},{8,0},{1,9},{9,1},{2,10},{10,2},{3,11},{11,3},{4,12},{12,4},... | collective-permute-start | bytes 7077896 | tf_op jit(solution)/shard_map/ppermute | solution.py:223
  31.2 7.2 %all-to-all-start.1 = ((f32[16,16,128]{2,1,0:T(8,128)}), f32[16,16,128]{2,1,0:T(8,128)S(1)}, u32[]{:S(2)}, u32[]{:S(2)}) async-start(f32[16,16,128]{2,1,0:T(8,128)} %get-tuple-element.26), calls=%async_computation.1 | async-start | bytes 262144 | tf_op jit(solution)/shard_map/all_to_all | solution.py:189
  38.5 2.2 %collective-permute-start.2 = (f32[2,16,128]{2,1,0:T(8,128)S(1)}, f32[2,16,128]{2,1,0:T(8,128)}, u32[]{:S(2)}, u32[]{:S(2)}) collective-permute-start(f32[2,16,128]{2,1,0:T(8,128)S(1)} %pad_maximum_fusion.6), channel_id=1, source_target_pairs={{0,32},{16,48},{32,64},{48,80},{64,96},{80,112},{96,128},{112,144}... | collective-permute-start | bytes 49160 | tf_op jit(solution)/shard_map/ppermute | solution.py:171
  41.3 8.2 %collective-permute-done.2 = f32[2,16,128]{2,1,0:T(8,128)} collective-permute-done((f32[2,16,128]{2,1,0:T(8,128)S(1)}, f32[2,16,128]{2,1,0:T(8,128)}, u32[]{:S(2)}, u32[]{:S(2)}) %collective-permute-start.2) | collective-permute-done | bytes 16416 | tf_op jit(solution)/shard_map/ppermute | solution.py:171
  49.5 1.3 pad_maximum_fusion.5
  50.9 1.5 %convolution_bitcast_fusion = f32[2,128]{1,0:T(2,128)S(1)} fusion(f32[8,128,128]{2,1,0:T(8,128)} %all-to-all-done, f32[2,8,128]{2,1,0:T(8,128)S(1)} %slice_reduce_fusion.2), kind=kOutput, calls=%fused_computation.5 | convolution fusion | flops 3145728 | bytes 533504 | tf_op jit(solution)/shard_map/dot_general | solution.py:227
  53.2 2.0 %add.94 = f32[48,96,128]{2,1,0:T(8,128)S(1)} add(f32[48,96,128]{2,1,0:T(8,128)S(1)} %get-tuple-element.22, f32[48,96,128]{2,1,0:T(8,128)} %collective-permute-done.1) | non-fusion elementwise | flops 589824 | bytes 7077888 | tf_op jit(solution)/shard_map/add | solution.py:244
  55.2 1.6 %pad_maximum_fusion = f32[4,1160,128]{2,1,0:T(8,128)} fusion(f32[4,8,128]{2,1,0:T(8,128)S(1)} %broadcast_in_dim.40, f32[4,1152,128]{2,1,0:T(8,128)S(1)} %bitcast.57), kind=kLoop, calls=%fused_computation | loop fusion | flops 593920 | bytes 4751360 | tf_op jit(solution)/shard_map/concatenate | solution.py:246
  56.8 4.1 %all-to-all-start.2 = ((f32[4,1160,128]{2,1,0:T(8,128)}), f32[4,1160,128]{2,1,0:T(8,128)S(1)}, u32[]{:S(2)}, u32[]{:S(2)}) async-start(f32[4,1160,128]{2,1,0:T(8,128)} %pad_maximum_fusion), calls=%async_computation.2 | async-start | bytes 4751360 | tf_op jit(solution)/shard_map/all_to_all | solution.py:189
  61.8 3.3 %collective-permute-start.5 = (f32[4,256,128]{2,1,0:T(8,128)}, f32[4,256,128]{2,1,0:T(8,128)}, u32[]{:S(2)}, u32[]{:S(2)}) collective-permute-start(f32[4,256,128]{2,1,0:T(8,128)} %dynamic-slice_bitcast_fusion), channel_id=1, source_target_pairs={{0,1},{1,0},{2,3},{3,2},{4,5},{5,4},{6,7},{7,6},{8,9},{9,8},{10,11... | collective-permute-start | bytes 1572872 | tf_op jit(solution)/shard_map/ppermute | solution.py:180
  65.1 3.0 %collective-permute-start.3 = (f32[4,16,128]{2,1,0:T(8,128)S(1)}, f32[4,16,128]{2,1,0:T(8,128)S(1)}, u32[]{:S(2)}, u32[]{:S(2)}) collective-permute-start(f32[4,16,128]{2,1,0:T(8,128)S(1)} %copy-done.7), channel_id=1, source_target_pairs={{0,64},{16,80},{32,96},{48,112},{64,128},{80,144},{96,160},{112,17... | collective-permute-start | bytes 98312 | tf_op jit(solution)/shard_map/ppermute | solution.py:171
  68.1 6.2 %collective-permute-start.4 = (f32[4,16,128]{2,1,0:T(8,128)S(1)}, f32[4,16,128]{2,1,0:T(8,128)}, u32[]{:S(2)}, u32[]{:S(2)}) collective-permute-start(f32[4,16,128]{2,1,0:T(8,128)S(1)} %copy-done.7), channel_id=1, source_target_pairs={{0,128},{16,144},{32,160},{48,176},{64,0},{80,16},{96,32},{112,48}... | collective-permute-start | bytes 98312 | tf_op jit(solution)/shard_map/ppermute | solution.py:171
  75.0 1.8 %collective-permute-done.4 = f32[4,16,128]{2,1,0:T(8,128)} collective-permute-done((f32[4,16,128]{2,1,0:T(8,128)S(1)}, f32[4,16,128]{2,1,0:T(8,128)}, u32[]{:S(2)}, u32[]{:S(2)}) %collective-permute-start.4) | collective-permute-done | bytes 32800 | tf_op jit(solution)/shard_map/ppermute | solution.py:171
  77.6 1.9 %bitcast_add_fusion = f32[4,256,128]{2,1,0:T(8,128)} fusion(f32[4,256,128]{2,1,0:T(8,128)} %collective-permute-done.5, f32[4,2,256,128]{3,2,1,0:T(8,128)S(1)} %bitcast.53, s32[]{:T(128)S(6)} %select_n.80), kind=kLoop, calls=%fused_computation.8 | loop fusion | flops 131072 | bytes 1572868 | tf_op jit(solution)/shard_map/add | solution.py:185
  79.5 9.6 %all-to-all-done.2 = f32[4,1160,128]{2,1,0:T(8,128)S(1)} async-done(((f32[4,1160,128]{2,1,0:T(8,128)}), f32[4,1160,128]{2,1,0:T(8,128)S(1)}, u32[]{:S(2)}, u32[]{:S(2)}) %all-to-all-start.2) | async-done | bytes 2375712 | tf_op jit(solution)/shard_map/all_to_all | solution.py:189
  89.3 3.9 %collective-permute-start.6 = (f32[2,256,128]{2,1,0:T(8,128)S(1)}, f32[2,256,128]{2,1,0:T(8,128)S(1)}, u32[]{:S(2)}, u32[]{:S(2)}) collective-permute-start(f32[2,256,128]{2,1,0:T(8,128)S(1)} %dynamic-slice_bitcast_fusion.1), channel_id=1, source_target_pairs={{0,2},{1,3},{2,0},{3,1},{4,6},{5,7},{6,4},{7,5},{8,10},{9,11},{10,... | collective-permute-start | bytes 786440 | tf_op jit(solution)/shard_map/ppermute | solution.py:180
  94.1 5.3 %all-to-all-start.3 = ((f32[12,120,128]{2,1,0:T(8,128)}), f32[12,120,128]{2,1,0:T(8,128)S(1)}, u32[]{:S(2)}, u32[]{:S(2)}) async-start(f32[12,120,128]{2,1,0:T(8,128)} %pad_maximum_fusion.1), calls=%async_computation.3 | async-start | bytes 1474560 | tf_op jit(solution)/shard_map/all_to_all | solution.py:189
  100.1 5.2 %collective-permute-done.6 = f32[2,256,128]{2,1,0:T(8,128)S(1)} collective-permute-done((f32[2,256,128]{2,1,0:T(8,128)S(1)}, f32[2,256,128]{2,1,0:T(8,128)S(1)}, u32[]{:S(2)}, u32[]{:S(2)}) %collective-permute-start.6) | collective-permute-done | bytes 262176 | tf_op jit(solution)/shard_map/ppermute | solution.py:180
  105.4 3.1 %collective-permute-start.8 = (f32[12,16,128]{2,1,0:T(8,128)S(1)}, f32[12,16,128]{2,1,0:T(8,128)S(1)}, u32[]{:S(2)}, u32[]{:S(2)}) collective-permute-start(f32[12,16,128]{2,1,0:T(8,128)S(1)} %pad_maximum_fusion.4), channel_id=1, source_target_pairs={{0,8},{8,0},{1,9},{9,1},{2,10},{10,2},{3,11},{11,3},{4,12},{12,4},... | collective-permute-start | bytes 294920 | tf_op jit(solution)/shard_map/ppermute | solution.py:171
  108.5 6.8 %collective-permute-start.7 = (f32[1,256,128]{2,1,0:T(8,128)S(1)}, f32[1,256,128]{2,1,0:T(8,128)S(1)}, u32[]{:S(2)}, u32[]{:S(2)}) collective-permute-start(f32[1,256,128]{2,1,0:T(8,128)S(1)} %constant_dynamic-slice_fusion.1), channel_id=1, source_target_pairs={{0,4},{1,5},{2,6},{3,7},{4,0},{5,1},{6,2},{7,3},{8,12},{9,13},{10,... | collective-permute-start | bytes 393224 | tf_op jit(solution)/shard_map/ppermute | solution.py:180
  115.3 2.2 %collective-permute-start.9 = (f32[24,16,128]{2,1,0:T(8,128)S(1)}, f32[24,16,128]{2,1,0:T(8,128)S(1)}, u32[]{:S(2)}, u32[]{:S(2)}) collective-permute-start(f32[24,16,128]{2,1,0:T(8,128)S(1)} %pad_maximum_fusion.3), channel_id=1, source_target_pairs={{0,192},{192,384},{384,576},{576,0},{1,193},{193,385},{385,577},{5... | collective-permute-start | bytes 589832 | tf_op jit(solution)/shard_map/ppermute | solution.py:171
  117.6 7.1 %collective-permute-done.9 = f32[24,16,128]{2,1,0:T(8,128)S(1)} collective-permute-done((f32[24,16,128]{2,1,0:T(8,128)S(1)}, f32[24,16,128]{2,1,0:T(8,128)S(1)}, u32[]{:S(2)}, u32[]{:S(2)}) %collective-permute-start.9) | collective-permute-done | bytes 196640 | tf_op jit(solution)/shard_map/ppermute | solution.py:171
  124.7 1.9 %collective-permute-start.10 = (f32[48,16,128]{2,1,0:T(8,128)S(1)}, f32[48,16,128]{2,1,0:T(8,128)S(1)}, u32[]{:S(2)}, u32[]{:S(2)}) collective-permute-start(f32[48,16,128]{2,1,0:T(8,128)S(1)} %pad_maximum_fusion.2), channel_id=1, source_target_pairs={{0,384},{192,576},{384,0},{576,192},{1,385},{193,577},{385,1},{577... | collective-permute-start | bytes 1179656 | tf_op jit(solution)/shard_map/ppermute | solution.py:171
  127.3 10.3 %collective-permute-done.10 = f32[48,16,128]{2,1,0:T(8,128)S(1)} collective-permute-done((f32[48,16,128]{2,1,0:T(8,128)S(1)}, f32[48,16,128]{2,1,0:T(8,128)S(1)}, u32[]{:S(2)}, u32[]{:S(2)}) %collective-permute-start.10) | collective-permute-done | bytes 393248 | tf_op jit(solution)/shard_map/ppermute | solution.py:171
  138.2 1.4 convolution_multiply_fusion.1
  140.3 1.4 convolution_multiply_fusion
  (71 shorter events, 9.8 us)
Async XLA Ops:
  0.6 23.8 %all-to-all-start = ((f32[8,128,128]{2,1,0:T(8,128)}), f32[8,128,128]{2,1,0:T(8,128)}, u32[]{:S(2)}, u32[]{:S(2)}) async-start(f32[8,128,128]{2,1,0:T(8,128)} %bitcast.64), calls=%async_computation | async-start | bytes 1048576 | tf_op jit(solution)/shard_map/all_to_all | solution.py:189
  8.3 16.1 %copy-start.9 = (f32[1,1024]{1,0:T(1,128)S(1)}, f32[1,1024]{1,0:T(1,128)}, u32[]{:S(2)}) copy-start(f32[1,1024]{1,0:T(1,128)} %param.19) | copy-start | bytes 12292
  8.3 16.1 %copy-start.10 = (f32[1,1024]{1,0:T(1,128)S(1)}, f32[1,1024]{1,0:T(1,128)}, u32[]{:S(2)}) copy-start(f32[1,1024]{1,0:T(1,128)} %param.18) | copy-start | bytes 12292
  9.1 15.3 %collective-permute-start = (f32[1,16,128]{2,1,0:T(8,128)S(1)}, f32[1,16,128]{2,1,0:T(8,128)S(1)}, u32[]{:S(2)}, u32[]{:S(2)}) collective-permute-start(f32[1,16,128]{2,1,0:T(8,128)S(1)} %pad_maximum_fusion.8), channel_id=1, source_target_pairs={{0,16},{16,32},{32,48},{48,64},{64,80},{80,96},{96,112},{112,128},... | collective-permute-start | bytes 24584 | tf_op jit(solution)/shard_map/ppermute | solution.py:171
  14.4 1.7 %copy-start = (bf16[9,1024,128]{2,1,0:T(8,128)(2,1)S(1)}, bf16[9,1024,128]{2,1,0:T(8,128)(2,1)}, u32[]{:S(2)}) copy-start(bf16[9,1024,128]{2,1,0:T(8,128)(2,1)} %param.14) | copy-start | bytes 7077892
  16.1 1.0 copy-start.2
  17.1 0.8 copy-start.3
  17.9 0.7 copy-start.4
  22.9 1.4 %copy-start.1 = (f32[48,96,128]{2,1,0:T(8,128)}, f32[48,96,128]{2,1,0:T(8,128)S(1)}, u32[]{:S(2)}) copy-start(f32[48,96,128]{2,1,0:T(8,128)S(1)} %get-tuple-element.25) | copy-start | bytes 7077892
  24.4 28.8 %collective-permute-start.1 = (f32[48,96,128]{2,1,0:T(8,128)}, f32[48,96,128]{2,1,0:T(8,128)}, u32[]{:S(2)}, u32[]{:S(2)}) collective-permute-start(f32[48,96,128]{2,1,0:T(8,128)} %copy-done.1), channel_id=1, source_target_pairs={{0,8},{8,0},{1,9},{9,1},{2,10},{10,2},{3,11},{11,3},{4,12},{12,4},... | collective-permute-start | bytes 7077896 | tf_op jit(solution)/shard_map/ppermute | solution.py:223
  31.2 19.6 %all-to-all-start.1 = ((f32[16,16,128]{2,1,0:T(8,128)}), f32[16,16,128]{2,1,0:T(8,128)S(1)}, u32[]{:S(2)}, u32[]{:S(2)}) async-start(f32[16,16,128]{2,1,0:T(8,128)} %get-tuple-element.26), calls=%async_computation.1 | async-start | bytes 262144 | tf_op jit(solution)/shard_map/all_to_all | solution.py:189
  38.5 11.0 %collective-permute-start.2 = (f32[2,16,128]{2,1,0:T(8,128)S(1)}, f32[2,16,128]{2,1,0:T(8,128)}, u32[]{:S(2)}, u32[]{:S(2)}) collective-permute-start(f32[2,16,128]{2,1,0:T(8,128)S(1)} %pad_maximum_fusion.6), channel_id=1, source_target_pairs={{0,32},{16,48},{32,64},{48,80},{64,96},{80,112},{96,128},{112,144}... | collective-permute-start | bytes 49160 | tf_op jit(solution)/shard_map/ppermute | solution.py:171
  56.8 8.3 %copy-start.7 = (f32[4,16,128]{2,1,0:T(8,128)S(1)}, f32[4,16,128]{2,1,0:T(8,128)}, u32[]{:S(2)}) copy-start(f32[4,16,128]{2,1,0:T(8,128)} %pad_maximum_fusion.5) | copy-start | bytes 98308
  56.8 32.2 %all-to-all-start.2 = ((f32[4,1160,128]{2,1,0:T(8,128)}), f32[4,1160,128]{2,1,0:T(8,128)S(1)}, u32[]{:S(2)}, u32[]{:S(2)}) async-start(f32[4,1160,128]{2,1,0:T(8,128)} %pad_maximum_fusion), calls=%async_computation.2 | async-start | bytes 4751360 | tf_op jit(solution)/shard_map/all_to_all | solution.py:189
  61.8 15.8 %collective-permute-start.5 = (f32[4,256,128]{2,1,0:T(8,128)}, f32[4,256,128]{2,1,0:T(8,128)}, u32[]{:S(2)}, u32[]{:S(2)}) collective-permute-start(f32[4,256,128]{2,1,0:T(8,128)} %dynamic-slice_bitcast_fusion), channel_id=1, source_target_pairs={{0,1},{1,0},{2,3},{3,2},{4,5},{5,4},{6,7},{7,6},{8,9},{9,8},{10,11... | collective-permute-start | bytes 1572872 | tf_op jit(solution)/shard_map/ppermute | solution.py:180
  65.1 9.3 %collective-permute-start.3 = (f32[4,16,128]{2,1,0:T(8,128)S(1)}, f32[4,16,128]{2,1,0:T(8,128)S(1)}, u32[]{:S(2)}, u32[]{:S(2)}) collective-permute-start(f32[4,16,128]{2,1,0:T(8,128)S(1)} %copy-done.7), channel_id=1, source_target_pairs={{0,64},{16,80},{32,96},{48,112},{64,128},{80,144},{96,160},{112,17... | collective-permute-start | bytes 98312 | tf_op jit(solution)/shard_map/ppermute | solution.py:171
  68.1 8.7 %collective-permute-start.4 = (f32[4,16,128]{2,1,0:T(8,128)S(1)}, f32[4,16,128]{2,1,0:T(8,128)}, u32[]{:S(2)}, u32[]{:S(2)}) collective-permute-start(f32[4,16,128]{2,1,0:T(8,128)S(1)} %copy-done.7), channel_id=1, source_target_pairs={{0,128},{16,144},{32,160},{48,176},{64,0},{80,16},{96,32},{112,48}... | collective-permute-start | bytes 98312 | tf_op jit(solution)/shard_map/ppermute | solution.py:171
  74.4 0.6 copy-start.8
  79.5 9.8 %copy-start.5 = (f32[4,256,128]{2,1,0:T(8,128)S(1)}, f32[4,256,128]{2,1,0:T(8,128)}, u32[]{:S(2)}) copy-start(f32[4,256,128]{2,1,0:T(8,128)} %bitcast_add_fusion) | copy-start | bytes 1572868
  89.2 10.9 %copy-start.11 = (s32[96]{0:T(128)S(1)}, s32[96]{0:T(128)}, u32[]{:S(2)}) copy-start(s32[96]{0:T(128)} %constant.158) | copy-start | bytes 1156
  89.2 10.9 %copy-start.12 = (s32[96]{0:T(128)S(1)}, s32[96]{0:T(128)}, u32[]{:S(2)}) copy-start(s32[96]{0:T(128)} %constant.159) | copy-start | bytes 1156
  89.2 10.9 %copy-start.13 = (s32[96]{0:T(128)S(1)}, s32[96]{0:T(128)}, u32[]{:S(2)}) copy-start(s32[96]{0:T(128)} %constant.160) | copy-start | bytes 1156
  89.2 16.1 %copy-start.6 = (f32[4,256,128]{2,1,0:T(8,128)S(1)}, f32[4,256,128]{2,1,0:T(8,128)}, u32[]{:S(2)}) copy-start(f32[4,256,128]{2,1,0:T(8,128)} %bitcast_add_fusion) | copy-start | bytes 1572868
  89.3 16.0 %collective-permute-start.6 = (f32[2,256,128]{2,1,0:T(8,128)S(1)}, f32[2,256,128]{2,1,0:T(8,128)S(1)}, u32[]{:S(2)}, u32[]{:S(2)}) collective-permute-start(f32[2,256,128]{2,1,0:T(8,128)S(1)} %dynamic-slice_bitcast_fusion.1), channel_id=1, source_target_pairs={{0,2},{1,3},{2,0},{3,1},{4,6},{5,7},{6,4},{7,5},{8,10},{9,11},{10,... | collective-permute-start | bytes 786440 | tf_op jit(solution)/shard_map/ppermute | solution.py:180
  94.1 43.6 %all-to-all-start.3 = ((f32[12,120,128]{2,1,0:T(8,128)}), f32[12,120,128]{2,1,0:T(8,128)S(1)}, u32[]{:S(2)}, u32[]{:S(2)}) async-start(f32[12,120,128]{2,1,0:T(8,128)} %pad_maximum_fusion.1), calls=%async_computation.3 | async-start | bytes 1474560 | tf_op jit(solution)/shard_map/all_to_all | solution.py:189
  105.4 10.0 %collective-permute-start.8 = (f32[12,16,128]{2,1,0:T(8,128)S(1)}, f32[12,16,128]{2,1,0:T(8,128)S(1)}, u32[]{:S(2)}, u32[]{:S(2)}) collective-permute-start(f32[12,16,128]{2,1,0:T(8,128)S(1)} %pad_maximum_fusion.4), channel_id=1, source_target_pairs={{0,8},{8,0},{1,9},{9,1},{2,10},{10,2},{3,11},{11,3},{4,12},{12,4},... | collective-permute-start | bytes 294920 | tf_op jit(solution)/shard_map/ppermute | solution.py:171
  108.5 18.1 %collective-permute-start.7 = (f32[1,256,128]{2,1,0:T(8,128)S(1)}, f32[1,256,128]{2,1,0:T(8,128)S(1)}, u32[]{:S(2)}, u32[]{:S(2)}) collective-permute-start(f32[1,256,128]{2,1,0:T(8,128)S(1)} %constant_dynamic-slice_fusion.1), channel_id=1, source_target_pairs={{0,4},{1,5},{2,6},{3,7},{4,0},{5,1},{6,2},{7,3},{8,12},{9,13},{10,... | collective-permute-start | bytes 393224 | tf_op jit(solution)/shard_map/ppermute | solution.py:180
  115.3 9.3 %collective-permute-start.9 = (f32[24,16,128]{2,1,0:T(8,128)S(1)}, f32[24,16,128]{2,1,0:T(8,128)S(1)}, u32[]{:S(2)}, u32[]{:S(2)}) collective-permute-start(f32[24,16,128]{2,1,0:T(8,128)S(1)} %pad_maximum_fusion.3), channel_id=1, source_target_pairs={{0,192},{192,384},{384,576},{576,0},{1,193},{193,385},{385,577},{5... | collective-permute-start | bytes 589832 | tf_op jit(solution)/shard_map/ppermute | solution.py:171
  124.7 12.9 %collective-permute-start.10 = (f32[48,16,128]{2,1,0:T(8,128)S(1)}, f32[48,16,128]{2,1,0:T(8,128)S(1)}, u32[]{:S(2)}, u32[]{:S(2)}) collective-permute-start(f32[48,16,128]{2,1,0:T(8,128)S(1)} %pad_maximum_fusion.2), channel_id=1, source_target_pairs={{0,384},{192,576},{384,0},{576,192},{1,385},{193,577},{385,1},{577... | collective-permute-start | bytes 1179656 | tf_op jit(solution)/shard_map/ppermute | solution.py:171

commit v7 on v6

--- a/solution.py
+++ b/solution.py
@@ -20,15 +20,37 @@
 
 
 def convolution_kernel(
-    side, core_ref, feat_ref, style_ref, weight_ref, grad_ref, source_ref,
-    sent_ref, kept_ref, inner_ref, tile_ref,
-    scaled_t, shifted, product, square, factor,
+    side, rows_dev, core_ref, feat_hbm, style_hbm, weight_hbm, grad_hbm, source_ref,
+    sent_hbm, kept_ref, inner_ref, tile_ref,
+    feat_ref, style_ref, weight_ref, grad_ref, sent_ref,
+    scaled_t, shifted, product, square, factor, in_sems, out_sems,
 ):
     pixels, channels = feat_ref.shape
     cols = grad_ref.shape[1]
     block = min(256, channels)
-    rows_dev = sent_ref.shape[1]
     f32, bf16 = jnp.float32, jnp.bfloat16
+
+    arrivals = [
+        pltpu.make_async_copy(source, target, in_sems.at[at])
+        for at, (source, target) in enumerate(
+            (
+                (style_hbm, style_ref),
+                (feat_hbm, feat_ref),
+                (weight_hbm, weight_ref),
+                (grad_hbm, grad_ref),
+            )
+        )
+    ]
+    for arrival in arrivals:
+        arrival.start()
+    arrivals[0].wait()
+    arrivals[1].wait()
+    style = style_ref[...]
+    for start in range(0, channels, block):
+        wide = feat_ref[:, start : start + block].astype(f32) * style[:, start : start + block]
+        scaled_t[start : start + block] = wide.astype(bf16).astype(f32).T.astype(bf16)
+    arrivals[2].wait()
+    arrivals[3].wait()
 
     for start in range(0, channels, LANES):
         total = jnp.zeros((LANES, cols), f32)
@@ -36,7 +58,6 @@
             wide = weight_ref[tap * channels + start : tap * channels + start + LANES].astype(f32)
             total = total + wide * wide
         square[start : start + LANES] = total
-    style = style_ref[...]
     style_sq = jnp.broadcast_to(style * style, (8, channels))
     norm = jnp.dot(style_sq, square[...], precision=highest, preferred_element_type=f32)
     demodulate = lax.rsqrt(norm[:1] + 1e-08)
@@ -57,8 +78,6 @@
 
     demod_grad = jnp.zeros((8, cols), f32)
     for start in range(0, channels, block):
-        wide = feat_ref[:, start : start + block].astype(f32) * style[:, start : start + block]
-        scaled_t[start : start + block] = wide.astype(bf16).astype(f32).T.astype(bf16)
         for tap in range(0, KTAPS, 2):
             taps = min(2, KTAPS - tap)
             result = jnp.dot(
@@ -109,6 +128,17 @@
         columns = jnp.broadcast_to(style_sq[:1, start : start + LANES], (LANES, LANES)).T
         factor[start : start + LANES] = columns * (2.0 * square_grad)
 
+    per_row = sent_ref.shape[1] // rows_dev
+    for row in range(sent_ref.shape[0]):
+        for target in (sent_ref, kept_ref):
+            target[row, per_row * rows_dev :] = jnp.zeros((8, cols), f32)
+
+    ncore = 2
+    departures = [
+        pltpu.make_async_copy(sent_ref.at[row], sent_hbm.at[row], out_sems.at[row])
+        for row in range(sent_ref.shape[0])
+    ]
+
     def emit(even_ref, odd_ref):
         total = KTAPS * channels
         first = 0
@@ -117,10 +147,16 @@
             source = first % channels
             size = min(rows_dev - at, channels - source)
             target = odd_ref if chunk % 2 else even_ref
-            target[chunk // 2, at : at + size] = product[first : first + size] + weight_ref[
+            row, place = divmod(chunk // 2, per_row)
+            at += place * rows_dev
+            target[row, at : at + size] = product[first : first + size] + weight_ref[
                 first : first + size
             ].astype(f32) * factor[source : source + size]
             first += size
+            if first % (ncore * per_row * rows_dev) == 0:
+                departures[row].start()
+        for departure in departures:
+            departure.wait()
 
     @pl.when(core_ref[0] == 0)
     def _():
@@ -132,36 +168,51 @@
 
 
 def convolution_part(core_id, features, styles, weight, grad_out, source, sizes):
-    chunks, rows_dev, peers = sizes
+    far, near, rows_dev, peers = sizes
     pixels, channels = features.shape
     cols = grad_out.shape[1]
     side = int(round(pixels**0.5))
     f32 = jnp.float32
     whole = pl.BlockSpec(memory_space=pltpu.VMEM)
+    away = pl.BlockSpec(memory_space=pltpu.HBM)
     tile_rows = channels // LANES + 8
     return pl.pallas_call(
-        functools.partial(convolution_kernel, side),
+        functools.partial(convolution_kernel, side, rows_dev),
         out_shape=(
-            jax.ShapeDtypeStruct((chunks, rows_dev, cols), f32),
-            jax.ShapeDtypeStruct((chunks, rows_dev, cols), f32),
+            pltpu.HBM((far, near * rows_dev + 8, cols), f32),
+            jax.ShapeDtypeStruct((far, near * rows_dev + 8, cols), f32),
             jax.ShapeDtypeStruct((channels // cols, pixels, cols), f32),
             jax.ShapeDtypeStruct((peers, tile_rows, cols), f32),
         ),
-        in_specs=[pl.BlockSpec(memory_space=pltpu.SMEM)] + [whole] * 5,
-        out_specs=[whole] * 4,
+        in_specs=[pl.BlockSpec(memory_space=pltpu.SMEM)] + [away] * 4 + [whole],
+        out_specs=[away] + [whole] * 3,
         scratch_shapes=[
+            pltpu.VMEM((pixels, channels), jnp.bfloat16),
+            pltpu.VMEM((1, channels), f32),
+            pltpu.VMEM((KTAPS * channels, cols), jnp.bfloat16),
+            pltpu.VMEM((pixels, cols), jnp.bfloat16),
+            pltpu.VMEM((far, near * rows_dev + 8, cols), f32),
             pltpu.VMEM((channels, pixels), jnp.bfloat16),
             pltpu.VMEM((pixels, KTAPS * cols), jnp.bfloat16),
             pltpu.VMEM((KTAPS * channels, cols), f32),
             pltpu.VMEM((channels, cols), f32),
             pltpu.VMEM((channels, cols), f32),
+            pltpu.SemaphoreType.DMA((4,)),
+            pltpu.SemaphoreType.DMA((far,)),
         ],
         compiler_params=pltpu.CompilerParams(vmem_limit_bytes=32 * 1024 * 1024),
         cost_estimate=pl.CostEstimate(
             flops=4 * pixels * KTAPS * channels * cols, transcendentals=0, bytes_accessed=12_000_000
         ),
         name="convolution_part",
-    )(core_id.astype(jnp.int32).reshape(1), features, styles, weight, grad_out, source)
+    )(
+        core_id.astype(jnp.int32).reshape(1),
+        *(
+            pltpu.with_memory_space_constraint(one, pltpu.HBM)
+            for one in (features, styles, weight, grad_out)
+        ),
+        source,
+    )
 
 
 def doubled(rows, name, have):
@@ -216,12 +267,12 @@
         conv_weight.reshape(KTAPS * channels, cols_dev),
         grad_out.reshape(pixels, cols_dev),
         jnp.broadcast_to(source[:, None], (1, cols_dev)),
-        (nx * nz, rows_dev, ncore * nchan),
+        (nx, nz, rows_dev, ncore * nchan),
     )
     tile, sent, map_rows, rows_z2 = lax.optimization_barrier((tile, sent, map_rows, rows_z2))
     parts = exchange(tile, ("core", "chan")).reshape(ncore, nchan, -1, LANES)
     coming = lax.ppermute(sent, "core", [(core, ncore - 1 - core) for core in range(ncore)])
-    rows_z4 = doubled(rows_z2, "z", 2)
+    inner_half = halved(inner_part, 1)
     style_grad = jnp.sum(parts[:, :, :-8], axis=1)
     hidden_rows = jnp.sum(
         lax.dot_general(
@@ -238,26 +289,21 @@
     riders = jnp.concatenate(
         [style_rows, hidden_rows, parts[:, 0, -1], jnp.zeros((8 - 3 * ncore, cols_dev))], axis=0
     )
-    coming, riders, rows_z4, inner_part = lax.optimization_barrier(
-        (coming, riders, rows_z4, inner_part)
-    )
-    pieces = kept + coming
+    coming, riders, rows_z2 = lax.optimization_barrier((coming, riders, rows_z2))
     moved = exchange(
-        jnp.concatenate(
-            [
-                pieces.reshape(nx, nz * rows_dev, cols_dev),
-                jnp.broadcast_to(riders[None], (nx,) + riders.shape),
-            ],
-            axis=1,
+        kept
+        + coming
+        + jnp.pad(
+            jnp.broadcast_to(riders[None], (nx,) + riders.shape),
+            ((0, 0), (nz * rows_dev, 0), (0, 0)),
         ),
         "x",
     )
-    inner_half = halved(inner_part, 1)
-    have = 4
-    rows_z = rows_z4
+    rows_z, have = rows_z2, 2
     while have < nz:
         rows_z = doubled(rows_z, "z", have)
         have = min(2 * have, nz)
+    gathered = doubled(rows_z, "core", 1)
     pieces = jnp.sum(moved[:, : nz * rows_dev], axis=0).reshape(nz, rows_dev, cols_dev)
     riders = jnp.concatenate(
         [
@@ -268,19 +314,20 @@
         ],
         axis=0,
     )
-    pieces, riders, rows_z, inner_half = lax.optimization_barrier(
-        (pieces, riders, rows_z, inner_half)
+    pieces, riders, gathered, inner_half = lax.optimization_barrier(
+        (pieces, riders, gathered, inner_half)
     )
     moved = exchange(
         jnp.concatenate([pieces, jnp.broadcast_to(riders[None], (nz,) + riders.shape)], axis=1), "z"
     )
-    inner_half = halved(inner_half, 2)
-    inner_half, rows_z = lax.optimization_barrier((inner_half, rows_z))
-    gathered = doubled(rows_z, "core", 1)
-    have = 1
-    while have < nx:
-        gathered = doubled(gathered, "x", have)
-        have *= 2
+    gathered = jnp.concatenate(
+        [gathered]
+        + [
+            lax.ppermute(gathered, "x", [(sender, (sender + hop) % nx) for sender in range(nx)])
+            for hop in range(1, nx)
+        ],
+        axis=0,
+    )
     back_x, back_core, back_z = np.meshgrid(
         np.arange(nx), np.arange(ncore), np.arange(nz), indexing="ij"
     )
@@ -289,7 +336,7 @@
         for name, back in (("x", back_x), ("z", back_z), ("core", back_core))
     ]
     row_ids = ((spots[0] * nz + spots[1]) * ncore + spots[2]).astype(jnp.float32)
-    bit = 4
+    bit = 2
     while bit < nchan:
         inner_half = halved(inner_half, bit)
         bit *= 2

time: 143 us -> 142 us (level)
  Pallas kernels: 4.31 us -> 6.9 us
  local copies, waits for them, and re-layouts: 8.77 us -> 6.52 us
  other arithmetic: 11.6 us -> 9.79 us
  waiting for transfers between devices: 42.1 us -> 43.9 us
    ppermute x7 -> x5, waiting for transfers between devices: 27.3 us -> 15.6 us  [doubled(): lax.ppermute(rows[:extra * per], name, [(sender, (sender + have) % size)...]
    ppermute x3, waiting for transfers between devices: 5.2 us -> 15.4 us  [halved(): lax.ppermute(lax.dynamic_index_in_dim(pairs, 1 - side, 1, keepdims=False)...]
    ppermute x0 -> x3, starting transfers between devices: none -> 9.83 us  [local(): lax.ppermute(gathered, 'x', [(sender, (sender + hop) % nx) for sender in...]
    ppermute x0 -> x3, waiting for transfers between devices: none -> 6.21 us  [local(): lax.ppermute(gathered, 'x', [(sender, (sender + hop) % nx) for sender in...]
    ppermute x3, starting transfers between devices: 13.9 us -> 8.71 us  [halved(): lax.ppermute(lax.dynamic_index_in_dim(pairs, 1 - side, 1, keepdims=False)...]
    unnamed x32 -> x21, local copies, waits for them, and re-layouts: 6.42 us -> 2.93 us
    all_to_all x4, starting transfers between devices: 24.3 us -> 21 us  [exchange(): return lax.all_to_all(blocks, axes, 0, 0, tiled=True)]
    all_to_all x4, waiting for transfers between devices: 9.61 us -> 6.71 us  [exchange(): return lax.all_to_all(blocks, axes, 0, 0, tiled=True)]
  transfers between devices with their start and end apart: 15 -> 16, of which waited for: 6 -> 7; matrix products, arithmetic and copies ran while one was open for 8% -> 9% of each run, Pallas kernels for 3% -> 5%
where the time goes in v7:
time: 142 us; the launch traced here: 141 us
  starting transfers between devices  66.5 us (47%)
  waiting for transfers between devices  43.9 us (31%)
  other arithmetic  9.79 us (7%)
  Pallas kernels  6.9 us (5%)
  local copies, waits for them, and re-layouts  6.52 us (5%)
  matrix products  4.64 us (3%)
  between operations  2.38 us (2%)
    ppermute x5, starting transfers between devices, doubled(): lax.ppermute(rows[:extra * per], name, [(sender, (sender + have) % size)...  21.4 us
    all_to_all x4, starting transfers between devices, exchange(): return lax.all_to_all(blocks, axes, 0, 0, tiled=True)  21 us
    ppermute x5, waiting for transfers between devices, doubled(): lax.ppermute(rows[:extra * per], name, [(sender, (sender + have) % size)...  15.6 us
    ppermute x3, waiting for transfers between devices, halved(): lax.ppermute(lax.dynamic_index_in_dim(pairs, 1 - side, 1, keepdims=False)...  15.4 us
    ppermute x3, starting transfers between devices, local(): lax.ppermute(gathered, 'x', [(sender, (sender + hop) % nx) for sender in...  9.83 us
    ppermute x3, starting transfers between devices, halved(): lax.ppermute(lax.dynamic_index_in_dim(pairs, 1 - side, 1, keepdims=False)...  8.71 us
    pallas_call x1, Pallas kernels, convolution_part(): pl.pallas_call(functools.partial(convolution_kernel, side, rows_dev), out...  6.9 us
    all_to_all x4, waiting for transfers between devices, exchange(): return lax.all_to_all(blocks, axes, 0, 0, tiled=True)  6.71 us
  transfers between devices with their start and end apart: 16, of which 7 were waited for; matrix products, arithmetic and copies ran while one was open for 9% of the time, Pallas kernels for 5%

profile of v7, /device:TPU:1, one launch (start us, length us, event | category | flops | bytes accessed | tf_op | source)
XLA Modules:
  0.0 140.6 jit_solution(978126016037762664)
XLA Ops:
  0.6 7.7 %all-to-all-start = ((f32[8,128,128]{2,1,0:T(8,128)}), f32[8,128,128]{2,1,0:T(8,128)}, u32[]{:S(2)}, u32[]{:S(2)}) async-start(f32[8,128,128]{2,1,0:T(8,128)} %bitcast.59), calls=%async_computation | async-start | bytes 1048576 | tf_op jit(solution)/shard_map/all_to_all | solution.py:240
  9.1 4.0 %collective-permute-start = (f32[1,16,128]{2,1,0:T(8,128)S(1)}, f32[1,16,128]{2,1,0:T(8,128)S(1)}, u32[]{:S(2)}, u32[]{:S(2)}) collective-permute-start(f32[1,16,128]{2,1,0:T(8,128)S(1)} %pad_maximum_fusion.4), channel_id=1, source_target_pairs={{0,16},{16,32},{32,48},{48,64},{64,80},{80,96},{96,112},{112,128},... | collective-permute-start | bytes 24584 | tf_op jit(solution)/shard_map/ppermute | solution.py:222
  14.4 6.9 %convolution_part.1 = (f32[4,1160,128]{2,1,0:T(8,128)}, f32[4,1160,128]{2,1,0:T(8,128)S(1)}, f32[8,256,128]{2,1,0:T(8,128)S(1)}, f32[16,16,128]{2,1,0:T(8,128)}) custom-call(s32[1]{0:T(128)} %bitcast.core_ref, bf16[256,1024]{1,0:T(8,128)(2,1)} %bitcast.74, f32[1,1024]{1,0:T(1,128)} %style_hbm.1, bf16[9216,128]{1,0:T(8,128)(2,1)} %bitcast.73, ...), custom_call_target="tpu_custom_call" | custom-call | flops 1207959552 | bytes 12000000 | tf_op jit(solution)/shard_map/convolution_part/pallas_call | solution.py:179
  21.3 3.1 %collective-permute-done = f32[1,16,128]{2,1,0:T(8,128)S(1)} collective-permute-done((f32[1,16,128]{2,1,0:T(8,128)S(1)}, f32[1,16,128]{2,1,0:T(8,128)S(1)}, u32[]{:S(2)}, u32[]{:S(2)}) %collective-permute-start) | collective-permute-done | bytes 8224 | tf_op jit(solution)/shard_map/ppermute | solution.py:222
  25.0 5.5 %collective-permute-start.1 = (f32[4,1160,128]{2,1,0:T(8,128)}, f32[4,1160,128]{2,1,0:T(8,128)}, u32[]{:S(2)}, u32[]{:S(2)}) collective-permute-start(f32[4,1160,128]{2,1,0:T(8,128)} %get-tuple-element.22), channel_id=1, source_target_pairs={{0,8},{8,0},{1,9},{9,1},{2,10},{10,2},{3,11},{11,3},{4,12},{12,4},... | collective-permute-start | bytes 7127048 | tf_op jit(solution)/shard_map/ppermute | solution.py:274
  30.5 5.6 %all-to-all-start.1 = ((f32[16,16,128]{2,1,0:T(8,128)}), f32[16,16,128]{2,1,0:T(8,128)S(1)}, u32[]{:S(2)}, u32[]{:S(2)}) async-start(f32[16,16,128]{2,1,0:T(8,128)} %get-tuple-element.23), calls=%async_computation.1 | async-start | bytes 262144 | tf_op jit(solution)/shard_map/all_to_all | solution.py:240
  36.7 6.7 %all-to-all-done.1 = f32[16,16,128]{2,1,0:T(8,128)S(1)} async-done(((f32[16,16,128]{2,1,0:T(8,128)}), f32[16,16,128]{2,1,0:T(8,128)S(1)}, u32[]{:S(2)}, u32[]{:S(2)}) %all-to-all-start.1) | async-done | bytes 131104 | tf_op jit(solution)/shard_map/all_to_all | solution.py:240
  43.4 1.6 %convolution_bitcast_fusion = f32[2,128]{1,0:T(2,128)S(1)} fusion(f32[8,128,128]{2,1,0:T(8,128)} %all-to-all-done, f32[2,8,128]{2,1,0:T(8,128)S(1)} %slice_reduce_fusion.2), kind=kOutput, calls=%fused_computation.5 | convolution fusion | flops 3145728 | bytes 533504 | tf_op jit(solution)/shard_map/dot_general | solution.py:278
  45.7 3.4 %pad_add_fusion = f32[4,1160,128]{2,1,0:T(8,128)} fusion(f32[4,8,128]{2,1,0:T(8,128)S(1)} %broadcast_in_dim.40, f32[4,1160,128]{2,1,0:T(8,128)S(1)} %get-tuple-element.19, f32[4,1160,128]{2,1,0:T(8,128)} %collective-permute-done.1), kind=kLoop, calls=%fused_computation | loop fusion | flops 1187840 | bytes 7143424 | tf_op jit(solution)/shard_map/add | solution.py:294
  49.1 4.1 %all-to-all-start.2 = ((f32[4,1160,128]{2,1,0:T(8,128)}), f32[4,1160,128]{2,1,0:T(8,128)S(1)}, u32[]{:S(2)}, u32[]{:S(2)}) async-start(f32[4,1160,128]{2,1,0:T(8,128)} %pad_add_fusion), calls=%async_computation.2 | async-start | bytes 4751360 | tf_op jit(solution)/shard_map/all_to_all | solution.py:240
  53.2 0.8 dynamic-slice_bitcast_fusion
  54.0 3.4 %collective-permute-start.6 = (f32[4,256,128]{2,1,0:T(8,128)}, f32[4,256,128]{2,1,0:T(8,128)}, u32[]{:S(2)}, u32[]{:S(2)}) collective-permute-start(f32[4,256,128]{2,1,0:T(8,128)} %dynamic-slice_bitcast_fusion), channel_id=1, source_target_pairs={{0,1},{1,0},{2,3},{3,2},{4,5},{5,4},{6,7},{7,6},{8,9},{9,8},{10,11... | collective-permute-start | bytes 1572872 | tf_op jit(solution)/shard_map/ppermute | solution.py:231
  57.5 2.1 %collective-permute-start.2 = (f32[2,16,128]{2,1,0:T(8,128)S(1)}, f32[2,16,128]{2,1,0:T(8,128)S(1)}, u32[]{:S(2)}, u32[]{:S(2)}) collective-permute-start(f32[2,16,128]{2,1,0:T(8,128)S(1)} %copy-done.1), channel_id=1, source_target_pairs={{0,32},{16,48},{32,64},{48,80},{64,96},{80,112},{96,128},{112,144}... | collective-permute-start | bytes 49160 | tf_op jit(solution)/shard_map/ppermute | solution.py:222
  60.2 8.7 %collective-permute-done.2 = f32[2,16,128]{2,1,0:T(8,128)S(1)} collective-permute-done((f32[2,16,128]{2,1,0:T(8,128)S(1)}, f32[2,16,128]{2,1,0:T(8,128)S(1)}, u32[]{:S(2)}, u32[]{:S(2)}) %collective-permute-start.2) | collective-permute-done | bytes 16416 | tf_op jit(solution)/shard_map/ppermute | solution.py:222
  69.6 5.6 %collective-permute-start.4 = (f32[4,16,128]{2,1,0:T(8,128)S(1)}, f32[4,16,128]{2,1,0:T(8,128)S(1)}, u32[]{:S(2)}, u32[]{:S(2)}) collective-permute-start(f32[4,16,128]{2,1,0:T(8,128)S(1)} %get-tuple-element.42), channel_id=1, source_target_pairs={{0,128},{16,144},{32,160},{48,176},{64,0},{80,16},{96,32},{112,48}... | collective-permute-start | bytes 98312 | tf_op jit(solution)/shard_map/ppermute | solution.py:222
  75.2 3.6 %collective-permute-start.3 = (f32[4,16,128]{2,1,0:T(8,128)S(1)}, f32[4,16,128]{2,1,0:T(8,128)S(1)}, u32[]{:S(2)}, u32[]{:S(2)}) collective-permute-start(f32[4,16,128]{2,1,0:T(8,128)S(1)} %get-tuple-element.42), channel_id=1, source_target_pairs={{0,64},{16,80},{32,96},{48,112},{64,128},{80,144},{96,160},{112,17... | collective-permute-start | bytes 98312 | tf_op jit(solution)/shard_map/ppermute | solution.py:222
  78.8 1.9 %bitcast_add_fusion = f32[4,256,128]{2,1,0:T(8,128)} fusion(f32[4,256,128]{2,1,0:T(8,128)} %collective-permute-done.6, f32[4,2,256,128]{3,2,1,0:T(8,128)S(1)} %bitcast.52, s32[]{:T(128)S(6)} %select_n.80), kind=kLoop, calls=%fused_computation.8 | loop fusion | flops 131072 | bytes 1572868 | tf_op jit(solution)/shard_map/add | solution.py:236
  80.7 3.8 %collective-permute-done.3 = f32[4,16,128]{2,1,0:T(8,128)S(1)} collective-permute-done((f32[4,16,128]{2,1,0:T(8,128)S(1)}, f32[4,16,128]{2,1,0:T(8,128)S(1)}, u32[]{:S(2)}, u32[]{:S(2)}) %collective-permute-start.3) | collective-permute-done | bytes 32800 | tf_op jit(solution)/shard_map/ppermute | solution.py:222
  84.5 6.1 %collective-permute-start.5 = (f32[12,16,128]{2,1,0:T(8,128)S(1)}, f32[12,16,128]{2,1,0:T(8,128)S(1)}, u32[]{:S(2)}, u32[]{:S(2)}) collective-permute-start(f32[12,16,128]{2,1,0:T(8,128)S(1)} %pad_maximum_fusion.1), channel_id=1, source_target_pairs={{0,8},{8,0},{1,9},{9,1},{2,10},{10,2},{3,11},{11,3},{4,12},{12,4},... | collective-permute-start | bytes 294920 | tf_op jit(solution)/shard_map/ppermute | solution.py:222
  92.7 0.9 pad_maximum_fusion
  93.6 3.6 %all-to-all-start.3 = ((f32[12,120,128]{2,1,0:T(8,128)}), f32[12,120,128]{2,1,0:T(8,128)S(1)}, u32[]{:S(2)}, u32[]{:S(2)}) async-start(f32[12,120,128]{2,1,0:T(8,128)} %pad_maximum_fusion), calls=%async_computation.3 | async-start | bytes 1474560 | tf_op jit(solution)/shard_map/all_to_all | solution.py:240
  98.0 4.9 %collective-permute-start.11 = (f32[24,16,128]{2,1,0:T(8,128)}, f32[24,16,128]{2,1,0:T(8,128)S(1)}, u32[]{:S(2)}, u32[]{:S(2)}) collective-permute-start(f32[24,16,128]{2,1,0:T(8,128)} %constant_dynamic-update-slice_fusion.2), channel_id=1, source_target_pairs={{0,576},{192,0},{384,192},{576,384},{1,577},{193,1},{385,193},{577... | collective-permute-start | bytes 589832 | tf_op jit(solution)/shard_map/ppermute | solution.py:326
  102.9 2.5 %collective-permute-start.10 = (f32[24,16,128]{2,1,0:T(8,128)}, f32[24,16,128]{2,1,0:T(8,128)S(1)}, u32[]{:S(2)}, u32[]{:S(2)}) collective-permute-start(f32[24,16,128]{2,1,0:T(8,128)} %constant_dynamic-update-slice_fusion.2), channel_id=1, source_target_pairs={{0,384},{192,576},{384,0},{576,192},{1,385},{193,577},{385,1},{577... | collective-permute-start | bytes 589832 | tf_op jit(solution)/shard_map/ppermute | solution.py:326
  105.4 2.5 %collective-permute-start.9 = (f32[24,16,128]{2,1,0:T(8,128)}, f32[24,16,128]{2,1,0:T(8,128)S(1)}, u32[]{:S(2)}, u32[]{:S(2)}) collective-permute-start(f32[24,16,128]{2,1,0:T(8,128)} %constant_dynamic-update-slice_fusion.2), channel_id=1, source_target_pairs={{0,192},{192,384},{384,576},{576,0},{1,193},{193,385},{385,577},{5... | collective-permute-start | bytes 589832 | tf_op jit(solution)/shard_map/ppermute | solution.py:326
  107.9 2.5 %collective-permute-start.7 = (f32[2,256,128]{2,1,0:T(8,128)S(1)}, f32[2,256,128]{2,1,0:T(8,128)S(1)}, u32[]{:S(2)}, u32[]{:S(2)}) collective-permute-start(f32[2,256,128]{2,1,0:T(8,128)S(1)} %dynamic-slice_bitcast_fusion.1), channel_id=1, source_target_pairs={{0,2},{1,3},{2,0},{3,1},{4,6},{5,7},{6,4},{7,5},{8,10},{9,11},{10,... | collective-permute-start | bytes 786440 | tf_op jit(solution)/shard_map/ppermute | solution.py:231
  110.4 0.9 constant_dynamic-update-slice_fusion.10
  111.3 6.2 %collective-permute-done.9 = f32[24,16,128]{2,1,0:T(8,128)S(1)} collective-permute-done((f32[24,16,128]{2,1,0:T(8,128)}, f32[24,16,128]{2,1,0:T(8,128)S(1)}, u32[]{:S(2)}, u32[]{:S(2)}) %collective-permute-start.9) | collective-permute-done | bytes 196640 | tf_op jit(solution)/shard_map/ppermute | solution.py:326
  117.6 6.7 %collective-permute-done.7 = f32[2,256,128]{2,1,0:T(8,128)S(1)} collective-permute-done((f32[2,256,128]{2,1,0:T(8,128)S(1)}, f32[2,256,128]{2,1,0:T(8,128)S(1)}, u32[]{:S(2)}, u32[]{:S(2)}) %collective-permute-start.7) | collective-permute-done | bytes 262176 | tf_op jit(solution)/shard_map/ppermute | solution.py:231
  124.4 2.8 %collective-permute-start.8 = (f32[1,256,128]{2,1,0:T(8,128)S(1)}, f32[1,256,128]{2,1,0:T(8,128)S(1)}, u32[]{:S(2)}, u32[]{:S(2)}) collective-permute-start(f32[1,256,128]{2,1,0:T(8,128)S(1)} %constant_dynamic-slice_fusion.1), channel_id=1, source_target_pairs={{0,4},{1,5},{2,6},{3,7},{4,0},{5,1},{6,2},{7,3},{8,12},{9,13},{10,... | collective-permute-start | bytes 393224 | tf_op jit(solution)/shard_map/ppermute | solution.py:231
  127.4 8.7 %collective-permute-done.8 = f32[1,256,128]{2,1,0:T(8,128)S(1)} collective-permute-done((f32[1,256,128]{2,1,0:T(8,128)S(1)}, f32[1,256,128]{2,1,0:T(8,128)S(1)}, u32[]{:S(2)}, u32[]{:S(2)}) %collective-permute-start.8) | collective-permute-done | bytes 131104 | tf_op jit(solution)/shard_map/ppermute | solution.py:231
  137.8 1.4 convolution_multiply_fusion.1
  139.2 1.4 convolution_multiply_fusion
  (60 shorter events, 8.7 us)
Async XLA Ops:
  0.6 24.4 %all-to-all-start = ((f32[8,128,128]{2,1,0:T(8,128)}), f32[8,128,128]{2,1,0:T(8,128)}, u32[]{:S(2)}, u32[]{:S(2)}) async-start(f32[8,128,128]{2,1,0:T(8,128)} %bitcast.59), calls=%async_computation | async-start | bytes 1048576 | tf_op jit(solution)/shard_map/all_to_all | solution.py:240
  8.3 16.1 %copy-start.2 = (f32[1,1024]{1,0:T(1,128)S(1)}, f32[1,1024]{1,0:T(1,128)}, u32[]{:S(2)}) copy-start(f32[1,1024]{1,0:T(1,128)} %param.19) | copy-start | bytes 12292
  8.3 16.1 %copy-start.3 = (f32[1,1024]{1,0:T(1,128)S(1)}, f32[1,1024]{1,0:T(1,128)}, u32[]{:S(2)}) copy-start(f32[1,1024]{1,0:T(1,128)} %param.18) | copy-start | bytes 12292
  9.1 15.3 %collective-permute-start = (f32[1,16,128]{2,1,0:T(8,128)S(1)}, f32[1,16,128]{2,1,0:T(8,128)S(1)}, u32[]{:S(2)}, u32[]{:S(2)}) collective-permute-start(f32[1,16,128]{2,1,0:T(8,128)S(1)} %pad_maximum_fusion.4), channel_id=1, source_target_pairs={{0,16},{16,32},{32,48},{48,64},{64,80},{80,96},{96,112},{112,128},... | collective-permute-start | bytes 24584 | tf_op jit(solution)/shard_map/ppermute | solution.py:222
  25.0 20.7 %collective-permute-start.1 = (f32[4,1160,128]{2,1,0:T(8,128)}, f32[4,1160,128]{2,1,0:T(8,128)}, u32[]{:S(2)}, u32[]{:S(2)}) collective-permute-start(f32[4,1160,128]{2,1,0:T(8,128)} %get-tuple-element.22), channel_id=1, source_target_pairs={{0,8},{8,0},{1,9},{9,1},{2,10},{10,2},{3,11},{11,3},{4,12},{12,4},... | collective-permute-start | bytes 7127048 | tf_op jit(solution)/shard_map/ppermute | solution.py:274
  30.5 12.9 %all-to-all-start.1 = ((f32[16,16,128]{2,1,0:T(8,128)}), f32[16,16,128]{2,1,0:T(8,128)S(1)}, u32[]{:S(2)}, u32[]{:S(2)}) async-start(f32[16,16,128]{2,1,0:T(8,128)} %get-tuple-element.23), calls=%async_computation.1 | async-start | bytes 262144 | tf_op jit(solution)/shard_map/all_to_all | solution.py:240
  49.1 8.4 %copy-start.1 = (f32[2,16,128]{2,1,0:T(8,128)S(1)}, f32[2,16,128]{2,1,0:T(8,128)}, u32[]{:S(2)}) copy-start(f32[2,16,128]{2,1,0:T(8,128)} %pad_maximum_fusion.2) | copy-start | bytes 49156
  49.1 43.4 %all-to-all-start.2 = ((f32[4,1160,128]{2,1,0:T(8,128)}), f32[4,1160,128]{2,1,0:T(8,128)S(1)}, u32[]{:S(2)}, u32[]{:S(2)}) async-start(f32[4,1160,128]{2,1,0:T(8,128)} %pad_add_fusion), calls=%async_computation.2 | async-start | bytes 4751360 | tf_op jit(solution)/shard_map/all_to_all | solution.py:240
  54.0 24.7 %collective-permute-start.6 = (f32[4,256,128]{2,1,0:T(8,128)}, f32[4,256,128]{2,1,0:T(8,128)}, u32[]{:S(2)}, u32[]{:S(2)}) collective-permute-start(f32[4,256,128]{2,1,0:T(8,128)} %dynamic-slice_bitcast_fusion), channel_id=1, source_target_pairs={{0,1},{1,0},{2,3},{3,2},{4,5},{5,4},{6,7},{7,6},{8,9},{9,8},{10,11... | collective-permute-start | bytes 1572872 | tf_op jit(solution)/shard_map/ppermute | solution.py:231
  57.5 11.5 %collective-permute-start.2 = (f32[2,16,128]{2,1,0:T(8,128)S(1)}, f32[2,16,128]{2,1,0:T(8,128)S(1)}, u32[]{:S(2)}, u32[]{:S(2)}) collective-permute-start(f32[2,16,128]{2,1,0:T(8,128)S(1)} %copy-done.1), channel_id=1, source_target_pairs={{0,32},{16,48},{32,64},{48,80},{64,96},{80,112},{96,128},{112,144}... | collective-permute-start | bytes 49160 | tf_op jit(solution)/shard_map/ppermute | solution.py:222
  69.6 11.1 %collective-permute-start.4 = (f32[4,16,128]{2,1,0:T(8,128)S(1)}, f32[4,16,128]{2,1,0:T(8,128)S(1)}, u32[]{:S(2)}, u32[]{:S(2)}) collective-permute-start(f32[4,16,128]{2,1,0:T(8,128)S(1)} %get-tuple-element.42), channel_id=1, source_target_pairs={{0,128},{16,144},{32,160},{48,176},{64,0},{80,16},{96,32},{112,48}... | collective-permute-start | bytes 98312 | tf_op jit(solution)/shard_map/ppermute | solution.py:222
  75.2 9.3 %collective-permute-start.3 = (f32[4,16,128]{2,1,0:T(8,128)S(1)}, f32[4,16,128]{2,1,0:T(8,128)S(1)}, u32[]{:S(2)}, u32[]{:S(2)}) collective-permute-start(f32[4,16,128]{2,1,0:T(8,128)S(1)} %get-tuple-element.42), channel_id=1, source_target_pairs={{0,64},{16,80},{32,96},{48,112},{64,128},{80,144},{96,160},{112,17... | collective-permute-start | bytes 98312 | tf_op jit(solution)/shard_map/ppermute | solution.py:222
  84.5 7.4 %collective-permute-start.5 = (f32[12,16,128]{2,1,0:T(8,128)S(1)}, f32[12,16,128]{2,1,0:T(8,128)S(1)}, u32[]{:S(2)}, u32[]{:S(2)}) collective-permute-start(f32[12,16,128]{2,1,0:T(8,128)S(1)} %pad_maximum_fusion.1), channel_id=1, source_target_pairs={{0,8},{8,0},{1,9},{9,1},{2,10},{10,2},{3,11},{11,3},{4,12},{12,4},... | collective-permute-start | bytes 294920 | tf_op jit(solution)/shard_map/ppermute | solution.py:222
  92.5 5.5 %copy-start.4 = (s32[96]{0:T(128)S(1)}, s32[96]{0:T(128)}, u32[]{:S(2)}) copy-start(s32[96]{0:T(128)} %constant.163) | copy-start | bytes 1156
  92.5 5.5 %copy-start.5 = (s32[96]{0:T(128)S(1)}, s32[96]{0:T(128)}, u32[]{:S(2)}) copy-start(s32[96]{0:T(128)} %constant.162) | copy-start | bytes 1156
  92.5 5.5 %copy-start.6 = (s32[96]{0:T(128)S(1)}, s32[96]{0:T(128)}, u32[]{:S(2)}) copy-start(s32[96]{0:T(128)} %constant.161) | copy-start | bytes 1156
  92.6 15.2 %copy-start = (f32[4,256,128]{2,1,0:T(8,128)S(1)}, f32[4,256,128]{2,1,0:T(8,128)}, u32[]{:S(2)}) copy-start(f32[4,256,128]{2,1,0:T(8,128)} %bitcast_add_fusion) | copy-start | bytes 1572868
  93.6 43.1 %all-to-all-start.3 = ((f32[12,120,128]{2,1,0:T(8,128)}), f32[12,120,128]{2,1,0:T(8,128)S(1)}, u32[]{:S(2)}, u32[]{:S(2)}) async-start(f32[12,120,128]{2,1,0:T(8,128)} %pad_maximum_fusion), calls=%async_computation.3 | async-start | bytes 1474560 | tf_op jit(solution)/shard_map/all_to_all | solution.py:240
  98.0 19.6 %collective-permute-start.11 = (f32[24,16,128]{2,1,0:T(8,128)}, f32[24,16,128]{2,1,0:T(8,128)S(1)}, u32[]{:S(2)}, u32[]{:S(2)}) collective-permute-start(f32[24,16,128]{2,1,0:T(8,128)} %constant_dynamic-update-slice_fusion.2), channel_id=1, source_target_pairs={{0,576},{192,0},{384,192},{576,384},{1,577},{193,1},{385,193},{577... | collective-permute-start | bytes 589832 | tf_op jit(solution)/shard_map/ppermute | solution.py:326
  102.9 14.7 %collective-permute-start.10 = (f32[24,16,128]{2,1,0:T(8,128)}, f32[24,16,128]{2,1,0:T(8,128)S(1)}, u32[]{:S(2)}, u32[]{:S(2)}) collective-permute-start(f32[24,16,128]{2,1,0:T(8,128)} %constant_dynamic-update-slice_fusion.2), channel_id=1, source_target_pairs={{0,384},{192,576},{384,0},{576,192},{1,385},{193,577},{385,1},{577... | collective-permute-start | bytes 589832 | tf_op jit(solution)/shard_map/ppermute | solution.py:326
  105.4 12.2 %collective-permute-start.9 = (f32[24,16,128]{2,1,0:T(8,128)}, f32[24,16,128]{2,1,0:T(8,128)S(1)}, u32[]{:S(2)}, u32[]{:S(2)}) collective-permute-start(f32[24,16,128]{2,1,0:T(8,128)} %constant_dynamic-update-slice_fusion.2), channel_id=1, source_target_pairs={{0,192},{192,384},{384,576},{576,0},{1,193},{193,385},{385,577},{5... | collective-permute-start | bytes 589832 | tf_op jit(solution)/shard_map/ppermute | solution.py:326
  107.9 16.4 %collective-permute-start.7 = (f32[2,256,128]{2,1,0:T(8,128)S(1)}, f32[2,256,128]{2,1,0:T(8,128)S(1)}, u32[]{:S(2)}, u32[]{:S(2)}) collective-permute-start(f32[2,256,128]{2,1,0:T(8,128)S(1)} %dynamic-slice_bitcast_fusion.1), channel_id=1, source_target_pairs={{0,2},{1,3},{2,0},{3,1},{4,6},{5,7},{6,4},{7,5},{8,10},{9,11},{10,... | collective-permute-start | bytes 786440 | tf_op jit(solution)/shard_map/ppermute | solution.py:231
  124.4 11.7 %collective-permute-start.8 = (f32[1,256,128]{2,1,0:T(8,128)S(1)}, f32[1,256,128]{2,1,0:T(8,128)S(1)}, u32[]{:S(2)}, u32[]{:S(2)}) collective-permute-start(f32[1,256,128]{2,1,0:T(8,128)S(1)} %constant_dynamic-slice_fusion.1), channel_id=1, source_target_pairs={{0,4},{1,5},{2,6},{3,7},{4,0},{5,1},{6,2},{7,3},{8,12},{9,13},{10,... | collective-permute-start | bytes 393224 | tf_op jit(solution)/shard_map/ppermute | solution.py:231

commit v8 on v7

--- a/solution.py
+++ b/solution.py
@@ -215,14 +215,16 @@
     )
 
 
-def doubled(rows, name, have):
+def gathered_from(rows, name, hops):
     size = lax.axis_size(name)
-    extra = min(have, size - have)
-    per = rows.shape[0] // have
-    coming = lax.ppermute(
-        rows[: extra * per], name, [(sender, (sender + have) % size) for sender in range(size)]
-    )
-    return jnp.concatenate([rows, coming], axis=0)
+    return jnp.concatenate(
+        [rows]
+        + [
+            lax.ppermute(rows, name, [(sender, (sender + hop) % size) for sender in range(size)])
+            for hop in hops
+        ],
+        axis=0,
+    )
 
 
 def halved(blocks, bit):
@@ -255,7 +257,7 @@
     own_rows = jnp.concatenate(
         [latents.reshape(1, -1, LANES), map_pre.reshape(1, -1, LANES)], axis=1
     )
-    rows_z2 = doubled(own_rows, "z", 1)
+    pair = gathered_from(own_rows, "core", (1,))
     map_rows = exchange(map_weight.reshape(nchan, -1, cols_dev), "chan")
 
     core_id = lax.axis_index("core")
@@ -269,7 +271,7 @@
         jnp.broadcast_to(source[:, None], (1, cols_dev)),
         (nx, nz, rows_dev, ncore * nchan),
     )
-    tile, sent, map_rows, rows_z2 = lax.optimization_barrier((tile, sent, map_rows, rows_z2))
+    tile, sent, map_rows, pair = lax.optimization_barrier((tile, sent, map_rows, pair))
     parts = exchange(tile, ("core", "chan")).reshape(ncore, nchan, -1, LANES)
     coming = lax.ppermute(sent, "core", [(core, ncore - 1 - core) for core in range(ncore)])
     inner_half = halved(inner_part, 1)
@@ -289,7 +291,8 @@
     riders = jnp.concatenate(
         [style_rows, hidden_rows, parts[:, 0, -1], jnp.zeros((8 - 3 * ncore, cols_dev))], axis=0
     )
-    coming, riders, rows_z2 = lax.optimization_barrier((coming, riders, rows_z2))
+    near = gathered_from(pair, "z", range(1, min(4, nz)))
+    coming, riders, near = lax.optimization_barrier((coming, riders, near))
     moved = exchange(
         kept
         + coming
@@ -299,11 +302,7 @@
         ),
         "x",
     )
-    rows_z, have = rows_z2, 2
-    while have < nz:
-        rows_z = doubled(rows_z, "z", have)
-        have = min(2 * have, nz)
-    gathered = doubled(rows_z, "core", 1)
+    gathered = gathered_from(near, "z", range(4, nz, 4))
     pieces = jnp.sum(moved[:, : nz * rows_dev], axis=0).reshape(nz, rows_dev, cols_dev)
     riders = jnp.concatenate(
         [
@@ -320,28 +319,26 @@
     moved = exchange(
         jnp.concatenate([pieces, jnp.broadcast_to(riders[None], (nz,) + riders.shape)], axis=1), "z"
     )
-    gathered = jnp.concatenate(
-        [gathered]
-        + [
-            lax.ppermute(gathered, "x", [(sender, (sender + hop) % nx) for sender in range(nx)])
-            for hop in range(1, nx)
-        ],
-        axis=0,
-    )
-    back_x, back_core, back_z = np.meshgrid(
-        np.arange(nx), np.arange(ncore), np.arange(nz), indexing="ij"
+    gathered = gathered_from(gathered, "x", range(1, nx))
+    back_x, back_z, back_core = np.meshgrid(
+        np.arange(nx), np.arange(nz), np.arange(ncore), indexing="ij"
     )
     spots = [
         (lax.axis_index(name) + lax.axis_size(name) - back.reshape(-1)) % lax.axis_size(name)
         for name, back in (("x", back_x), ("z", back_z), ("core", back_core))
     ]
     row_ids = ((spots[0] * nz + spots[1]) * ncore + spots[2]).astype(jnp.float32)
-    bit = 2
-    while bit < nchan:
-        inner_half = halved(inner_half, bit)
-        bit *= 2
+    group = inner_half.shape[0]
+    place = chan_id // 2
+    grad_inner = lax.dynamic_index_in_dim(inner_half, place, 0, keepdims=False)
+    for flip in range(1, group):
+        grad_inner = grad_inner + lax.ppermute(
+            lax.dynamic_index_in_dim(inner_half, place ^ flip, 0, keepdims=False),
+            "chan",
+            [(sender, sender ^ (2 * flip)) for sender in range(nchan)],
+        )
     style_cols = lax.dynamic_slice_in_dim(styles, chan_id * cols_dev, cols_dev, 1)
-    grad_input = (inner_half[0] * style_cols).astype(jnp.bfloat16)
+    grad_input = (grad_inner * style_cols).astype(jnp.bfloat16)
     grad_weight = jnp.sum(moved[:, :rows_dev], axis=0) / batch_size
 
     per = nx * ncore

time: 142 us -> 136 us (0.958)
  the two profiles are of different devices: /device:TPU:1 before, /device:TPU:8 now
where the time goes in v8:
time: 136 us; the launch traced here: 135 us
  starting transfers between devices  85.4 us (63%)
  waiting for transfers between devices  21.7 us (16%)
  other arithmetic  11.1 us (8%)
  Pallas kernels  6.89 us (5%)
  matrix products  4.64 us (3%)
  local copies, waits for them, and re-layouts  2.5 us (2%)
  between operations  2.42 us (2%)
    ppermute x9, starting transfers between devices, gathered_from(): lax.ppermute(rows, name, [(sender, (sender + hop) % size) for sender in r...  35.2 us
    all_to_all x4, starting transfers between devices, exchange(): return lax.all_to_all(blocks, axes, 0, 0, tiled=True)  33.4 us
    ppermute x3, starting transfers between devices, local(): lax.ppermute(lax.dynamic_index_in_dim(inner_half, place ^ flip, 0, keepdi...  12.2 us
    ppermute x9, waiting for transfers between devices, gathered_from(): lax.ppermute(rows, name, [(sender, (sender + hop) % size) for sender in r...  11.8 us
    all_to_all x4, waiting for transfers between devices, exchange(): return lax.all_to_all(blocks, axes, 0, 0, tiled=True)  7.63 us
    pallas_call x1, Pallas kernels, convolution_part(): pl.pallas_call(functools.partial(convolution_kernel, side, rows_dev), out...  6.89 us
    add x1, other arithmetic, local(): kept + coming  3.35 us
  transfers between devices with their start and end apart: 18, of which 5 were waited for; matrix products, arithmetic and copies ran while one was open for 7% of the time, Pallas kernels for 5%

profile of v8, /device:TPU:8, one launch (start us, length us, event | category | flops | bytes accessed | tf_op | source)
XLA Modules:
  0.0 134.6 jit_solution(16419226508982232292)
XLA Ops:
  0.6 13.5 %all-to-all-start = ((f32[8,128,128]{2,1,0:T(8,128)}), f32[8,128,128]{2,1,0:T(8,128)}, u32[]{:S(2)}, u32[]{:S(2)}) async-start(f32[8,128,128]{2,1,0:T(8,128)} %bitcast.68), calls=%async_computation | async-start | bytes 1048576 | tf_op jit(solution)/shard_map/all_to_all | solution.py:242
  14.9 1.9 %collective-permute-start = (f32[1,16,128]{2,1,0:T(8,128)S(1)}, f32[1,16,128]{2,1,0:T(8,128)S(1)}, u32[]{:S(2)}, u32[]{:S(2)}) collective-permute-start(f32[1,16,128]{2,1,0:T(8,128)S(1)} %pad_maximum_fusion.5), channel_id=1, source_target_pairs={{0,8},{8,0},{1,9},{9,1},{2,10},{10,2},{3,11},{11,3},{4,12},{12,4},... | collective-permute-start | bytes 24584 | tf_op jit(solution)/shard_map/ppermute | solution.py:223
  18.1 6.9 %convolution_part.1 = (f32[4,1160,128]{2,1,0:T(8,128)}, f32[4,1160,128]{2,1,0:T(8,128)S(1)}, f32[8,256,128]{2,1,0:T(8,128)S(1)}, f32[16,16,128]{2,1,0:T(8,128)}) custom-call(s32[1]{0:T(128)} %bitcast.core_ref, bf16[256,1024]{1,0:T(8,128)(2,1)} %bitcast.83, f32[1,1024]{1,0:T(1,128)} %style_hbm.1, bf16[9216,128]{1,0:T(8,128)(2,1)} %bitcast.82, ...), custom_call_target="tpu_custom_call" | custom-call | flops 1207959552 | bytes 12000000 | tf_op jit(solution)/shard_map/convolution_part/pallas_call | solution.py:179
  25.7 2.4 %collective-permute-start.1 = (f32[4,1160,128]{2,1,0:T(8,128)}, f32[4,1160,128]{2,1,0:T(8,128)}, u32[]{:S(2)}, u32[]{:S(2)}) collective-permute-start(f32[4,1160,128]{2,1,0:T(8,128)} %get-tuple-element.22), channel_id=1, source_target_pairs={{0,8},{8,0},{1,9},{9,1},{2,10},{10,2},{3,11},{11,3},{4,12},{12,4},... | collective-permute-start | bytes 7127048 | tf_op jit(solution)/shard_map/ppermute | solution.py:276
  28.1 7.3 %all-to-all-start.1 = ((f32[16,16,128]{2,1,0:T(8,128)}), f32[16,16,128]{2,1,0:T(8,128)S(1)}, u32[]{:S(2)}, u32[]{:S(2)}) async-start(f32[16,16,128]{2,1,0:T(8,128)} %get-tuple-element.23), calls=%async_computation.1 | async-start | bytes 262144 | tf_op jit(solution)/shard_map/all_to_all | solution.py:242
  35.4 3.6 %collective-permute-start.4 = (f32[2,16,128]{2,1,0:T(8,128)}, f32[2,16,128]{2,1,0:T(8,128)}, u32[]{:S(2)}, u32[]{:S(2)}) collective-permute-start(f32[2,16,128]{2,1,0:T(8,128)} %pad_maximum_fusion.3), channel_id=1, source_target_pairs={{0,48},{16,64},{32,80},{48,96},{64,112},{80,128},{96,144},{112,160... | collective-permute-start | bytes 49160 | tf_op jit(solution)/shard_map/ppermute | solution.py:223
  38.9 7.3 %collective-permute-start.3 = (f32[2,16,128]{2,1,0:T(8,128)}, f32[2,16,128]{2,1,0:T(8,128)}, u32[]{:S(2)}, u32[]{:S(2)}) collective-permute-start(f32[2,16,128]{2,1,0:T(8,128)} %pad_maximum_fusion.3), channel_id=1, source_target_pairs={{0,32},{16,48},{32,64},{48,80},{64,96},{80,112},{96,128},{112,144}... | collective-permute-start | bytes 49160 | tf_op jit(solution)/shard_map/ppermute | solution.py:223
  46.2 4.3 %collective-permute-start.2 = (f32[2,16,128]{2,1,0:T(8,128)}, f32[2,16,128]{2,1,0:T(8,128)}, u32[]{:S(2)}, u32[]{:S(2)}) collective-permute-start(f32[2,16,128]{2,1,0:T(8,128)} %pad_maximum_fusion.3), channel_id=1, source_target_pairs={{0,16},{16,32},{32,48},{48,64},{64,80},{80,96},{96,112},{112,128},... | collective-permute-start | bytes 49160 | tf_op jit(solution)/shard_map/ppermute | solution.py:223
  51.1 2.3 %collective-permute-done.2 = f32[2,16,128]{2,1,0:T(8,128)} collective-permute-done((f32[2,16,128]{2,1,0:T(8,128)}, f32[2,16,128]{2,1,0:T(8,128)}, u32[]{:S(2)}, u32[]{:S(2)}) %collective-permute-start.2) | collective-permute-done | bytes 16416 | tf_op jit(solution)/shard_map/ppermute | solution.py:223
  53.4 1.4 %pad_maximum_fusion.2 = f32[8,16,128]{2,1,0:T(8,128)} fusion(f32[2,16,128]{2,1,0:T(8,128)} %collective-permute-done.4, f32[2,16,128]{2,1,0:T(8,128)} %collective-permute-done.3, f32[2,16,128]{2,1,0:T(8,128)} %collective-permute-done.2, f32[2,16,128]{2,1,0:T(8,128)} %pad_maximum_fusion.3), kind=kLoop, calls=%fused_computation.29 | loop fusion | flops 49152 | bytes 131072 | tf_op jit(solution)/shard_map/concatenate | solution.py:220
  54.8 1.6 %convolution_bitcast_fusion = f32[2,128]{1,0:T(2,128)S(1)} fusion(f32[8,128,128]{2,1,0:T(8,128)} %all-to-all-done, f32[2,8,128]{2,1,0:T(8,128)S(1)} %slice_reduce_fusion.2), kind=kOutput, calls=%fused_computation.5 | convolution fusion | flops 3145728 | bytes 533504 | tf_op jit(solution)/shard_map/dot_general | solution.py:280
  57.1 3.3 %pad_add_fusion = f32[4,1160,128]{2,1,0:T(8,128)} fusion(f32[4,8,128]{2,1,0:T(8,128)S(1)} %broadcast_in_dim.40, f32[4,1160,128]{2,1,0:T(8,128)S(1)} %get-tuple-element.19, f32[4,1160,128]{2,1,0:T(8,128)} %collective-permute-done.1), kind=kLoop, calls=%fused_computation | loop fusion | flops 1187840 | bytes 7143424 | tf_op jit(solution)/shard_map/add | solution.py:297
  60.4 4.4 %all-to-all-start.2 = ((f32[4,1160,128]{2,1,0:T(8,128)}), f32[4,1160,128]{2,1,0:T(8,128)S(1)}, u32[]{:S(2)}, u32[]{:S(2)}) async-start(f32[4,1160,128]{2,1,0:T(8,128)} %pad_add_fusion), calls=%async_computation.2 | async-start | bytes 4751360 | tf_op jit(solution)/shard_map/all_to_all | solution.py:242
  64.9 0.8 dynamic-slice_bitcast_fusion
  65.7 2.2 %collective-permute-start.7 = (f32[4,256,128]{2,1,0:T(8,128)}, f32[4,256,128]{2,1,0:T(8,128)}, u32[]{:S(2)}, u32[]{:S(2)}) collective-permute-start(f32[4,256,128]{2,1,0:T(8,128)} %dynamic-slice_bitcast_fusion), channel_id=1, source_target_pairs={{0,1},{1,0},{2,3},{3,2},{4,5},{5,4},{6,7},{7,6},{8,9},{9,8},{10,11... | collective-permute-start | bytes 1572872 | tf_op jit(solution)/shard_map/ppermute | solution.py:233
  67.9 6.5 %collective-permute-start.6 = (f32[8,16,128]{2,1,0:T(8,128)S(1)}, f32[8,16,128]{2,1,0:T(8,128)S(1)}, u32[]{:S(2)}, u32[]{:S(2)}) collective-permute-start(f32[8,16,128]{2,1,0:T(8,128)S(1)} %copy-done.1), channel_id=1, source_target_pairs={{0,128},{16,144},{32,160},{48,176},{64,0},{80,16},{96,32},{112,48}... | collective-permute-start | bytes 196616 | tf_op jit(solution)/shard_map/ppermute | solution.py:223
  74.4 3.3 %collective-permute-start.5 = (f32[8,16,128]{2,1,0:T(8,128)S(1)}, f32[8,16,128]{2,1,0:T(8,128)S(1)}, u32[]{:S(2)}, u32[]{:S(2)}) collective-permute-start(f32[8,16,128]{2,1,0:T(8,128)S(1)} %copy-done.1), channel_id=1, source_target_pairs={{0,64},{16,80},{32,96},{48,112},{64,128},{80,144},{96,160},{112,17... | collective-permute-start | bytes 196616 | tf_op jit(solution)/shard_map/ppermute | solution.py:223
  77.6 2.3 %collective-permute-done.7 = f32[4,256,128]{2,1,0:T(8,128)} collective-permute-done((f32[4,256,128]{2,1,0:T(8,128)}, f32[4,256,128]{2,1,0:T(8,128)}, u32[]{:S(2)}, u32[]{:S(2)}) %collective-permute-start.7) | collective-permute-done | bytes 524320 | tf_op jit(solution)/shard_map/ppermute | solution.py:233
  79.9 1.9 %bitcast_add_fusion = f32[4,256,128]{2,1,0:T(8,128)} fusion(f32[4,256,128]{2,1,0:T(8,128)} %collective-permute-done.7, f32[4,2,256,128]{3,2,1,0:T(8,128)S(1)} %bitcast.63, s32[]{:T(128)S(6)} %select_n.68), kind=kLoop, calls=%fused_computation.8 | loop fusion | flops 131072 | bytes 1572868 | tf_op jit(solution)/shard_map/add | solution.py:238
  81.8 3.4 %collective-permute-done.5 = f32[8,16,128]{2,1,0:T(8,128)S(1)} collective-permute-done((f32[8,16,128]{2,1,0:T(8,128)S(1)}, f32[8,16,128]{2,1,0:T(8,128)S(1)}, u32[]{:S(2)}, u32[]{:S(2)}) %collective-permute-start.5) | collective-permute-done | bytes 65568 | tf_op jit(solution)/shard_map/ppermute | solution.py:223
  85.2 7.6 %all-to-all-done.2 = f32[4,1160,128]{2,1,0:T(8,128)S(1)} async-done(((f32[4,1160,128]{2,1,0:T(8,128)}), f32[4,1160,128]{2,1,0:T(8,128)S(1)}, u32[]{:S(2)}, u32[]{:S(2)}) %all-to-all-start.2) | async-done | bytes 2375712 | tf_op jit(solution)/shard_map/all_to_all | solution.py:242
  93.0 0.9 pad_maximum_fusion
  93.9 8.2 %all-to-all-start.3 = ((f32[12,120,128]{2,1,0:T(8,128)}), f32[12,120,128]{2,1,0:T(8,128)S(1)}, u32[]{:S(2)}, u32[]{:S(2)}) async-start(f32[12,120,128]{2,1,0:T(8,128)} %pad_maximum_fusion), calls=%async_computation.3 | async-start | bytes 1474560 | tf_op jit(solution)/shard_map/all_to_all | solution.py:242
  102.3 4.3 %collective-permute-start.8 = (f32[256,128]{1,0:T(8,128)S(1)}, f32[256,128]{1,0:T(8,128)S(1)}, u32[]{:S(2)}, u32[]{:S(2)}) collective-permute-start(f32[256,128]{1,0:T(8,128)S(1)} %get-tuple-element.42), channel_id=1, source_target_pairs={{0,2},{1,3},{2,0},{3,1},{4,6},{5,7},{6,4},{7,5},{8,10},{9,11},{10,... | collective-permute-start | bytes 393224 | tf_op jit(solution)/shard_map/ppermute | solution.py:335
  106.6 4.6 %collective-permute-start.10 = (f32[256,128]{1,0:T(8,128)S(1)}, f32[256,128]{1,0:T(8,128)S(1)}, u32[]{:S(2)}, u32[]{:S(2)}) collective-permute-start(f32[256,128]{1,0:T(8,128)S(1)} %get-tuple-element.43), channel_id=1, source_target_pairs={{0,6},{1,7},{2,4},{3,5},{4,2},{5,3},{6,0},{7,1},{8,14},{9,15},{10,... | collective-permute-start | bytes 393224 | tf_op jit(solution)/shard_map/ppermute | solution.py:335
  111.2 3.3 %collective-permute-start.9 = (f32[256,128]{1,0:T(8,128)S(1)}, f32[256,128]{1,0:T(8,128)S(1)}, u32[]{:S(2)}, u32[]{:S(2)}) collective-permute-start(f32[256,128]{1,0:T(8,128)S(1)} %get-tuple-element.44), channel_id=1, source_target_pairs={{0,4},{1,5},{2,6},{3,7},{4,0},{5,1},{6,2},{7,3},{8,12},{9,13},{10,... | collective-permute-start | bytes 393224 | tf_op jit(solution)/shard_map/ppermute | solution.py:335
  115.2 3.1 %collective-permute-start.13 = (f32[24,16,128]{2,1,0:T(8,128)S(1)}, f32[24,16,128]{2,1,0:T(8,128)S(1)}, u32[]{:S(2)}, u32[]{:S(2)}) collective-permute-start(f32[24,16,128]{2,1,0:T(8,128)S(1)} %pad_maximum_fusion.1), channel_id=1, source_target_pairs={{0,576},{192,0},{384,192},{576,384},{1,577},{193,1},{385,193},{577... | collective-permute-start | bytes 589832 | tf_op jit(solution)/shard_map/ppermute | solution.py:223
  118.3 3.4 %collective-permute-start.12 = (f32[24,16,128]{2,1,0:T(8,128)S(1)}, f32[24,16,128]{2,1,0:T(8,128)S(1)}, u32[]{:S(2)}, u32[]{:S(2)}) collective-permute-start(f32[24,16,128]{2,1,0:T(8,128)S(1)} %pad_maximum_fusion.1), channel_id=1, source_target_pairs={{0,384},{192,576},{384,0},{576,192},{1,385},{193,577},{385,1},{577... | collective-permute-start | bytes 589832 | tf_op jit(solution)/shard_map/ppermute | solution.py:223
  121.7 1.9 %collective-permute-start.11 = (f32[24,16,128]{2,1,0:T(8,128)S(1)}, f32[24,16,128]{2,1,0:T(8,128)S(1)}, u32[]{:S(2)}, u32[]{:S(2)}) collective-permute-start(f32[24,16,128]{2,1,0:T(8,128)S(1)} %pad_maximum_fusion.1), channel_id=1, source_target_pairs={{0,192},{192,384},{384,576},{576,0},{1,193},{193,385},{385,577},{5... | collective-permute-start | bytes 589832 | tf_op jit(solution)/shard_map/ppermute | solution.py:223
  124.3 6.1 %collective-permute-done.11 = f32[24,16,128]{2,1,0:T(8,128)S(1)} collective-permute-done((f32[24,16,128]{2,1,0:T(8,128)S(1)}, f32[24,16,128]{2,1,0:T(8,128)S(1)}, u32[]{:S(2)}, u32[]{:S(2)}) %collective-permute-start.11) | collective-permute-done | bytes 196640 | tf_op jit(solution)/shard_map/ppermute | solution.py:223
  131.8 1.4 %convolution_multiply_fusion.1 = f32[1024,128]{1,0:T(8,128)} fusion(f32[96,256]{1,0:T(8,128)S(1)} %fusion.8, f32[12,8,8,128]{3,2,1,0:T(8,128)S(1)} %bitcast.65), kind=kOutput, calls=%fused_computation.3 | convolution fusion | flops 75923456 | bytes 966656 | tf_op jit(solution)/shard_map/dot_general | solution.py:364
  133.2 1.4 %convolution_multiply_fusion = f32[1024,128]{1,0:T(8,128)} fusion(f32[12,8,8,128]{3,2,1,0:T(8,128)S(1)} %bitcast.67, f32[96,256]{1,0:T(8,128)S(1)} %fusion.8, f32[96,1024]{1,0:T(8,128)S(1)} %bitcast.69, s32[]{:T(128)S(6)} %select_n.75), kind=kOutput, calls=%fused_computation.2 | convolution fusion | flops 75665408 | bytes 1015812 | tf_op jit(solution)/shard_map/dot_general | solution.py:369
  (57 shorter events, 5.6 us)
Async XLA Ops:
  0.6 25.1 %all-to-all-start = ((f32[8,128,128]{2,1,0:T(8,128)}), f32[8,128,128]{2,1,0:T(8,128)}, u32[]{:S(2)}, u32[]{:S(2)}) async-start(f32[8,128,128]{2,1,0:T(8,128)} %bitcast.68), calls=%async_computation | async-start | bytes 1048576 | tf_op jit(solution)/shard_map/all_to_all | solution.py:242
  14.1 10.9 %copy-start.2 = (f32[1,1024]{1,0:T(1,128)S(1)}, f32[1,1024]{1,0:T(1,128)}, u32[]{:S(2)}) copy-start(f32[1,1024]{1,0:T(1,128)} %param.19) | copy-start | bytes 12292
  14.1 10.9 %copy-start.3 = (f32[1,1024]{1,0:T(1,128)S(1)}, f32[1,1024]{1,0:T(1,128)}, u32[]{:S(2)}) copy-start(f32[1,1024]{1,0:T(1,128)} %param.18) | copy-start | bytes 12292
  14.9 10.1 %collective-permute-start = (f32[1,16,128]{2,1,0:T(8,128)S(1)}, f32[1,16,128]{2,1,0:T(8,128)S(1)}, u32[]{:S(2)}, u32[]{:S(2)}) collective-permute-start(f32[1,16,128]{2,1,0:T(8,128)S(1)} %pad_maximum_fusion.5), channel_id=1, source_target_pairs={{0,8},{8,0},{1,9},{9,1},{2,10},{10,2},{3,11},{11,3},{4,12},{12,4},... | collective-permute-start | bytes 24584 | tf_op jit(solution)/shard_map/ppermute | solution.py:223
  25.7 31.4 %collective-permute-start.1 = (f32[4,1160,128]{2,1,0:T(8,128)}, f32[4,1160,128]{2,1,0:T(8,128)}, u32[]{:S(2)}, u32[]{:S(2)}) collective-permute-start(f32[4,1160,128]{2,1,0:T(8,128)} %get-tuple-element.22), channel_id=1, source_target_pairs={{0,8},{8,0},{1,9},{9,1},{2,10},{10,2},{3,11},{11,3},{4,12},{12,4},... | collective-permute-start | bytes 7127048 | tf_op jit(solution)/shard_map/ppermute | solution.py:276
  28.1 26.7 %all-to-all-start.1 = ((f32[16,16,128]{2,1,0:T(8,128)}), f32[16,16,128]{2,1,0:T(8,128)S(1)}, u32[]{:S(2)}, u32[]{:S(2)}) async-start(f32[16,16,128]{2,1,0:T(8,128)} %get-tuple-element.23), calls=%async_computation.1 | async-start | bytes 262144 | tf_op jit(solution)/shard_map/all_to_all | solution.py:242
  35.4 15.8 %collective-permute-start.4 = (f32[2,16,128]{2,1,0:T(8,128)}, f32[2,16,128]{2,1,0:T(8,128)}, u32[]{:S(2)}, u32[]{:S(2)}) collective-permute-start(f32[2,16,128]{2,1,0:T(8,128)} %pad_maximum_fusion.3), channel_id=1, source_target_pairs={{0,48},{16,64},{32,80},{48,96},{64,112},{80,128},{96,144},{112,160... | collective-permute-start | bytes 49160 | tf_op jit(solution)/shard_map/ppermute | solution.py:223
  38.9 12.2 %collective-permute-start.3 = (f32[2,16,128]{2,1,0:T(8,128)}, f32[2,16,128]{2,1,0:T(8,128)}, u32[]{:S(2)}, u32[]{:S(2)}) collective-permute-start(f32[2,16,128]{2,1,0:T(8,128)} %pad_maximum_fusion.3), channel_id=1, source_target_pairs={{0,32},{16,48},{32,64},{48,80},{64,96},{80,112},{96,128},{112,144}... | collective-permute-start | bytes 49160 | tf_op jit(solution)/shard_map/ppermute | solution.py:223
  46.2 7.2 %collective-permute-start.2 = (f32[2,16,128]{2,1,0:T(8,128)}, f32[2,16,128]{2,1,0:T(8,128)}, u32[]{:S(2)}, u32[]{:S(2)}) collective-permute-start(f32[2,16,128]{2,1,0:T(8,128)} %pad_maximum_fusion.3), channel_id=1, source_target_pairs={{0,16},{16,32},{32,48},{48,64},{64,80},{80,96},{96,112},{112,128},... | collective-permute-start | bytes 49160 | tf_op jit(solution)/shard_map/ppermute | solution.py:223
  60.4 7.4 %copy-start.1 = (f32[8,16,128]{2,1,0:T(8,128)S(1)}, f32[8,16,128]{2,1,0:T(8,128)}, u32[]{:S(2)}) copy-start(f32[8,16,128]{2,1,0:T(8,128)} %pad_maximum_fusion.2) | copy-start | bytes 196612
  60.4 32.4 %all-to-all-start.2 = ((f32[4,1160,128]{2,1,0:T(8,128)}), f32[4,1160,128]{2,1,0:T(8,128)S(1)}, u32[]{:S(2)}, u32[]{:S(2)}) async-start(f32[4,1160,128]{2,1,0:T(8,128)} %pad_add_fusion), calls=%async_computation.2 | async-start | bytes 4751360 | tf_op jit(solution)/shard_map/all_to_all | solution.py:242
  65.7 14.2 %collective-permute-start.7 = (f32[4,256,128]{2,1,0:T(8,128)}, f32[4,256,128]{2,1,0:T(8,128)}, u32[]{:S(2)}, u32[]{:S(2)}) collective-permute-start(f32[4,256,128]{2,1,0:T(8,128)} %dynamic-slice_bitcast_fusion), channel_id=1, source_target_pairs={{0,1},{1,0},{2,3},{3,2},{4,5},{5,4},{6,7},{7,6},{8,9},{9,8},{10,11... | collective-permute-start | bytes 1572872 | tf_op jit(solution)/shard_map/ppermute | solution.py:233
  67.9 13.9 %collective-permute-start.6 = (f32[8,16,128]{2,1,0:T(8,128)S(1)}, f32[8,16,128]{2,1,0:T(8,128)S(1)}, u32[]{:S(2)}, u32[]{:S(2)}) collective-permute-start(f32[8,16,128]{2,1,0:T(8,128)S(1)} %copy-done.1), channel_id=1, source_target_pairs={{0,128},{16,144},{32,160},{48,176},{64,0},{80,16},{96,32},{112,48}... | collective-permute-start | bytes 196616 | tf_op jit(solution)/shard_map/ppermute | solution.py:223
  74.4 10.8 %collective-permute-start.5 = (f32[8,16,128]{2,1,0:T(8,128)S(1)}, f32[8,16,128]{2,1,0:T(8,128)S(1)}, u32[]{:S(2)}, u32[]{:S(2)}) collective-permute-start(f32[8,16,128]{2,1,0:T(8,128)S(1)} %copy-done.1), channel_id=1, source_target_pairs={{0,64},{16,80},{32,96},{48,112},{64,128},{80,144},{96,160},{112,17... | collective-permute-start | bytes 196616 | tf_op jit(solution)/shard_map/ppermute | solution.py:223
  92.8 9.4 %copy-start.4 = (s32[96]{0:T(128)S(1)}, s32[96]{0:T(128)}, u32[]{:S(2)}) copy-start(s32[96]{0:T(128)} %constant.144) | copy-start | bytes 1156
  92.8 9.4 %copy-start.5 = (s32[96]{0:T(128)S(1)}, s32[96]{0:T(128)}, u32[]{:S(2)}) copy-start(s32[96]{0:T(128)} %constant.143) | copy-start | bytes 1156
  92.8 9.4 %copy-start.6 = (s32[96]{0:T(128)S(1)}, s32[96]{0:T(128)}, u32[]{:S(2)}) copy-start(s32[96]{0:T(128)} %constant.142) | copy-start | bytes 1156
  93.0 9.3 %copy-start = (f32[4,256,128]{2,1,0:T(8,128)S(1)}, f32[4,256,128]{2,1,0:T(8,128)}, u32[]{:S(2)}) copy-start(f32[4,256,128]{2,1,0:T(8,128)} %bitcast_add_fusion) | copy-start | bytes 1572868
  93.9 36.8 %all-to-all-start.3 = ((f32[12,120,128]{2,1,0:T(8,128)}), f32[12,120,128]{2,1,0:T(8,128)S(1)}, u32[]{:S(2)}, u32[]{:S(2)}) async-start(f32[12,120,128]{2,1,0:T(8,128)} %pad_maximum_fusion), calls=%async_computation.3 | async-start | bytes 1474560 | tf_op jit(solution)/shard_map/all_to_all | solution.py:242
  102.3 19.4 %collective-permute-start.8 = (f32[256,128]{1,0:T(8,128)S(1)}, f32[256,128]{1,0:T(8,128)S(1)}, u32[]{:S(2)}, u32[]{:S(2)}) collective-permute-start(f32[256,128]{1,0:T(8,128)S(1)} %get-tuple-element.42), channel_id=1, source_target_pairs={{0,2},{1,3},{2,0},{3,1},{4,6},{5,7},{6,4},{7,5},{8,10},{9,11},{10,... | collective-permute-start | bytes 393224 | tf_op jit(solution)/shard_map/ppermute | solution.py:335
  106.6 17.0 %collective-permute-start.10 = (f32[256,128]{1,0:T(8,128)S(1)}, f32[256,128]{1,0:T(8,128)S(1)}, u32[]{:S(2)}, u32[]{:S(2)}) collective-permute-start(f32[256,128]{1,0:T(8,128)S(1)} %get-tuple-element.43), channel_id=1, source_target_pairs={{0,6},{1,7},{2,4},{3,5},{4,2},{5,3},{6,0},{7,1},{8,14},{9,15},{10,... | collective-permute-start | bytes 393224 | tf_op jit(solution)/shard_map/ppermute | solution.py:335
  111.2 12.4 %collective-permute-start.9 = (f32[256,128]{1,0:T(8,128)S(1)}, f32[256,128]{1,0:T(8,128)S(1)}, u32[]{:S(2)}, u32[]{:S(2)}) collective-permute-start(f32[256,128]{1,0:T(8,128)S(1)} %get-tuple-element.44), channel_id=1, source_target_pairs={{0,4},{1,5},{2,6},{3,7},{4,0},{5,1},{6,2},{7,3},{8,12},{9,13},{10,... | collective-permute-start | bytes 393224 | tf_op jit(solution)/shard_map/ppermute | solution.py:335
  115.2 15.3 %collective-permute-start.13 = (f32[24,16,128]{2,1,0:T(8,128)S(1)}, f32[24,16,128]{2,1,0:T(8,128)S(1)}, u32[]{:S(2)}, u32[]{:S(2)}) collective-permute-start(f32[24,16,128]{2,1,0:T(8,128)S(1)} %pad_maximum_fusion.1), channel_id=1, source_target_pairs={{0,576},{192,0},{384,192},{576,384},{1,577},{193,1},{385,193},{577... | collective-permute-start | bytes 589832 | tf_op jit(solution)/shard_map/ppermute | solution.py:223
  118.3 12.2 %collective-permute-start.12 = (f32[24,16,128]{2,1,0:T(8,128)S(1)}, f32[24,16,128]{2,1,0:T(8,128)S(1)}, u32[]{:S(2)}, u32[]{:S(2)}) collective-permute-start(f32[24,16,128]{2,1,0:T(8,128)S(1)} %pad_maximum_fusion.1), channel_id=1, source_target_pairs={{0,384},{192,576},{384,0},{576,192},{1,385},{193,577},{385,1},{577... | collective-permute-start | bytes 589832 | tf_op jit(solution)/shard_map/ppermute | solution.py:223
  121.7 8.8 %collective-permute-start.11 = (f32[24,16,128]{2,1,0:T(8,128)S(1)}, f32[24,16,128]{2,1,0:T(8,128)S(1)}, u32[]{:S(2)}, u32[]{:S(2)}) collective-permute-start(f32[24,16,128]{2,1,0:T(8,128)S(1)} %pad_maximum_fusion.1), channel_id=1, source_target_pairs={{0,192},{192,384},{384,576},{576,0},{1,193},{193,385},{385,577},{5... | collective-permute-start | bytes 589832 | tf_op jit(solution)/shard_map/ppermute | solution.py:223

commit v9 on v8

--- a/solution.py
+++ b/solution.py
@@ -215,16 +215,12 @@
     )
 
 
-def gathered_from(rows, name, hops):
+def arriving(rows, name, hops):
     size = lax.axis_size(name)
-    return jnp.concatenate(
-        [rows]
-        + [
-            lax.ppermute(rows, name, [(sender, (sender + hop) % size) for sender in range(size)])
-            for hop in hops
-        ],
-        axis=0,
-    )
+    return [
+        lax.ppermute(rows, name, [(sender, (sender + hop) % size) for sender in range(size)])
+        for hop in hops
+    ]
 
 
 def halved(blocks, bit):
@@ -257,7 +253,6 @@
     own_rows = jnp.concatenate(
         [latents.reshape(1, -1, LANES), map_pre.reshape(1, -1, LANES)], axis=1
     )
-    pair = gathered_from(own_rows, "core", (1,))
     map_rows = exchange(map_weight.reshape(nchan, -1, cols_dev), "chan")
 
     core_id = lax.axis_index("core")
@@ -271,7 +266,7 @@
         jnp.broadcast_to(source[:, None], (1, cols_dev)),
         (nx, nz, rows_dev, ncore * nchan),
     )
-    tile, sent, map_rows, pair = lax.optimization_barrier((tile, sent, map_rows, pair))
+    tile, sent, map_rows, own_rows = lax.optimization_barrier((tile, sent, map_rows, own_rows))
     parts = exchange(tile, ("core", "chan")).reshape(ncore, nchan, -1, LANES)
     coming = lax.ppermute(sent, "core", [(core, ncore - 1 - core) for core in range(ncore)])
     inner_half = halved(inner_part, 1)
@@ -291,7 +286,7 @@
     riders = jnp.concatenate(
         [style_rows, hidden_rows, parts[:, 0, -1], jnp.zeros((8 - 3 * ncore, cols_dev))], axis=0
     )
-    near = gathered_from(pair, "z", range(1, min(4, nz)))
+    near = arriving(own_rows, "z", range(1, min(4, nz)))
     coming, riders, near = lax.optimization_barrier((coming, riders, near))
     moved = exchange(
         kept
@@ -302,7 +297,9 @@
         ),
         "x",
     )
-    gathered = gathered_from(near, "z", range(4, nz, 4))
+    near = jnp.concatenate([own_rows] + near, axis=0)
+    gathered = jnp.concatenate([near] + arriving(near, "z", range(4, nz, 4)), axis=0)
+    gathered = jnp.concatenate([gathered] + arriving(gathered, "core", (1,)), axis=0)
     pieces = jnp.sum(moved[:, : nz * rows_dev], axis=0).reshape(nz, rows_dev, cols_dev)
     riders = jnp.concatenate(
         [
@@ -319,9 +316,9 @@
     moved = exchange(
         jnp.concatenate([pieces, jnp.broadcast_to(riders[None], (nz,) + riders.shape)], axis=1), "z"
     )
-    gathered = gathered_from(gathered, "x", range(1, nx))
-    back_x, back_z, back_core = np.meshgrid(
-        np.arange(nx), np.arange(nz), np.arange(ncore), indexing="ij"
+    gathered = jnp.concatenate([gathered] + arriving(gathered, "x", range(1, nx)), axis=0)
+    back_x, back_core, back_z = np.meshgrid(
+        np.arange(nx), np.arange(ncore), np.arange(nz), indexing="ij"
     )
     spots = [
         (lax.axis_index(name) + lax.axis_size(name) - back.reshape(-1)) % lax.axis_size(name)

time: 136 us -> 138 us (1.015)
  the two profiles are of different devices: /device:TPU:8 before, /device:TPU:2 now
where the time goes in v9:
time: 138 us; the launch traced here: 137 us
  starting transfers between devices  81.9 us (59%)
  waiting for transfers between devices  21.4 us (16%)
  local copies, waits for them, and re-layouts  9.83 us (7%)
  other arithmetic  9.7 us (7%)
  Pallas kernels  6.89 us (5%)
  matrix products  4.66 us (3%)
  between operations  2.37 us (2%)
    ppermute x9, starting transfers between devices, arriving(): lax.ppermute(rows, name, [(sender, (sender + hop) % size) for sender in r...  42.3 us
    all_to_all x4, starting transfers between devices, exchange(): return lax.all_to_all(blocks, axes, 0, 0, tiled=True)  21.9 us
    ppermute x3, starting transfers between devices, local(): lax.ppermute(lax.dynamic_index_in_dim(inner_half, place ^ flip, 0, keepdi...  12.2 us
    ppermute x9, waiting for transfers between devices, arriving(): lax.ppermute(rows, name, [(sender, (sender + hop) % size) for sender in r...  11.6 us
    all_to_all x4, waiting for transfers between devices, exchange(): return lax.all_to_all(blocks, axes, 0, 0, tiled=True)  9.82 us
    pallas_call x1, Pallas kernels, convolution_part(): pl.pallas_call(functools.partial(convolution_kernel, side, rows_dev), out...  6.89 us
    unnamed x19, local copies, waits for them, and re-layouts  6.22 us
    ppermute x1, starting transfers between devices, halved(): lax.ppermute(lax.dynamic_index_in_dim(pairs, 1 - side, 1, keepdims=False)...  3.66 us
  transfers between devices with their start and end apart: 18, of which 7 were waited for; matrix products, arithmetic and copies ran while one was open for 12% of the time, Pallas kernels for 5%

profile of v9, /device:TPU:2, one launch (start us, length us, event | category | flops | bytes accessed | tf_op | source)
XLA Modules:
  0.0 136.8 jit_solution(8747649204507440257)
XLA Ops:
  0.6 7.1 %all-to-all-start = ((f32[8,128,128]{2,1,0:T(8,128)}), f32[8,128,128]{2,1,0:T(8,128)}, u32[]{:S(2)}, u32[]{:S(2)}) async-start(f32[8,128,128]{2,1,0:T(8,128)} %bitcast.68), calls=%async_computation | async-start | bytes 1048576 | tf_op jit(solution)/shard_map/all_to_all | solution.py:238
  9.1 1.3 pad_maximum_fusion.2
  10.4 6.9 %convolution_part.1 = (f32[4,1160,128]{2,1,0:T(8,128)}, f32[4,1160,128]{2,1,0:T(8,128)S(1)}, f32[8,256,128]{2,1,0:T(8,128)S(1)}, f32[16,16,128]{2,1,0:T(8,128)}) custom-call(s32[1]{0:T(128)} %bitcast.core_ref, bf16[256,1024]{1,0:T(8,128)(2,1)} %bitcast.81, f32[1,1024]{1,0:T(1,128)} %style_hbm.1, bf16[9216,128]{1,0:T(8,128)(2,1)} %bitcast.80, ...), custom_call_target="tpu_custom_call" | custom-call | flops 1207959552 | bytes 12000000 | tf_op jit(solution)/shard_map/convolution_part/pallas_call | solution.py:179
  17.3 8.1 %all-to-all-done = f32[8,128,128]{2,1,0:T(8,128)} async-done(((f32[8,128,128]{2,1,0:T(8,128)}), f32[8,128,128]{2,1,0:T(8,128)}, u32[]{:S(2)}, u32[]{:S(2)}) %all-to-all-start) | async-done | bytes 524320 | tf_op jit(solution)/shard_map/all_to_all | solution.py:238
  25.3 1.9 %collective-permute-start = (f32[4,1160,128]{2,1,0:T(8,128)}, f32[4,1160,128]{2,1,0:T(8,128)}, u32[]{:S(2)}, u32[]{:S(2)}) collective-permute-start(f32[4,1160,128]{2,1,0:T(8,128)} %get-tuple-element.24), channel_id=1, source_target_pairs={{0,8},{8,0},{1,9},{9,1},{2,10},{10,2},{3,11},{11,3},{4,12},{12,4},... | collective-permute-start | bytes 7127048 | tf_op jit(solution)/shard_map/ppermute | solution.py:271
  27.3 3.5 %all-to-all-start.1 = ((f32[16,16,128]{2,1,0:T(8,128)}), f32[16,16,128]{2,1,0:T(8,128)S(1)}, u32[]{:S(2)}, u32[]{:S(2)}) async-start(f32[16,16,128]{2,1,0:T(8,128)} %get-tuple-element.25), calls=%async_computation.1 | async-start | bytes 262144 | tf_op jit(solution)/shard_map/all_to_all | solution.py:238
  31.4 4.3 %collective-permute-start.1 = (f32[1,16,128]{2,1,0:T(8,128)}, f32[1,16,128]{2,1,0:T(8,128)}, u32[]{:S(2)}, u32[]{:S(2)}) collective-permute-start(f32[1,16,128]{2,1,0:T(8,128)} %pad_maximum_fusion.2), channel_id=1, source_target_pairs={{0,16},{16,32},{32,48},{48,64},{64,80},{80,96},{96,112},{112,128},... | collective-permute-start | bytes 24584 | tf_op jit(solution)/shard_map/ppermute | solution.py:221
  35.7 6.1 %collective-permute-start.2 = (f32[1,16,128]{2,1,0:T(8,128)}, f32[1,16,128]{2,1,0:T(8,128)}, u32[]{:S(2)}, u32[]{:S(2)}) collective-permute-start(f32[1,16,128]{2,1,0:T(8,128)} %pad_maximum_fusion.2), channel_id=1, source_target_pairs={{0,32},{16,48},{32,64},{48,80},{64,96},{80,112},{96,128},{112,144}... | collective-permute-start | bytes 24584 | tf_op jit(solution)/shard_map/ppermute | solution.py:221
  41.8 9.1 %collective-permute-start.3 = (f32[1,16,128]{2,1,0:T(8,128)}, f32[1,16,128]{2,1,0:T(8,128)}, u32[]{:S(2)}, u32[]{:S(2)}) collective-permute-start(f32[1,16,128]{2,1,0:T(8,128)} %pad_maximum_fusion.2), channel_id=1, source_target_pairs={{0,48},{16,64},{32,80},{48,96},{64,112},{80,128},{96,144},{112,160... | collective-permute-start | bytes 24584 | tf_op jit(solution)/shard_map/ppermute | solution.py:221
  51.0 1.6 %convolution_bitcast_fusion = f32[2,128]{1,0:T(2,128)S(1)} fusion(f32[8,128,128]{2,1,0:T(8,128)} %all-to-all-done, f32[2,8,128]{2,1,0:T(8,128)S(1)} %slice_reduce_fusion.2), kind=kOutput, calls=%fused_computation.5 | convolution fusion | flops 3145728 | bytes 533504 | tf_op jit(solution)/shard_map/dot_general | solution.py:275
  54.2 3.4 %pad_add_fusion = f32[4,1160,128]{2,1,0:T(8,128)} fusion(f32[4,8,128]{2,1,0:T(8,128)S(1)} %broadcast_in_dim.40, f32[4,1160,128]{2,1,0:T(8,128)S(1)} %get-tuple-element.21, f32[4,1160,128]{2,1,0:T(8,128)} %collective-permute-done), kind=kLoop, calls=%fused_computation | loop fusion | flops 1187840 | bytes 7143424 | tf_op jit(solution)/shard_map/add | solution.py:292
  57.5 5.0 %all-to-all-start.2 = ((f32[4,1160,128]{2,1,0:T(8,128)}), f32[4,1160,128]{2,1,0:T(8,128)S(1)}, u32[]{:S(2)}, u32[]{:S(2)}) async-start(f32[4,1160,128]{2,1,0:T(8,128)} %pad_add_fusion), calls=%async_computation.2 | async-start | bytes 4751360 | tf_op jit(solution)/shard_map/all_to_all | solution.py:238
  63.3 3.7 %collective-permute-start.7 = (f32[4,256,128]{2,1,0:T(8,128)}, f32[4,256,128]{2,1,0:T(8,128)}, u32[]{:S(2)}, u32[]{:S(2)}) collective-permute-start(f32[4,256,128]{2,1,0:T(8,128)} %dynamic-slice_bitcast_fusion), channel_id=1, source_target_pairs={{0,1},{1,0},{2,3},{3,2},{4,5},{5,4},{6,7},{7,6},{8,9},{9,8},{10,11... | collective-permute-start | bytes 1572872 | tf_op jit(solution)/shard_map/ppermute | solution.py:229
  67.6 1.3 constant_dynamic-update-slice_fusion.8
  70.2 1.3 constant_dynamic-update-slice_fusion.6
  71.5 7.1 %collective-permute-start.4 = (f32[4,16,128]{2,1,0:T(8,128)S(1)}, f32[4,16,128]{2,1,0:T(8,128)S(1)}, u32[]{:S(2)}, u32[]{:S(2)}) collective-permute-start(f32[4,16,128]{2,1,0:T(8,128)S(1)} %get-tuple-element.55), channel_id=1, source_target_pairs={{0,64},{16,80},{32,96},{48,112},{64,128},{80,144},{96,160},{112,17... | collective-permute-start | bytes 98312 | tf_op jit(solution)/shard_map/ppermute | solution.py:221
  78.7 3.3 %collective-permute-start.5 = (f32[4,16,128]{2,1,0:T(8,128)S(1)}, f32[4,16,128]{2,1,0:T(8,128)S(1)}, u32[]{:S(2)}, u32[]{:S(2)}) collective-permute-start(f32[4,16,128]{2,1,0:T(8,128)S(1)} %get-tuple-element.55), channel_id=1, source_target_pairs={{0,128},{16,144},{32,160},{48,176},{64,0},{80,16},{96,32},{112,48}... | collective-permute-start | bytes 98312 | tf_op jit(solution)/shard_map/ppermute | solution.py:221
  82.7 5.7 %collective-permute-done.5 = f32[4,16,128]{2,1,0:T(8,128)S(1)} collective-permute-done((f32[4,16,128]{2,1,0:T(8,128)S(1)}, f32[4,16,128]{2,1,0:T(8,128)S(1)}, u32[]{:S(2)}, u32[]{:S(2)}) %collective-permute-start.5) | collective-permute-done | bytes 32800 | tf_op jit(solution)/shard_map/ppermute | solution.py:221
  89.0 1.9 %collective-permute-start.6 = (f32[12,16,128]{2,1,0:T(8,128)}, f32[12,16,128]{2,1,0:T(8,128)S(1)}, u32[]{:S(2)}, u32[]{:S(2)}) collective-permute-start(f32[12,16,128]{2,1,0:T(8,128)} %get-tuple-element.49), channel_id=1, source_target_pairs={{0,8},{8,0},{1,9},{9,1},{2,10},{10,2},{3,11},{11,3},{4,12},{12,4},... | collective-permute-start | bytes 294920 | tf_op jit(solution)/shard_map/ppermute | solution.py:221
  90.9 1.9 %bitcast_add_fusion = f32[4,256,128]{2,1,0:T(8,128)} fusion(f32[4,256,128]{2,1,0:T(8,128)} %collective-permute-done.7, f32[4,2,256,128]{3,2,1,0:T(8,128)S(1)} %bitcast.63, s32[]{:T(128)S(6)} %select_n.68), kind=kLoop, calls=%fused_computation.8 | loop fusion | flops 131072 | bytes 1572868 | tf_op jit(solution)/shard_map/add | solution.py:234
  94.6 6.3 %all-to-all-start.3 = ((f32[12,120,128]{2,1,0:T(8,128)}), f32[12,120,128]{2,1,0:T(8,128)S(1)}, u32[]{:S(2)}, u32[]{:S(2)}) async-start(f32[12,120,128]{2,1,0:T(8,128)} %pad_maximum_fusion), calls=%async_computation.3 | async-start | bytes 1474560 | tf_op jit(solution)/shard_map/all_to_all | solution.py:238
  101.0 4.6 %collective-permute-start.10 = (f32[256,128]{1,0:T(8,128)S(1)}, f32[256,128]{1,0:T(8,128)S(1)}, u32[]{:S(2)}, u32[]{:S(2)}) collective-permute-start(f32[256,128]{1,0:T(8,128)S(1)} %get-tuple-element.47), channel_id=1, source_target_pairs={{0,6},{1,7},{2,4},{3,5},{4,2},{5,3},{6,0},{7,1},{8,14},{9,15},{10,... | collective-permute-start | bytes 393224 | tf_op jit(solution)/shard_map/ppermute | solution.py:332
  105.7 4.3 %collective-permute-start.8 = (f32[256,128]{1,0:T(8,128)S(1)}, f32[256,128]{1,0:T(8,128)S(1)}, u32[]{:S(2)}, u32[]{:S(2)}) collective-permute-start(f32[256,128]{1,0:T(8,128)S(1)} %get-tuple-element.46), channel_id=1, source_target_pairs={{0,2},{1,3},{2,0},{3,1},{4,6},{5,7},{6,4},{7,5},{8,10},{9,11},{10,... | collective-permute-start | bytes 393224 | tf_op jit(solution)/shard_map/ppermute | solution.py:332
  109.9 3.3 %collective-permute-start.9 = (f32[256,128]{1,0:T(8,128)S(1)}, f32[256,128]{1,0:T(8,128)S(1)}, u32[]{:S(2)}, u32[]{:S(2)}) collective-permute-start(f32[256,128]{1,0:T(8,128)S(1)} %get-tuple-element.48), channel_id=1, source_target_pairs={{0,4},{1,5},{2,6},{3,7},{4,0},{5,1},{6,2},{7,3},{8,12},{9,13},{10,... | collective-permute-start | bytes 393224 | tf_op jit(solution)/shard_map/ppermute | solution.py:332
  113.9 3.4 %collective-permute-start.11 = (f32[24,16,128]{2,1,0:T(8,128)}, f32[24,16,128]{2,1,0:T(8,128)S(1)}, u32[]{:S(2)}, u32[]{:S(2)}) collective-permute-start(f32[24,16,128]{2,1,0:T(8,128)} %constant_dynamic-update-slice_fusion.10), channel_id=1, source_target_pairs={{0,192},{192,384},{384,576},{576,0},{1,193},{193,385},{385,577},{5... | collective-permute-start | bytes 589832 | tf_op jit(solution)/shard_map/ppermute | solution.py:221
  117.3 2.5 %collective-permute-start.12 = (f32[24,16,128]{2,1,0:T(8,128)}, f32[24,16,128]{2,1,0:T(8,128)S(1)}, u32[]{:S(2)}, u32[]{:S(2)}) collective-permute-start(f32[24,16,128]{2,1,0:T(8,128)} %constant_dynamic-update-slice_fusion.10), channel_id=1, source_target_pairs={{0,384},{192,576},{384,0},{576,192},{1,385},{193,577},{385,1},{577... | collective-permute-start | bytes 589832 | tf_op jit(solution)/shard_map/ppermute | solution.py:221
  120.8 4.5 %collective-permute-start.13 = (f32[24,16,128]{2,1,0:T(8,128)}, f32[24,16,128]{2,1,0:T(8,128)S(1)}, u32[]{:S(2)}, u32[]{:S(2)}) collective-permute-start(f32[24,16,128]{2,1,0:T(8,128)} %constant_dynamic-update-slice_fusion.10), channel_id=1, source_target_pairs={{0,576},{192,0},{384,192},{576,384},{1,577},{193,1},{385,193},{577... | collective-permute-start | bytes 589832 | tf_op jit(solution)/shard_map/ppermute | solution.py:221
  126.1 2.1 %collective-permute-done.12 = f32[24,16,128]{2,1,0:T(8,128)S(1)} collective-permute-done((f32[24,16,128]{2,1,0:T(8,128)}, f32[24,16,128]{2,1,0:T(8,128)S(1)}, u32[]{:S(2)}, u32[]{:S(2)}) %collective-permute-start.12) | collective-permute-done | bytes 196640 | tf_op jit(solution)/shard_map/ppermute | solution.py:221
  128.1 2.9 %collective-permute-done.13 = f32[24,16,128]{2,1,0:T(8,128)S(1)} collective-permute-done((f32[24,16,128]{2,1,0:T(8,128)}, f32[24,16,128]{2,1,0:T(8,128)S(1)}, u32[]{:S(2)}, u32[]{:S(2)}) %collective-permute-start.13) | collective-permute-done | bytes 196640 | tf_op jit(solution)/shard_map/ppermute | solution.py:221
  131.2 1.7 %all-to-all-done.3 = f32[12,120,128]{2,1,0:T(8,128)S(1)} async-done(((f32[12,120,128]{2,1,0:T(8,128)}), f32[12,120,128]{2,1,0:T(8,128)S(1)}, u32[]{:S(2)}, u32[]{:S(2)}) %all-to-all-start.3) | async-done | bytes 737312 | tf_op jit(solution)/shard_map/all_to_all | solution.py:238
  133.4 1.4 %convolution_multiply_fusion.1 = f32[1024,128]{1,0:T(8,128)} fusion(f32[96,256]{1,0:T(8,128)S(1)} %fusion.8, f32[12,8,8,128]{3,2,1,0:T(8,128)S(1)} %bitcast.65), kind=kOutput, calls=%fused_computation.3 | convolution fusion | flops 75923456 | bytes 966656 | tf_op jit(solution)/shard_map/dot_general | solution.py:361
  135.4 1.4 %convolution_multiply_fusion = f32[1024,128]{1,0:T(8,128)} fusion(f32[12,8,8,128]{3,2,1,0:T(8,128)S(1)} %bitcast.67, f32[96,256]{1,0:T(8,128)S(1)} %fusion.8, f32[96,1024]{1,0:T(8,128)S(1)} %bitcast.69, s32[]{:T(128)S(6)} %select_n.75), kind=kOutput, calls=%fused_computation.2 | convolution fusion | flops 75665408 | bytes 1015812 | tf_op jit(solution)/shard_map/dot_general | solution.py:366
  (57 shorter events, 11.7 us)
Async XLA Ops:
  0.6 24.7 %all-to-all-start = ((f32[8,128,128]{2,1,0:T(8,128)}), f32[8,128,128]{2,1,0:T(8,128)}, u32[]{:S(2)}, u32[]{:S(2)}) async-start(f32[8,128,128]{2,1,0:T(8,128)} %bitcast.68), calls=%async_computation | async-start | bytes 1048576 | tf_op jit(solution)/shard_map/all_to_all | solution.py:238
  25.3 28.8 %collective-permute-start = (f32[4,1160,128]{2,1,0:T(8,128)}, f32[4,1160,128]{2,1,0:T(8,128)}, u32[]{:S(2)}, u32[]{:S(2)}) collective-permute-start(f32[4,1160,128]{2,1,0:T(8,128)} %get-tuple-element.24), channel_id=1, source_target_pairs={{0,8},{8,0},{1,9},{9,1},{2,10},{10,2},{3,11},{11,3},{4,12},{12,4},... | collective-permute-start | bytes 7127048 | tf_op jit(solution)/shard_map/ppermute | solution.py:271
  27.3 23.7 %all-to-all-start.1 = ((f32[16,16,128]{2,1,0:T(8,128)}), f32[16,16,128]{2,1,0:T(8,128)S(1)}, u32[]{:S(2)}, u32[]{:S(2)}) async-start(f32[16,16,128]{2,1,0:T(8,128)} %get-tuple-element.25), calls=%async_computation.1 | async-start | bytes 262144 | tf_op jit(solution)/shard_map/all_to_all | solution.py:238
  31.4 21.9 %collective-permute-start.1 = (f32[1,16,128]{2,1,0:T(8,128)}, f32[1,16,128]{2,1,0:T(8,128)}, u32[]{:S(2)}, u32[]{:S(2)}) collective-permute-start(f32[1,16,128]{2,1,0:T(8,128)} %pad_maximum_fusion.2), channel_id=1, source_target_pairs={{0,16},{16,32},{32,48},{48,64},{64,80},{80,96},{96,112},{112,128},... | collective-permute-start | bytes 24584 | tf_op jit(solution)/shard_map/ppermute | solution.py:221
  35.7 17.6 %collective-permute-start.2 = (f32[1,16,128]{2,1,0:T(8,128)}, f32[1,16,128]{2,1,0:T(8,128)}, u32[]{:S(2)}, u32[]{:S(2)}) collective-permute-start(f32[1,16,128]{2,1,0:T(8,128)} %pad_maximum_fusion.2), channel_id=1, source_target_pairs={{0,32},{16,48},{32,64},{48,80},{64,96},{80,112},{96,128},{112,144}... | collective-permute-start | bytes 24584 | tf_op jit(solution)/shard_map/ppermute | solution.py:221
  41.8 12.3 %collective-permute-start.3 = (f32[1,16,128]{2,1,0:T(8,128)}, f32[1,16,128]{2,1,0:T(8,128)}, u32[]{:S(2)}, u32[]{:S(2)}) collective-permute-start(f32[1,16,128]{2,1,0:T(8,128)} %pad_maximum_fusion.2), channel_id=1, source_target_pairs={{0,48},{16,64},{32,80},{48,96},{64,112},{80,128},{96,144},{112,160... | collective-permute-start | bytes 24584 | tf_op jit(solution)/shard_map/ppermute | solution.py:221
  57.5 9.5 %copy-start.1 = (f32[1,16,128]{2,1,0:T(8,128)S(1)}, f32[1,16,128]{2,1,0:T(8,128)}, u32[]{:S(2)}) copy-start(f32[1,16,128]{2,1,0:T(8,128)} %pad_maximum_fusion.2) | copy-start | bytes 24580
  57.5 36.0 %all-to-all-start.2 = ((f32[4,1160,128]{2,1,0:T(8,128)}), f32[4,1160,128]{2,1,0:T(8,128)S(1)}, u32[]{:S(2)}, u32[]{:S(2)}) async-start(f32[4,1160,128]{2,1,0:T(8,128)} %pad_add_fusion), calls=%async_computation.2 | async-start | bytes 4751360 | tf_op jit(solution)/shard_map/all_to_all | solution.py:238
  63.3 27.6 %collective-permute-start.7 = (f32[4,256,128]{2,1,0:T(8,128)}, f32[4,256,128]{2,1,0:T(8,128)}, u32[]{:S(2)}, u32[]{:S(2)}) collective-permute-start(f32[4,256,128]{2,1,0:T(8,128)} %dynamic-slice_bitcast_fusion), channel_id=1, source_target_pairs={{0,1},{1,0},{2,3},{3,2},{4,5},{5,4},{6,7},{7,6},{8,9},{9,8},{10,11... | collective-permute-start | bytes 1572872 | tf_op jit(solution)/shard_map/ppermute | solution.py:229
  71.5 10.5 %collective-permute-start.4 = (f32[4,16,128]{2,1,0:T(8,128)S(1)}, f32[4,16,128]{2,1,0:T(8,128)S(1)}, u32[]{:S(2)}, u32[]{:S(2)}) collective-permute-start(f32[4,16,128]{2,1,0:T(8,128)S(1)} %get-tuple-element.55), channel_id=1, source_target_pairs={{0,64},{16,80},{32,96},{48,112},{64,128},{80,144},{96,160},{112,17... | collective-permute-start | bytes 98312 | tf_op jit(solution)/shard_map/ppermute | solution.py:221
  78.7 9.7 %collective-permute-start.5 = (f32[4,16,128]{2,1,0:T(8,128)S(1)}, f32[4,16,128]{2,1,0:T(8,128)S(1)}, u32[]{:S(2)}, u32[]{:S(2)}) collective-permute-start(f32[4,16,128]{2,1,0:T(8,128)S(1)} %get-tuple-element.55), channel_id=1, source_target_pairs={{0,128},{16,144},{32,160},{48,176},{64,0},{80,16},{96,32},{112,48}... | collective-permute-start | bytes 98312 | tf_op jit(solution)/shard_map/ppermute | solution.py:221
  89.0 3.8 %collective-permute-start.6 = (f32[12,16,128]{2,1,0:T(8,128)}, f32[12,16,128]{2,1,0:T(8,128)S(1)}, u32[]{:S(2)}, u32[]{:S(2)}) collective-permute-start(f32[12,16,128]{2,1,0:T(8,128)} %get-tuple-element.49), channel_id=1, source_target_pairs={{0,8},{8,0},{1,9},{9,1},{2,10},{10,2},{3,11},{11,3},{4,12},{12,4},... | collective-permute-start | bytes 294920 | tf_op jit(solution)/shard_map/ppermute | solution.py:221
  93.5 7.4 %copy-start.2 = (s32[96]{0:T(128)S(1)}, s32[96]{0:T(128)}, u32[]{:S(2)}) copy-start(s32[96]{0:T(128)} %constant.142) | copy-start | bytes 1156
  93.5 7.4 %copy-start.3 = (s32[96]{0:T(128)S(1)}, s32[96]{0:T(128)}, u32[]{:S(2)}) copy-start(s32[96]{0:T(128)} %constant.143) | copy-start | bytes 1156
  93.5 7.4 %copy-start.4 = (s32[96]{0:T(128)S(1)}, s32[96]{0:T(128)}, u32[]{:S(2)}) copy-start(s32[96]{0:T(128)} %constant.144) | copy-start | bytes 1156
  93.7 7.3 %copy-start = (f32[4,256,128]{2,1,0:T(8,128)S(1)}, f32[4,256,128]{2,1,0:T(8,128)}, u32[]{:S(2)}) copy-start(f32[4,256,128]{2,1,0:T(8,128)} %bitcast_add_fusion) | copy-start | bytes 1572868
  94.6 38.3 %all-to-all-start.3 = ((f32[12,120,128]{2,1,0:T(8,128)}), f32[12,120,128]{2,1,0:T(8,128)S(1)}, u32[]{:S(2)}, u32[]{:S(2)}) async-start(f32[12,120,128]{2,1,0:T(8,128)} %pad_maximum_fusion), calls=%async_computation.3 | async-start | bytes 1474560 | tf_op jit(solution)/shard_map/all_to_all | solution.py:238
  101.0 19.8 %collective-permute-start.10 = (f32[256,128]{1,0:T(8,128)S(1)}, f32[256,128]{1,0:T(8,128)S(1)}, u32[]{:S(2)}, u32[]{:S(2)}) collective-permute-start(f32[256,128]{1,0:T(8,128)S(1)} %get-tuple-element.47), channel_id=1, source_target_pairs={{0,6},{1,7},{2,4},{3,5},{4,2},{5,3},{6,0},{7,1},{8,14},{9,15},{10,... | collective-permute-start | bytes 393224 | tf_op jit(solution)/shard_map/ppermute | solution.py:332
  105.7 19.7 %collective-permute-start.8 = (f32[256,128]{1,0:T(8,128)S(1)}, f32[256,128]{1,0:T(8,128)S(1)}, u32[]{:S(2)}, u32[]{:S(2)}) collective-permute-start(f32[256,128]{1,0:T(8,128)S(1)} %get-tuple-element.46), channel_id=1, source_target_pairs={{0,2},{1,3},{2,0},{3,1},{4,6},{5,7},{6,4},{7,5},{8,10},{9,11},{10,... | collective-permute-start | bytes 393224 | tf_op jit(solution)/shard_map/ppermute | solution.py:332
  109.9 15.4 %collective-permute-start.9 = (f32[256,128]{1,0:T(8,128)S(1)}, f32[256,128]{1,0:T(8,128)S(1)}, u32[]{:S(2)}, u32[]{:S(2)}) collective-permute-start(f32[256,128]{1,0:T(8,128)S(1)} %get-tuple-element.48), channel_id=1, source_target_pairs={{0,4},{1,5},{2,6},{3,7},{4,0},{5,1},{6,2},{7,3},{8,12},{9,13},{10,... | collective-permute-start | bytes 393224 | tf_op jit(solution)/shard_map/ppermute | solution.py:332
  113.9 12.1 %collective-permute-start.11 = (f32[24,16,128]{2,1,0:T(8,128)}, f32[24,16,128]{2,1,0:T(8,128)S(1)}, u32[]{:S(2)}, u32[]{:S(2)}) collective-permute-start(f32[24,16,128]{2,1,0:T(8,128)} %constant_dynamic-update-slice_fusion.10), channel_id=1, source_target_pairs={{0,192},{192,384},{384,576},{576,0},{1,193},{193,385},{385,577},{5... | collective-permute-start | bytes 589832 | tf_op jit(solution)/shard_map/ppermute | solution.py:221
  117.3 10.8 %collective-permute-start.12 = (f32[24,16,128]{2,1,0:T(8,128)}, f32[24,16,128]{2,1,0:T(8,128)S(1)}, u32[]{:S(2)}, u32[]{:S(2)}) collective-permute-start(f32[24,16,128]{2,1,0:T(8,128)} %constant_dynamic-update-slice_fusion.10), channel_id=1, source_target_pairs={{0,384},{192,576},{384,0},{576,192},{1,385},{193,577},{385,1},{577... | collective-permute-start | bytes 589832 | tf_op jit(solution)/shard_map/ppermute | solution.py:221
  120.8 10.2 %collective-permute-start.13 = (f32[24,16,128]{2,1,0:T(8,128)}, f32[24,16,128]{2,1,0:T(8,128)S(1)}, u32[]{:S(2)}, u32[]{:S(2)}) collective-permute-start(f32[24,16,128]{2,1,0:T(8,128)} %constant_dynamic-update-slice_fusion.10), channel_id=1, source_target_pairs={{0,576},{192,0},{384,192},{576,384},{1,577},{193,1},{385,193},{577... | collective-permute-start | bytes 589832 | tf_op jit(solution)/shard_map/ppermute | solution.py:221

commit v10 on v9

--- a/solution.py
+++ b/solution.py
@@ -253,6 +253,7 @@
     own_rows = jnp.concatenate(
         [latents.reshape(1, -1, LANES), map_pre.reshape(1, -1, LANES)], axis=1
     )
+    pair = jnp.concatenate([own_rows] + arriving(own_rows, "core", (1,)), axis=0)
     map_rows = exchange(map_weight.reshape(nchan, -1, cols_dev), "chan")
 
     core_id = lax.axis_index("core")
@@ -266,7 +267,7 @@
         jnp.broadcast_to(source[:, None], (1, cols_dev)),
         (nx, nz, rows_dev, ncore * nchan),
     )
-    tile, sent, map_rows, own_rows = lax.optimization_barrier((tile, sent, map_rows, own_rows))
+    tile, sent, map_rows, pair = lax.optimization_barrier((tile, sent, map_rows, pair))
     parts = exchange(tile, ("core", "chan")).reshape(ncore, nchan, -1, LANES)
     coming = lax.ppermute(sent, "core", [(core, ncore - 1 - core) for core in range(ncore)])
     inner_half = halved(inner_part, 1)
@@ -286,7 +287,7 @@
     riders = jnp.concatenate(
         [style_rows, hidden_rows, parts[:, 0, -1], jnp.zeros((8 - 3 * ncore, cols_dev))], axis=0
     )
-    near = arriving(own_rows, "z", range(1, min(4, nz)))
+    near = arriving(pair, "z", range(1, min(4, nz)))
     coming, riders, near = lax.optimization_barrier((coming, riders, near))
     moved = exchange(
         kept
@@ -297,9 +298,8 @@
         ),
         "x",
     )
-    near = jnp.concatenate([own_rows] + near, axis=0)
+    near = lax.optimization_barrier(jnp.concatenate([pair] + near, axis=0))
     gathered = jnp.concatenate([near] + arriving(near, "z", range(4, nz, 4)), axis=0)
-    gathered = jnp.concatenate([gathered] + arriving(gathered, "core", (1,)), axis=0)
     pieces = jnp.sum(moved[:, : nz * rows_dev], axis=0).reshape(nz, rows_dev, cols_dev)
     riders = jnp.concatenate(
         [
@@ -317,8 +317,8 @@
         jnp.concatenate([pieces, jnp.broadcast_to(riders[None], (nz,) + riders.shape)], axis=1), "z"
     )
     gathered = jnp.concatenate([gathered] + arriving(gathered, "x", range(1, nx)), axis=0)
-    back_x, back_core, back_z = np.meshgrid(
-        np.arange(nx), np.arange(ncore), np.arange(nz), indexing="ij"
+    back_x, back_z, back_core = np.meshgrid(
+        np.arange(nx), np.arange(nz), np.arange(ncore), indexing="ij"
     )
     spots = [
         (lax.axis_index(name) + lax.axis_size(name) - back.reshape(-1)) % lax.axis_size(name)

time: 138 us -> 133 us (0.964)
  the two profiles are of different devices: /device:TPU:2 before, /device:TPU:8 now
where the time goes in v10:
time: 133 us; the launch traced here: 132 us
  starting transfers between devices  85 us (64%)
  waiting for transfers between devices  19.6 us (15%)
  other arithmetic  10.5 us (8%)
  Pallas kernels  6.89 us (5%)
  matrix products  4.64 us (3%)
  local copies, waits for them, and re-layouts  2.49 us (2%)
  between operations  2.42 us (2%)
    ppermute x9, starting transfers between devices, arriving(): lax.ppermute(rows, name, [(sender, (sender + hop) % size) for sender in r...  35.1 us
    all_to_all x4, starting transfers between devices, exchange(): return lax.all_to_all(blocks, axes, 0, 0, tiled=True)  33 us
    ppermute x3, starting transfers between devices, local(): lax.ppermute(lax.dynamic_index_in_dim(inner_half, place ^ flip, 0, keepdi...  12.2 us
    ppermute x9, waiting for transfers between devices, arriving(): lax.ppermute(rows, name, [(sender, (sender + hop) % size) for sender in r...  10.2 us
    all_to_all x4, waiting for transfers between devices, exchange(): return lax.all_to_all(blocks, axes, 0, 0, tiled=True)  7.47 us
    pallas_call x1, Pallas kernels, convolution_part(): pl.pallas_call(functools.partial(convolution_kernel, side, rows_dev), out...  6.89 us
    add x1, other arithmetic, local(): kept + coming  3.35 us
  transfers between devices with their start and end apart: 18, of which 5 were waited for; matrix products, arithmetic and copies ran while one was open for 7% of the time, Pallas kernels for 5%

profile of v10, /device:TPU:8, one launch (start us, length us, event | category | flops | bytes accessed | tf_op | source)
XLA Modules:
  0.0 131.5 jit_solution(9804189958530747855)
XLA Ops:
  0.6 13.5 %all-to-all-start = ((f32[8,128,128]{2,1,0:T(8,128)}), f32[8,128,128]{2,1,0:T(8,128)}, u32[]{:S(2)}, u32[]{:S(2)}) async-start(f32[8,128,128]{2,1,0:T(8,128)} %bitcast.68), calls=%async_computation | async-start | bytes 1048576 | tf_op jit(solution)/shard_map/all_to_all | solution.py:238
  14.1 0.8 pad_maximum_fusion.5
  14.9 1.9 %collective-permute-start = (f32[1,16,128]{2,1,0:T(8,128)S(1)}, f32[1,16,128]{2,1,0:T(8,128)S(1)}, u32[]{:S(2)}, u32[]{:S(2)}) collective-permute-start(f32[1,16,128]{2,1,0:T(8,128)S(1)} %pad_maximum_fusion.5), channel_id=1, source_target_pairs={{0,8},{8,0},{1,9},{9,1},{2,10},{10,2},{3,11},{11,3},{4,12},{12,4},... | collective-permute-start | bytes 24584 | tf_op jit(solution)/shard_map/ppermute | solution.py:221
  18.1 6.9 %convolution_part.1 = (f32[4,1160,128]{2,1,0:T(8,128)}, f32[4,1160,128]{2,1,0:T(8,128)S(1)}, f32[8,256,128]{2,1,0:T(8,128)S(1)}, f32[16,16,128]{2,1,0:T(8,128)}) custom-call(s32[1]{0:T(128)} %bitcast.core_ref, bf16[256,1024]{1,0:T(8,128)(2,1)} %bitcast.83, f32[1,1024]{1,0:T(1,128)} %style_hbm.1, bf16[9216,128]{1,0:T(8,128)(2,1)} %bitcast.82, ...), custom_call_target="tpu_custom_call" | custom-call | flops 1207959552 | bytes 12000000 | tf_op jit(solution)/shard_map/convolution_part/pallas_call | solution.py:179
  25.7 2.4 %collective-permute-start.1 = (f32[4,1160,128]{2,1,0:T(8,128)}, f32[4,1160,128]{2,1,0:T(8,128)}, u32[]{:S(2)}, u32[]{:S(2)}) collective-permute-start(f32[4,1160,128]{2,1,0:T(8,128)} %get-tuple-element.24), channel_id=1, source_target_pairs={{0,8},{8,0},{1,9},{9,1},{2,10},{10,2},{3,11},{11,3},{4,12},{12,4},... | collective-permute-start | bytes 7127048 | tf_op jit(solution)/shard_map/ppermute | solution.py:272
  28.1 7.3 %all-to-all-start.1 = ((f32[16,16,128]{2,1,0:T(8,128)}), f32[16,16,128]{2,1,0:T(8,128)S(1)}, u32[]{:S(2)}, u32[]{:S(2)}) async-start(f32[16,16,128]{2,1,0:T(8,128)} %get-tuple-element.25), calls=%async_computation.1 | async-start | bytes 262144 | tf_op jit(solution)/shard_map/all_to_all | solution.py:238
  35.9 3.6 %collective-permute-start.4 = (f32[2,16,128]{2,1,0:T(8,128)}, f32[2,16,128]{2,1,0:T(8,128)}, u32[]{:S(2)}, u32[]{:S(2)}) collective-permute-start(f32[2,16,128]{2,1,0:T(8,128)} %pad_maximum_fusion.3), channel_id=1, source_target_pairs={{0,48},{16,64},{32,80},{48,96},{64,112},{80,128},{96,144},{112,160... | collective-permute-start | bytes 49160 | tf_op jit(solution)/shard_map/ppermute | solution.py:221
  39.5 7.3 %collective-permute-start.3 = (f32[2,16,128]{2,1,0:T(8,128)}, f32[2,16,128]{2,1,0:T(8,128)}, u32[]{:S(2)}, u32[]{:S(2)}) collective-permute-start(f32[2,16,128]{2,1,0:T(8,128)} %pad_maximum_fusion.3), channel_id=1, source_target_pairs={{0,32},{16,48},{32,64},{48,80},{64,96},{80,112},{96,128},{112,144}... | collective-permute-start | bytes 49160 | tf_op jit(solution)/shard_map/ppermute | solution.py:221
  46.8 4.3 %collective-permute-start.2 = (f32[2,16,128]{2,1,0:T(8,128)}, f32[2,16,128]{2,1,0:T(8,128)}, u32[]{:S(2)}, u32[]{:S(2)}) collective-permute-start(f32[2,16,128]{2,1,0:T(8,128)} %pad_maximum_fusion.3), channel_id=1, source_target_pairs={{0,16},{16,32},{32,48},{48,64},{64,80},{80,96},{96,112},{112,128},... | collective-permute-start | bytes 49160 | tf_op jit(solution)/shard_map/ppermute | solution.py:221
  51.2 1.6 %convolution_bitcast_fusion = f32[2,128]{1,0:T(2,128)S(1)} fusion(f32[8,128,128]{2,1,0:T(8,128)} %all-to-all-done, f32[2,8,128]{2,1,0:T(8,128)S(1)} %slice_reduce_fusion.2), kind=kOutput, calls=%fused_computation.5 | convolution fusion | flops 3145728 | bytes 533504 | tf_op jit(solution)/shard_map/dot_general | solution.py:276
  54.0 3.3 %pad_add_fusion = f32[4,1160,128]{2,1,0:T(8,128)} fusion(f32[4,8,128]{2,1,0:T(8,128)S(1)} %broadcast_in_dim.40, f32[4,1160,128]{2,1,0:T(8,128)S(1)} %get-tuple-element.21, f32[4,1160,128]{2,1,0:T(8,128)} %collective-permute-done.1), kind=kLoop, calls=%fused_computation | loop fusion | flops 1187840 | bytes 7143424 | tf_op jit(solution)/shard_map/add | solution.py:293
  57.3 4.4 %all-to-all-start.2 = ((f32[4,1160,128]{2,1,0:T(8,128)}), f32[4,1160,128]{2,1,0:T(8,128)S(1)}, u32[]{:S(2)}, u32[]{:S(2)}) async-start(f32[4,1160,128]{2,1,0:T(8,128)} %pad_add_fusion), calls=%async_computation.2 | async-start | bytes 4751360 | tf_op jit(solution)/shard_map/all_to_all | solution.py:238
  61.8 0.8 dynamic-slice_bitcast_fusion
  62.6 2.2 %collective-permute-start.7 = (f32[4,256,128]{2,1,0:T(8,128)}, f32[4,256,128]{2,1,0:T(8,128)}, u32[]{:S(2)}, u32[]{:S(2)}) collective-permute-start(f32[4,256,128]{2,1,0:T(8,128)} %dynamic-slice_bitcast_fusion), channel_id=1, source_target_pairs={{0,1},{1,0},{2,3},{3,2},{4,5},{5,4},{6,7},{7,6},{8,9},{9,8},{10,11... | collective-permute-start | bytes 1572872 | tf_op jit(solution)/shard_map/ppermute | solution.py:229
  64.8 0.8 pad_maximum_fusion.2
  65.5 6.5 %collective-permute-start.6 = (f32[8,16,128]{2,1,0:T(8,128)S(1)}, f32[8,16,128]{2,1,0:T(8,128)S(1)}, u32[]{:S(2)}, u32[]{:S(2)}) collective-permute-start(f32[8,16,128]{2,1,0:T(8,128)S(1)} %pad_maximum_fusion.2), channel_id=1, source_target_pairs={{0,128},{16,144},{32,160},{48,176},{64,0},{80,16},{96,32},{112,48}... | collective-permute-start | bytes 196616 | tf_op jit(solution)/shard_map/ppermute | solution.py:221
  72.0 3.3 %collective-permute-start.5 = (f32[8,16,128]{2,1,0:T(8,128)S(1)}, f32[8,16,128]{2,1,0:T(8,128)S(1)}, u32[]{:S(2)}, u32[]{:S(2)}) collective-permute-start(f32[8,16,128]{2,1,0:T(8,128)S(1)} %pad_maximum_fusion.2), channel_id=1, source_target_pairs={{0,64},{16,80},{32,96},{48,112},{64,128},{80,144},{96,160},{112,17... | collective-permute-start | bytes 196616 | tf_op jit(solution)/shard_map/ppermute | solution.py:221
  75.3 1.9 %collective-permute-done.7 = f32[4,256,128]{2,1,0:T(8,128)} collective-permute-done((f32[4,256,128]{2,1,0:T(8,128)}, f32[4,256,128]{2,1,0:T(8,128)}, u32[]{:S(2)}, u32[]{:S(2)}) %collective-permute-start.7) | collective-permute-done | bytes 524320 | tf_op jit(solution)/shard_map/ppermute | solution.py:229
  77.2 1.9 %bitcast_add_fusion = f32[4,256,128]{2,1,0:T(8,128)} fusion(f32[4,256,128]{2,1,0:T(8,128)} %collective-permute-done.7, f32[4,2,256,128]{3,2,1,0:T(8,128)S(1)} %bitcast.63, s32[]{:T(128)S(6)} %select_n.68), kind=kLoop, calls=%fused_computation.8 | loop fusion | flops 131072 | bytes 1572868 | tf_op jit(solution)/shard_map/add | solution.py:234
  79.1 3.5 %collective-permute-done.5 = f32[8,16,128]{2,1,0:T(8,128)S(1)} collective-permute-done((f32[8,16,128]{2,1,0:T(8,128)S(1)}, f32[8,16,128]{2,1,0:T(8,128)S(1)}, u32[]{:S(2)}, u32[]{:S(2)}) %collective-permute-start.5) | collective-permute-done | bytes 65568 | tf_op jit(solution)/shard_map/ppermute | solution.py:221
  82.6 7.5 %all-to-all-done.2 = f32[4,1160,128]{2,1,0:T(8,128)S(1)} async-done(((f32[4,1160,128]{2,1,0:T(8,128)}), f32[4,1160,128]{2,1,0:T(8,128)S(1)}, u32[]{:S(2)}, u32[]{:S(2)}) %all-to-all-start.2) | async-done | bytes 2375712 | tf_op jit(solution)/shard_map/all_to_all | solution.py:238
  90.3 0.9 pad_maximum_fusion
  91.2 7.8 %all-to-all-start.3 = ((f32[12,120,128]{2,1,0:T(8,128)}), f32[12,120,128]{2,1,0:T(8,128)S(1)}, u32[]{:S(2)}, u32[]{:S(2)}) async-start(f32[12,120,128]{2,1,0:T(8,128)} %pad_maximum_fusion), calls=%async_computation.3 | async-start | bytes 1474560 | tf_op jit(solution)/shard_map/all_to_all | solution.py:238
  99.2 4.3 %collective-permute-start.8 = (f32[256,128]{1,0:T(8,128)S(1)}, f32[256,128]{1,0:T(8,128)S(1)}, u32[]{:S(2)}, u32[]{:S(2)}) collective-permute-start(f32[256,128]{1,0:T(8,128)S(1)} %get-tuple-element.46), channel_id=1, source_target_pairs={{0,2},{1,3},{2,0},{3,1},{4,6},{5,7},{6,4},{7,5},{8,10},{9,11},{10,... | collective-permute-start | bytes 393224 | tf_op jit(solution)/shard_map/ppermute | solution.py:332
  103.5 4.6 %collective-permute-start.10 = (f32[256,128]{1,0:T(8,128)S(1)}, f32[256,128]{1,0:T(8,128)S(1)}, u32[]{:S(2)}, u32[]{:S(2)}) collective-permute-start(f32[256,128]{1,0:T(8,128)S(1)} %get-tuple-element.47), channel_id=1, source_target_pairs={{0,6},{1,7},{2,4},{3,5},{4,2},{5,3},{6,0},{7,1},{8,14},{9,15},{10,... | collective-permute-start | bytes 393224 | tf_op jit(solution)/shard_map/ppermute | solution.py:332
  108.1 3.3 %collective-permute-start.9 = (f32[256,128]{1,0:T(8,128)S(1)}, f32[256,128]{1,0:T(8,128)S(1)}, u32[]{:S(2)}, u32[]{:S(2)}) collective-permute-start(f32[256,128]{1,0:T(8,128)S(1)} %get-tuple-element.48), channel_id=1, source_target_pairs={{0,4},{1,5},{2,6},{3,7},{4,0},{5,1},{6,2},{7,3},{8,12},{9,13},{10,... | collective-permute-start | bytes 393224 | tf_op jit(solution)/shard_map/ppermute | solution.py:332
  112.1 3.1 %collective-permute-start.13 = (f32[24,16,128]{2,1,0:T(8,128)S(1)}, f32[24,16,128]{2,1,0:T(8,128)S(1)}, u32[]{:S(2)}, u32[]{:S(2)}) collective-permute-start(f32[24,16,128]{2,1,0:T(8,128)S(1)} %pad_maximum_fusion.1), channel_id=1, source_target_pairs={{0,576},{192,0},{384,192},{576,384},{1,577},{193,1},{385,193},{577... | collective-permute-start | bytes 589832 | tf_op jit(solution)/shard_map/ppermute | solution.py:221
  115.2 3.4 %collective-permute-start.12 = (f32[24,16,128]{2,1,0:T(8,128)S(1)}, f32[24,16,128]{2,1,0:T(8,128)S(1)}, u32[]{:S(2)}, u32[]{:S(2)}) collective-permute-start(f32[24,16,128]{2,1,0:T(8,128)S(1)} %pad_maximum_fusion.1), channel_id=1, source_target_pairs={{0,384},{192,576},{384,0},{576,192},{1,385},{193,577},{385,1},{577... | collective-permute-start | bytes 589832 | tf_op jit(solution)/shard_map/ppermute | solution.py:221
  118.6 1.9 %collective-permute-start.11 = (f32[24,16,128]{2,1,0:T(8,128)S(1)}, f32[24,16,128]{2,1,0:T(8,128)S(1)}, u32[]{:S(2)}, u32[]{:S(2)}) collective-permute-start(f32[24,16,128]{2,1,0:T(8,128)S(1)} %pad_maximum_fusion.1), channel_id=1, source_target_pairs={{0,192},{192,384},{384,576},{576,0},{1,193},{193,385},{385,577},{5... | collective-permute-start | bytes 589832 | tf_op jit(solution)/shard_map/ppermute | solution.py:221
  121.2 6.1 %collective-permute-done.11 = f32[24,16,128]{2,1,0:T(8,128)S(1)} collective-permute-done((f32[24,16,128]{2,1,0:T(8,128)S(1)}, f32[24,16,128]{2,1,0:T(8,128)S(1)}, u32[]{:S(2)}, u32[]{:S(2)}) %collective-permute-start.11) | collective-permute-done | bytes 196640 | tf_op jit(solution)/shard_map/ppermute | solution.py:221
  128.7 1.4 %convolution_multiply_fusion.1 = f32[1024,128]{1,0:T(8,128)} fusion(f32[96,256]{1,0:T(8,128)S(1)} %fusion.8, f32[12,8,8,128]{3,2,1,0:T(8,128)S(1)} %bitcast.65), kind=kOutput, calls=%fused_computation.3 | convolution fusion | flops 75923456 | bytes 966656 | tf_op jit(solution)/shard_map/dot_general | solution.py:361
  130.1 1.4 %convolution_multiply_fusion = f32[1024,128]{1,0:T(8,128)} fusion(f32[12,8,8,128]{3,2,1,0:T(8,128)S(1)} %bitcast.67, f32[96,256]{1,0:T(8,128)S(1)} %fusion.8, f32[96,1024]{1,0:T(8,128)S(1)} %bitcast.69, s32[]{:T(128)S(6)} %select_n.75), kind=kOutput, calls=%fused_computation.2 | convolution fusion | flops 75665408 | bytes 1015812 | tf_op jit(solution)/shard_map/dot_general | solution.py:366
  (57 shorter events, 5.4 us)
Async XLA Ops:
  0.6 25.1 %all-to-all-start = ((f32[8,128,128]{2,1,0:T(8,128)}), f32[8,128,128]{2,1,0:T(8,128)}, u32[]{:S(2)}, u32[]{:S(2)}) async-start(f32[8,128,128]{2,1,0:T(8,128)} %bitcast.68), calls=%async_computation | async-start | bytes 1048576 | tf_op jit(solution)/shard_map/all_to_all | solution.py:238
  14.1 10.9 %copy-start.2 = (f32[1,1024]{1,0:T(1,128)S(1)}, f32[1,1024]{1,0:T(1,128)}, u32[]{:S(2)}) copy-start(f32[1,1024]{1,0:T(1,128)} %param.19) | copy-start | bytes 12292
  14.1 10.9 %copy-start.3 = (f32[1,1024]{1,0:T(1,128)S(1)}, f32[1,1024]{1,0:T(1,128)}, u32[]{:S(2)}) copy-start(f32[1,1024]{1,0:T(1,128)} %param.18) | copy-start | bytes 12292
  14.9 10.1 %collective-permute-start = (f32[1,16,128]{2,1,0:T(8,128)S(1)}, f32[1,16,128]{2,1,0:T(8,128)S(1)}, u32[]{:S(2)}, u32[]{:S(2)}) collective-permute-start(f32[1,16,128]{2,1,0:T(8,128)S(1)} %pad_maximum_fusion.5), channel_id=1, source_target_pairs={{0,8},{8,0},{1,9},{9,1},{2,10},{10,2},{3,11},{11,3},{4,12},{12,4},... | collective-permute-start | bytes 24584 | tf_op jit(solution)/shard_map/ppermute | solution.py:221
  25.7 28.3 %collective-permute-start.1 = (f32[4,1160,128]{2,1,0:T(8,128)}, f32[4,1160,128]{2,1,0:T(8,128)}, u32[]{:S(2)}, u32[]{:S(2)}) collective-permute-start(f32[4,1160,128]{2,1,0:T(8,128)} %get-tuple-element.24), channel_id=1, source_target_pairs={{0,8},{8,0},{1,9},{9,1},{2,10},{10,2},{3,11},{11,3},{4,12},{12,4},... | collective-permute-start | bytes 7127048 | tf_op jit(solution)/shard_map/ppermute | solution.py:272
  28.1 23.0 %all-to-all-start.1 = ((f32[16,16,128]{2,1,0:T(8,128)}), f32[16,16,128]{2,1,0:T(8,128)S(1)}, u32[]{:S(2)}, u32[]{:S(2)}) async-start(f32[16,16,128]{2,1,0:T(8,128)} %get-tuple-element.25), calls=%async_computation.1 | async-start | bytes 262144 | tf_op jit(solution)/shard_map/all_to_all | solution.py:238
  35.9 17.5 %collective-permute-start.4 = (f32[2,16,128]{2,1,0:T(8,128)}, f32[2,16,128]{2,1,0:T(8,128)}, u32[]{:S(2)}, u32[]{:S(2)}) collective-permute-start(f32[2,16,128]{2,1,0:T(8,128)} %pad_maximum_fusion.3), channel_id=1, source_target_pairs={{0,48},{16,64},{32,80},{48,96},{64,112},{80,128},{96,144},{112,160... | collective-permute-start | bytes 49160 | tf_op jit(solution)/shard_map/ppermute | solution.py:221
  39.5 14.0 %collective-permute-start.3 = (f32[2,16,128]{2,1,0:T(8,128)}, f32[2,16,128]{2,1,0:T(8,128)}, u32[]{:S(2)}, u32[]{:S(2)}) collective-permute-start(f32[2,16,128]{2,1,0:T(8,128)} %pad_maximum_fusion.3), channel_id=1, source_target_pairs={{0,32},{16,48},{32,64},{48,80},{64,96},{80,112},{96,128},{112,144}... | collective-permute-start | bytes 49160 | tf_op jit(solution)/shard_map/ppermute | solution.py:221
  46.8 7.2 %collective-permute-start.2 = (f32[2,16,128]{2,1,0:T(8,128)}, f32[2,16,128]{2,1,0:T(8,128)}, u32[]{:S(2)}, u32[]{:S(2)}) collective-permute-start(f32[2,16,128]{2,1,0:T(8,128)} %pad_maximum_fusion.3), channel_id=1, source_target_pairs={{0,16},{16,32},{32,48},{48,64},{64,80},{80,96},{96,112},{112,128},... | collective-permute-start | bytes 49160 | tf_op jit(solution)/shard_map/ppermute | solution.py:221
  57.3 7.4 %copy-start.1 = (f32[2,16,128]{2,1,0:T(8,128)S(1)}, f32[2,16,128]{2,1,0:T(8,128)}, u32[]{:S(2)}) copy-start(f32[2,16,128]{2,1,0:T(8,128)} %pad_maximum_fusion.3) | copy-start | bytes 49156
  57.3 32.7 %all-to-all-start.2 = ((f32[4,1160,128]{2,1,0:T(8,128)}), f32[4,1160,128]{2,1,0:T(8,128)S(1)}, u32[]{:S(2)}, u32[]{:S(2)}) async-start(f32[4,1160,128]{2,1,0:T(8,128)} %pad_add_fusion), calls=%async_computation.2 | async-start | bytes 4751360 | tf_op jit(solution)/shard_map/all_to_all | solution.py:238
  62.6 14.6 %collective-permute-start.7 = (f32[4,256,128]{2,1,0:T(8,128)}, f32[4,256,128]{2,1,0:T(8,128)}, u32[]{:S(2)}, u32[]{:S(2)}) collective-permute-start(f32[4,256,128]{2,1,0:T(8,128)} %dynamic-slice_bitcast_fusion), channel_id=1, source_target_pairs={{0,1},{1,0},{2,3},{3,2},{4,5},{5,4},{6,7},{7,6},{8,9},{9,8},{10,11... | collective-permute-start | bytes 1572872 | tf_op jit(solution)/shard_map/ppermute | solution.py:229
  65.5 13.5 %collective-permute-start.6 = (f32[8,16,128]{2,1,0:T(8,128)S(1)}, f32[8,16,128]{2,1,0:T(8,128)S(1)}, u32[]{:S(2)}, u32[]{:S(2)}) collective-permute-start(f32[8,16,128]{2,1,0:T(8,128)S(1)} %pad_maximum_fusion.2), channel_id=1, source_target_pairs={{0,128},{16,144},{32,160},{48,176},{64,0},{80,16},{96,32},{112,48}... | collective-permute-start | bytes 196616 | tf_op jit(solution)/shard_map/ppermute | solution.py:221
  72.0 10.6 %collective-permute-start.5 = (f32[8,16,128]{2,1,0:T(8,128)S(1)}, f32[8,16,128]{2,1,0:T(8,128)S(1)}, u32[]{:S(2)}, u32[]{:S(2)}) collective-permute-start(f32[8,16,128]{2,1,0:T(8,128)S(1)} %pad_maximum_fusion.2), channel_id=1, source_target_pairs={{0,64},{16,80},{32,96},{48,112},{64,128},{80,144},{96,160},{112,17... | collective-permute-start | bytes 196616 | tf_op jit(solution)/shard_map/ppermute | solution.py:221
  90.1 9.0 %copy-start.4 = (s32[96]{0:T(128)S(1)}, s32[96]{0:T(128)}, u32[]{:S(2)}) copy-start(s32[96]{0:T(128)} %constant.144) | copy-start | bytes 1156
  90.1 9.0 %copy-start.5 = (s32[96]{0:T(128)S(1)}, s32[96]{0:T(128)}, u32[]{:S(2)}) copy-start(s32[96]{0:T(128)} %constant.143) | copy-start | bytes 1156
  90.1 9.0 %copy-start.6 = (s32[96]{0:T(128)S(1)}, s32[96]{0:T(128)}, u32[]{:S(2)}) copy-start(s32[96]{0:T(128)} %constant.142) | copy-start | bytes 1156
  90.2 8.9 %copy-start = (f32[4,256,128]{2,1,0:T(8,128)S(1)}, f32[4,256,128]{2,1,0:T(8,128)}, u32[]{:S(2)}) copy-start(f32[4,256,128]{2,1,0:T(8,128)} %bitcast_add_fusion) | copy-start | bytes 1572868
  91.2 36.4 %all-to-all-start.3 = ((f32[12,120,128]{2,1,0:T(8,128)}), f32[12,120,128]{2,1,0:T(8,128)S(1)}, u32[]{:S(2)}, u32[]{:S(2)}) async-start(f32[12,120,128]{2,1,0:T(8,128)} %pad_maximum_fusion), calls=%async_computation.3 | async-start | bytes 1474560 | tf_op jit(solution)/shard_map/all_to_all | solution.py:238
  99.2 19.4 %collective-permute-start.8 = (f32[256,128]{1,0:T(8,128)S(1)}, f32[256,128]{1,0:T(8,128)S(1)}, u32[]{:S(2)}, u32[]{:S(2)}) collective-permute-start(f32[256,128]{1,0:T(8,128)S(1)} %get-tuple-element.46), channel_id=1, source_target_pairs={{0,2},{1,3},{2,0},{3,1},{4,6},{5,7},{6,4},{7,5},{8,10},{9,11},{10,... | collective-permute-start | bytes 393224 | tf_op jit(solution)/shard_map/ppermute | solution.py:332
  103.5 17.0 %collective-permute-start.10 = (f32[256,128]{1,0:T(8,128)S(1)}, f32[256,128]{1,0:T(8,128)S(1)}, u32[]{:S(2)}, u32[]{:S(2)}) collective-permute-start(f32[256,128]{1,0:T(8,128)S(1)} %get-tuple-element.47), channel_id=1, source_target_pairs={{0,6},{1,7},{2,4},{3,5},{4,2},{5,3},{6,0},{7,1},{8,14},{9,15},{10,... | collective-permute-start | bytes 393224 | tf_op jit(solution)/shard_map/ppermute | solution.py:332
  108.1 12.4 %collective-permute-start.9 = (f32[256,128]{1,0:T(8,128)S(1)}, f32[256,128]{1,0:T(8,128)S(1)}, u32[]{:S(2)}, u32[]{:S(2)}) collective-permute-start(f32[256,128]{1,0:T(8,128)S(1)} %get-tuple-element.48), channel_id=1, source_target_pairs={{0,4},{1,5},{2,6},{3,7},{4,0},{5,1},{6,2},{7,3},{8,12},{9,13},{10,... | collective-permute-start | bytes 393224 | tf_op jit(solution)/shard_map/ppermute | solution.py:332
  112.1 15.3 %collective-permute-start.13 = (f32[24,16,128]{2,1,0:T(8,128)S(1)}, f32[24,16,128]{2,1,0:T(8,128)S(1)}, u32[]{:S(2)}, u32[]{:S(2)}) collective-permute-start(f32[24,16,128]{2,1,0:T(8,128)S(1)} %pad_maximum_fusion.1), channel_id=1, source_target_pairs={{0,576},{192,0},{384,192},{576,384},{1,577},{193,1},{385,193},{577... | collective-permute-start | bytes 589832 | tf_op jit(solution)/shard_map/ppermute | solution.py:221
  115.2 12.2 %collective-permute-start.12 = (f32[24,16,128]{2,1,0:T(8,128)S(1)}, f32[24,16,128]{2,1,0:T(8,128)S(1)}, u32[]{:S(2)}, u32[]{:S(2)}) collective-permute-start(f32[24,16,128]{2,1,0:T(8,128)S(1)} %pad_maximum_fusion.1), channel_id=1, source_target_pairs={{0,384},{192,576},{384,0},{576,192},{1,385},{193,577},{385,1},{577... | collective-permute-start | bytes 589832 | tf_op jit(solution)/shard_map/ppermute | solution.py:221
  118.6 8.8 %collective-permute-start.11 = (f32[24,16,128]{2,1,0:T(8,128)S(1)}, f32[24,16,128]{2,1,0:T(8,128)S(1)}, u32[]{:S(2)}, u32[]{:S(2)}) collective-permute-start(f32[24,16,128]{2,1,0:T(8,128)S(1)} %pad_maximum_fusion.1), channel_id=1, source_target_pairs={{0,192},{192,384},{384,576},{576,0},{1,193},{193,385},{385,577},{5... | collective-permute-start | bytes 589832 | tf_op jit(solution)/shard_map/ppermute | solution.py:221
